TPU v7x, 1024 devices: a whole 8x8x8 slice. The times are simulated.
1024 devices in a mesh: rows: 8 (over z), cols: 8 (over x), rep: 16 (over y, core).
Axes of the slice: x: 8, y: 8, z: 8, core: 2. Of those that a mesh axis runs over, the one named last changes fastest.
Arguments:
- feature_map: bfloat16 [16, 64, 128, 384], P('rep', 'rows', 'cols'), may hold values from -6 to 6
- dw_kernel: float32 [7, 7, 384], replicated, may hold values from -0.875 to 0.875
- dw_bias: float32 [384], replicated, may hold values from -3 to 3
- layer_norm_gain: float32 [384], replicated, may hold values from 0.5 to 1.5
- layer_norm_bias: float32 [384], replicated, may hold values from -3 to 3
- w_expand: bfloat16 [384, 1536], replicated, may hold values from -0.3125 to 0.3125
- b_expand: float32 [1536], replicated, may hold values from -3 to 3
- w_reduce: bfloat16 [1536, 384], replicated, may hold values from -0.15625 to 0.15625
- b_reduce: float32 [384], replicated, may hold values from -3 to 3
- layer_scale: float32 [384], replicated, may hold values from 0.5 to 1.5
- cotangent: bfloat16 [16, 64, 128, 384], P('rep', 'rows', 'cols'), may hold values from -6 to 6
Outputs:
- block_out: bfloat16 [16, 64, 128, 384], P('rep', 'rows', 'cols')
- grad_input: bfloat16 [16, 64, 128, 384], P('rep', 'rows', 'cols')
- grad_expand: float32 [384, 1536], P('rep', ('rows', 'cols'))
- grad_reduce_t: float32 [384, 1536], P('rep', ('rows', 'cols'))
- grad_kernel: float32 [7, 7, 384], replicated
- grad_vectors: float32 [5, 384], replicated
- grad_bexp: float32 [1536], replicated
All inputs are finite; a program needn't handle non-finite values.
Results may differ from a plain program's by a relative error of at most 0.0062.
Values may be sent and summed in bfloat16 or wider, within the bound.
No kernel may reach another device: no remote copies, remote signals or barrier semaphores. Data moves between devices by JAX's collectives and lax.ppermute only.
A program may use at most 32 MiB of HBM per device.

v0:
```python
import jax
import jax.numpy as jnp
from jax import lax
from jax.sharding import PartitionSpec as P

EPS = 1e-06
INV_ROOT_TWO = 0.7071067811865476
INV_ROOT_TWO_PI = 0.3989422804014327


def extended(cells, sides, width):
    for axis, dim in sides:
        count = lax.axis_size(axis)
        ends = count - 1
        head = lax.slice_in_dim(cells, 0, width, axis=dim)
        tail = lax.slice_in_dim(cells, cells.shape[dim] - width, cells.shape[dim], axis=dim)
        cells = jnp.concatenate(
            [
                lax.ppermute(tail, axis, [(i, (i + 1) % count) for i in range(ends)]),
                cells,
                lax.ppermute(head, axis, [((i + 1) % count, i) for i in range(ends)]),
            ],
            axis=dim,
        )
    return cells


def depthwise(padded, kernel, height, width):
    total = jnp.zeros((height, width, padded.shape[-1]), jnp.float32)
    for i in range(7):
        for j in range(7):
            total = total + kernel[i, j] * padded[i : i + height, j : j + width].astype(jnp.float32)
    return total


def front_pass(
    xpad,
    gout,
    dw_kernel,
    dw_bias,
    layer_norm_gain,
    layer_norm_bias,
    w_expand,
    b_expand,
    w_reduce,
    b_reduce,
    layer_scale,
    height,
    width,
):
    chans = xpad.shape[-1]
    conv = depthwise(xpad, dw_kernel, height, width) + dw_bias
    flat = conv.reshape(-1, chans)
    centered_input = flat - jnp.mean(flat, axis=-1, keepdims=True)
    inverse_deviation = lax.rsqrt(
        jnp.mean(centered_input * centered_input, axis=-1, keepdims=True) + EPS
    )
    standardized_input = centered_input * inverse_deviation
    normalized_rows = (standardized_input * layer_norm_gain + layer_norm_bias).astype(jnp.bfloat16)
    pre = jnp.dot(normalized_rows, w_expand, preferred_element_type=jnp.float32) + b_expand
    cdf = 0.5 * (1.0 + lax.erf(pre * INV_ROOT_TWO))
    act = (pre * cdf).astype(jnp.bfloat16)
    branch = jnp.dot(act, w_reduce, preferred_element_type=jnp.float32) + b_reduce
    inner = xpad[3 : 3 + height, 3 : 3 + width].reshape(-1, chans).astype(jnp.float32)
    block_out = (inner + layer_scale * branch).astype(jnp.bfloat16).reshape(height, width, chans)
    grad = gout.reshape(-1, chans).astype(jnp.float32)
    scaled = grad * layer_scale
    g_branch = scaled.astype(jnp.bfloat16)
    g_scale = jnp.sum(grad * branch, axis=0)
    g_breduce = jnp.sum(scaled, axis=0)
    grad_reduce_t = lax.dot_general(
        g_branch, act, (((0,), (0,)), ((), ())), preferred_element_type=jnp.float32
    )
    g_act = lax.dot_general(
        g_branch, w_reduce, (((1,), (1,)), ((), ())), preferred_element_type=jnp.float32
    )
    pdf = jnp.exp(-0.5 * pre * pre) * INV_ROOT_TWO_PI
    g_pre = g_act * (cdf + pre * pdf)
    g_bexp = jnp.sum(g_pre, axis=0)
    g_pre_b = g_pre.astype(jnp.bfloat16)
    grad_expand = lax.dot_general(
        normalized_rows, g_pre_b, (((0,), (0,)), ((), ())), preferred_element_type=jnp.float32
    )
    grad_normalized = lax.dot_general(
        g_pre_b, w_expand, (((1,), (1,)), ((), ())), preferred_element_type=jnp.float32
    )
    grad_norm_gain = jnp.sum(grad_normalized * standardized_input, axis=0)
    g_lnbias = jnp.sum(grad_normalized, axis=0)
    scaled_grad_input = grad_normalized * layer_norm_gain
    grad_convolution = inverse_deviation * (
        scaled_grad_input
        - jnp.mean(scaled_grad_input, axis=-1, keepdims=True)
        - standardized_input
        * jnp.mean(scaled_grad_input * standardized_input, axis=-1, keepdims=True)
    )
    g_dwbias = jnp.sum(grad_convolution, axis=0)
    vectors = jnp.stack([g_dwbias, grad_norm_gain, g_lnbias, g_breduce, g_scale])
    return (
        block_out,
        grad_convolution.reshape(height, width, chans),
        grad_expand,
        grad_reduce_t,
        vectors,
        g_bexp,
    )


def back_pass(gpad, xpad, gout, dw_kernel, height, width):
    inner = gpad[3 : 3 + height, 3 : 3 + width]
    grad_in = gout.astype(jnp.float32)
    kernel_rows = []
    for i in range(7):
        row_terms = []
        for j in range(7):
            part = xpad[i : i + height, j : j + width].astype(jnp.float32)
            row_terms.append(jnp.sum(inner * part, axis=(0, 1)))
            grad_in = (
                grad_in + dw_kernel[i, j] * gpad[6 - i : 6 - i + height, 6 - j : 6 - j + width]
            )
        kernel_rows.append(jnp.stack(row_terms))
    return (grad_in.astype(jnp.bfloat16), jnp.stack(kernel_rows))


def per_device(
    feature_map,
    dw_kernel,
    dw_bias,
    layer_norm_gain,
    layer_norm_bias,
    w_expand,
    b_expand,
    w_reduce,
    b_reduce,
    layer_scale,
    cotangent,
):
    height, width = (feature_map.shape[1], feature_map.shape[2])
    xpad = extended(feature_map, (("rows", 1), ("cols", 2)), 3)[0]
    gout = cotangent[0]
    block_out, grad_convolution, gexp, gred, vectors, gbexp = front_pass(
        xpad,
        gout,
        dw_kernel,
        dw_bias,
        layer_norm_gain,
        layer_norm_bias,
        w_expand,
        b_expand,
        w_reduce,
        b_reduce,
        layer_scale,
        height,
        width,
    )
    stacked = jnp.stack([gexp, gred])
    gpad = extended(grad_convolution, (("rows", 0), ("cols", 1)), 3)
    grad_in, gker = back_pass(gpad, xpad, gout, dw_kernel, height, width)
    partial_sum = lax.psum_scatter(stacked, "rep", scatter_dimension=1, tiled=True)
    summed = lax.psum_scatter(partial_sum, ("rows", "cols"), scatter_dimension=2, tiled=True)
    gker, vectors, gbexp = lax.psum((gker, vectors, gbexp), ("rows", "cols", "rep"))
    count = lax.axis_size("rows") * height * lax.axis_size("cols") * width * lax.axis_size("rep")
    scale = 1.0 / jnp.sqrt(jnp.float32(count))
    return (
        block_out[None],
        grad_in[None],
        summed[0] * scale,
        summed[1] * scale,
        gker * scale,
        vectors * scale,
        gbexp * scale,
    )


def solution(mesh):
    in_specs = (
        P("rep", "rows", "cols", None),
        P(),
        P(),
        P(),
        P(),
        P(),
        P(),
        P(),
        P(),
        P(),
        P("rep", "rows", "cols", None),
    )
    out_specs = (
        P("rep", "rows", "cols", None),
        P("rep", "rows", "cols", None),
        P("rep", ("rows", "cols")),
        P("rep", ("rows", "cols")),
        P(),
        P(),
        P(),
    )
    return jax.shard_map(
        per_device, mesh=mesh, in_specs=in_specs, out_specs=out_specs, check_vma=False
    )
```

profile of v0, /device:TPU:1, one launch (start us, length us, event | category | flops | bytes accessed | tf_op | source)
XLA Modules:
  0.0 495.7 jit_solution(13965165051081966435)
XLA Ops:
  8.0 0.0 copy-start
  8.0 0.0 all-reduce.5.cloned.1.call-start
  8.1 0.9 fusion.177
  9.0 1.3 collective-permute-start.1
  10.2 6.4 %collective-permute-start = (bf16[1,3,16,384]{3,2,1,0:T(8,128)(2,1)S(1)}, bf16[1,3,16,384]{3,2,1,0:T(8,128)(2,1)S(1)}, u32[]{:S(2)}, u32[]{:S(2)}) collective-permute-start(bf16[1,3,16,384]{3,2,1,0:T(8,128)(2,1)S(1)} %get-tuple-element.129), channel_id=1, source_target_pairs={{0,128},{128,256},{256,384},{384,512},{512,640},{640,768},{768,896... | collective-permute-start | bytes 110600 | tf_op jit(solution)/shard_map/ppermute | solution.py:19
  16.6 1.1 slice_reduce_fusion.47
  17.7 1.2 slice_reduce_fusion.48
  19.0 0.0 collective-permute-done
  19.0 0.9 constant_dynamic-update-slice_fusion.1
  19.9 0.0 collective-permute-done.1
  20.0 3.1 collective-permute-start.2
  23.1 1.3 collective-permute-start.3
  24.4 1.0 slice_reduce_fusion.46
  25.4 0.0 collective-permute-done.2
  25.4 2.8 collective-permute-done.3
  28.2 0.1 maximum_bitcast_fusion
  28.3 0.0 copy-start.4
  28.3 0.0 copy-start.8
  28.4 0.0 copy-start.5
  28.4 1.6 fusion.173
  30.0 0.1 div.15
  30.0 0.2 multiply_reduce_fusion.3
  30.2 0.1 rsqrt.12
  30.3 0.1 add_convert_fusion
  30.5 0.0 copy-start.1
  30.5 0.0 copy-start.2
  30.5 0.0 copy-start.6
  30.5 0.0 copy-start.9
  30.5 0.4 multiply_convert_fusion
  30.9 0.8 copy-done.1
  31.7 1.0 fusion.161
  32.8 0.6 fusion.178
  33.3 0.6 multiply_reduce_fusion
  34.0 0.2 fusion.172
  34.1 0.3 fusion.41
  34.4 0.4 fusion.99
  34.9 0.4 fusion.82
  35.3 2.0 convolution_bitcast_fusion.1
  37.2 1.9 convolution_bitcast_fusion
  40.0 0.0 copy-start.3
  40.0 0.6 copy-done.3
  40.6 0.0 all-reduce.5.cloned.1.call-update
  40.6 0.0 reduce-scatter.3.cloned.1.call-start
  40.7 4.8 pad_maximum_fusion
  45.5 0.0 reduce-scatter.3.cloned.1.call-update
  45.5 0.0 all-reduce.7.cloned.1.call-start
  45.7 1.3 dynamic-slice
  47.7 1.3 collective-permute-start.5
  49.0 5.2 %collective-permute-start.4 = (f32[3,16,384]{2,1,0:T(8,128)S(1)}, f32[3,16,384]{2,1,0:T(8,128)S(1)}, u32[]{:S(2)}, u32[]{:S(2)}) collective-permute-start(f32[3,16,384]{2,1,0:T(8,128)S(1)} %bitcast.130), channel_id=1, source_target_pairs={{0,128},{128,256},{256,384},{384,512},{512,640},{640,768},{768,896... | collective-permute-start | bytes 221192 | tf_op jit(solution)/shard_map/ppermute | solution.py:19
  54.2 126.8 %all-reduce.1 = (f32[5,384]{1,0:T(8,128)S(1)}, f32[1536]{0:T(1024)S(1)}) all-reduce(f32[5,384]{1,0:T(8,128)S(1)} %stack.291, f32[1536]{0:T(1024)S(1)} %get-tuple-element.133), channel_id=1, replica_groups=mesh['rows'=8,'cols'=8,'rep'=16] {'rows','cols','rep'}, use_global_device_ids=true, to_apply=%region_61.0 | all-reduce | flops 3456 | bytes 27648 | tf_op jit(solution)/shard_map/psum | solution.py:160
  181.1 0.6 broadcast_multiply_fusion.1
  181.7 0.6 broadcast_multiply_fusion.2
  182.3 0.0 collective-permute-done.5
  182.3 1.3 collective-permute-start.6
  183.6 4.0 collective-permute-start.7
  187.6 143.3 %all-reduce.5.cloned.1.call-done = f32[7,7,384]{2,1,0:T(8,128)} async-done(((f32[7,7,384]{2,1,0:T(8,128)}), f32[7,7,384]{2,1,0:T(8,128)}) %all-reduce.5.cloned.1.call-update) | async-done | bytes 75280 | tf_op jit(solution)/shard_map/psum | solution.py:160
  330.9 1.5 broadcast_multiply_fusion
  332.4 0.0 collective-permute-done.6
  332.4 0.1 pad_maximum_fusion.1
  332.5 0.0 reduce-scatter.3.cloned.1.call-done
  332.6 0.0 all-reduce.7.cloned.1.call-update
  332.6 2.0 fusion.169
  334.6 152.2 %all-reduce.7.cloned.1.call-done = f32[2,24,1536]{2,1,0:T(8,128)} async-done(((f32[2,24,1536]{2,1,0:T(8,128)}), f32[2,24,1536]{2,1,0:T(8,128)}) %all-reduce.7.cloned.1.call-update) | async-done | bytes 294928
  486.8 1.4 fusion.170
  (90 shorter events, 0.7 us)
Async XLA Ops:
  8.0 22.4 %copy-start = (bf16[384,1536]{1,0:T(8,128)(2,1)S(1)}, bf16[384,1536]{1,0:T(8,128)(2,1)}, u32[]{:S(2)}) copy-start(bf16[384,1536]{1,0:T(8,128)(2,1)} %param.16) | copy-start | bytes 3538948
  8.0 20.3 %copy-start.7 = (f32[384]{0:T(512)S(1)}, f32[384]{0:T(512)}, u32[]{:S(2)}) copy-start(f32[384]{0:T(512)} %param.13) | copy-start | bytes 4612
  8.0 322.9 %all-reduce.5.cloned.1.call-start = ((), (), s32[]{:S(2)}) async-start(), calls=%async_computation.2 | async-start | bytes 172032 | tf_op jit(solution)/shard_map/psum | solution.py:160
  9.0 11.0 %collective-permute-start.1 = (bf16[1,3,16,384]{3,2,1,0:T(8,128)(2,1)S(1)}, bf16[1,3,16,384]{3,2,1,0:T(8,128)(2,1)S(1)}, u32[]{:S(2)}, u32[]{:S(2)}) collective-permute-start(bf16[1,3,16,384]{3,2,1,0:T(8,128)(2,1)S(1)} %get-tuple-element.128), channel_id=1, source_target_pairs={{128,0},{256,128},{384,256},{512,384},{640,512},{768,640},{896,768... | collective-permute-start | bytes 110600 | tf_op jit(solution)/shard_map/ppermute | solution.py:21
  10.2 8.7 %collective-permute-start = (bf16[1,3,16,384]{3,2,1,0:T(8,128)(2,1)S(1)}, bf16[1,3,16,384]{3,2,1,0:T(8,128)(2,1)S(1)}, u32[]{:S(2)}, u32[]{:S(2)}) collective-permute-start(bf16[1,3,16,384]{3,2,1,0:T(8,128)(2,1)S(1)} %get-tuple-element.129), channel_id=1, source_target_pairs={{0,128},{128,256},{256,384},{384,512},{512,640},{640,768},{768,896... | collective-permute-start | bytes 110600 | tf_op jit(solution)/shard_map/ppermute | solution.py:19
  20.0 5.4 %collective-permute-start.2 = (bf16[1,14,3,384]{3,2,1,0:T(4,128)(2,1)S(1)}, bf16[1,14,3,384]{3,2,1,0:T(4,128)(2,1)S(1)}, u32[]{:S(2)}, u32[]{:S(2)}) collective-permute-start(bf16[1,14,3,384]{3,2,1,0:T(4,128)(2,1)S(1)} %get-tuple-element.125), channel_id=1, source_target_pairs={{0,16},{16,32},{32,48},{48,64},{64,80},{80,96},{96,112},{1,17},{17... | collective-permute-start | bytes 96776 | tf_op jit(solution)/shard_map/ppermute | solution.py:19
  23.1 5.1 %collective-permute-start.3 = (bf16[1,14,3,384]{3,2,1,0:T(4,128)(2,1)S(1)}, bf16[1,14,3,384]{3,2,1,0:T(4,128)(2,1)S(1)}, u32[]{:S(2)}, u32[]{:S(2)}) collective-permute-start(bf16[1,14,3,384]{3,2,1,0:T(4,128)(2,1)S(1)} %get-tuple-element.126), channel_id=1, source_target_pairs={{16,0},{32,16},{48,32},{64,48},{80,64},{96,80},{112,96},{17,1},{33... | collective-permute-start | bytes 96776 | tf_op jit(solution)/shard_map/ppermute | solution.py:21
  28.3 2.0 copy-start.4
  28.3 2.0 copy-start.8
  28.4 2.1 copy-start.5
  30.5 1.3 copy-start.1
  30.5 1.3 copy-start.2
  30.5 1.3 copy-start.6
  30.5 1.2 copy-start.9
  40.0 0.6 copy-start.3
  40.6 291.9 %reduce-scatter.3.cloned.1.call-start = ((), (), s32[]{:S(2)}) async-start(), calls=%async_computation.1 | async-start | bytes 5013504 | tf_op jit(solution)/shard_map/reduce_scatter | solution.py:158
  45.5 441.3 %all-reduce.7.cloned.1.call-start = ((), (), s32[]{:S(2)}) async-start(), calls=%async_computation.3 | async-start | bytes 589824
  47.7 134.6 %collective-permute-start.5 = (f32[3,16,384]{2,1,0:T(8,128)S(1)}, f32[3,16,384]{2,1,0:T(8,128)S(1)}, u32[]{:S(2)}, u32[]{:S(2)}) collective-permute-start(f32[3,16,384]{2,1,0:T(8,128)S(1)} %bitcast.131), channel_id=1, source_target_pairs={{128,0},{256,128},{384,256},{512,384},{640,512},{768,640},{896,768... | collective-permute-start | bytes 221192 | tf_op jit(solution)/shard_map/ppermute | solution.py:21
  49.0 133.3 %collective-permute-start.4 = (f32[3,16,384]{2,1,0:T(8,128)S(1)}, f32[3,16,384]{2,1,0:T(8,128)S(1)}, u32[]{:S(2)}, u32[]{:S(2)}) collective-permute-start(f32[3,16,384]{2,1,0:T(8,128)S(1)} %bitcast.130), channel_id=1, source_target_pairs={{0,128},{128,256},{256,384},{384,512},{512,640},{640,768},{768,896... | collective-permute-start | bytes 221192 | tf_op jit(solution)/shard_map/ppermute | solution.py:19
  182.3 150.1 %collective-permute-start.6 = (f32[14,3,384]{2,1,0:T(4,128)S(1)}, f32[14,3,384]{2,1,0:T(4,128)S(1)}, u32[]{:S(2)}, u32[]{:S(2)}) collective-permute-start(f32[14,3,384]{2,1,0:T(4,128)S(1)} %get-tuple-element.117), channel_id=1, source_target_pairs={{16,0},{32,16},{48,32},{64,48},{80,64},{96,80},{112,96},{17,1},{33... | collective-permute-start | bytes 193544 | tf_op jit(solution)/shard_map/ppermute | solution.py:21
  183.6 148.8 %collective-permute-start.7 = (f32[14,3,384]{2,1,0:T(4,128)S(1)}, f32[14,3,384]{2,1,0:T(4,128)S(1)}, u32[]{:S(2)}, u32[]{:S(2)}) collective-permute-start(f32[14,3,384]{2,1,0:T(4,128)S(1)} %get-tuple-element.118), channel_id=1, source_target_pairs={{0,16},{16,32},{32,48},{48,64},{64,80},{80,96},{96,112},{1,17},{17... | collective-permute-start | bytes 193544 | tf_op jit(solution)/shard_map/ppermute | solution.py:19
Sparse Core Ops, SparseCore 0:
  40.8 290.0 all-reduce.4
Sparse Core Ops, SparseCore 1:
  45.6 80.0 reduce-scatter.2
  332.7 154.1 all-reduce.6
where the time goes:
time: 500 us; the launch traced here: 496 us
  waiting for transfers between devices  298 us (60%)
  blocking collectives  127 us (25%)
  starting transfers between devices  24 us (5%)
  between operations  16.9 us (3%)
  other arithmetic  14.5 us (3%)
  local copies, waits for them, and re-layouts  8.55 us (2%)
  matrix products  6.5 us (1%)
    unnamed x4, waiting for transfers between devices  152 us
    psum x1, waiting for transfers between devices, per_device(): lax.psum((gker, vectors, gbexp), ('rows', 'cols', 'rep'))  143 us
    psum x1, blocking collectives, per_device(): lax.psum((gker, vectors, gbexp), ('rows', 'cols', 'rep'))  127 us
    ppermute x4, starting transfers between devices, extended(): lax.ppermute(tail, axis, [(i, (i + 1) % count) for i in range(ends)])  18.7 us
  transfers between devices with their start and end apart: 11, of which 3 were waited for; matrix products, arithmetic and copies ran while one was open for 3% of the time, Pallas kernels for 0%

commit v1 on v0

v1 whole, which is shorter than its diff:
```python
import functools

import jax
import jax.numpy as jnp
from jax import lax
from jax.experimental import pallas as pl
from jax.experimental.pallas import tpu as pltpu
from jax.sharding import Mesh
from jax.sharding import PartitionSpec as P

EPS = 1e-06
INV_ROOT_TWO = 0.7071067811865476
INV_ROOT_TWO_PI = 0.3989422804014327
F32 = jnp.float32
BF16 = jnp.bfloat16
D = 384
FF = 1536
LANES = 128
BLOCKS = D // LANES
HALO = 3
PIECES = 64
FROWS = FF // PIECES
DROWS = 24
BIG = BLOCKS * FROWS
ROWS = BIG + 8
LIMIT = pltpu.CompilerParams(vmem_limit_bytes=50 * 1024 * 1024)


def matmul(a, b, ca, cb):
    return lax.dot_general(a, b, (((ca,), (cb,)), ((), ())), preferred_element_type=F32)


def front_kernel(
    core_ref,
    x_ref,
    top_ref,
    bot_ref,
    left_ref,
    right_ref,
    cot_ref,
    dwk_ref,
    dwb_ref,
    gain_ref,
    lnb_ref,
    wexp_ref,
    bexp_ref,
    wred_ref,
    bred_ref,
    ls_ref,
    idx_ref,
    block_ref,
    gconv_ref,
    mine_ref,
    send_ref,
    xp,
    conv,
    both,
    small,
):
    height, width = x_ref.shape[0], x_ref.shape[1]
    pixels = height * width
    xp[HALO : HALO + height, HALO : HALO + width, :] = x_ref[...].astype(F32)
    xp[0:HALO, HALO : HALO + width, :] = top_ref[...].astype(F32)
    xp[HALO + height :, HALO : HALO + width, :] = bot_ref[...].astype(F32)
    xp[:, 0:HALO, :] = left_ref[...].astype(F32)
    xp[:, HALO + width : 2 * HALO + width, :] = right_ref[...].astype(F32)
    for l in range(BLOCKS):
        ln = slice(LANES * l, LANES * (l + 1))
        acc = jnp.zeros((height, width, LANES), F32)
        for j in range(7):
            s = xp[:, j : j + width, ln]
            for i in range(7):
                acc = acc + dwk_ref[i, j : j + 1, ln] * s[i : i + height]
        conv[:, ln] = acc.reshape(pixels, LANES)
    flat = conv[...] + dwb_ref[...]
    centered = flat - jnp.mean(flat, axis=-1, keepdims=True)
    inv = lax.rsqrt(jnp.mean(centered * centered, axis=-1, keepdims=True) + EPS)
    xhat = centered * inv
    normed = (xhat * gain_ref[...] + lnb_ref[...]).astype(BF16)
    grad = cot_ref[...].astype(F32).reshape(pixels, D)
    scaled = grad * ls_ref[...]
    g_branch = scaled.astype(BF16)
    small[...] = jnp.zeros_like(small)
    for f in range(4):
        sl = slice(D * f, D * (f + 1))
        pre = matmul(normed, wexp_ref[:, sl], 1, 0) + bexp_ref[:, sl]
        cdf = 0.5 * (1.0 + lax.erf(pre * INV_ROOT_TWO))
        pdf = jnp.exp(-0.5 * pre * pre) * INV_ROOT_TWO_PI
        g_act = matmul(g_branch, wred_ref[sl, :], 1, 1)
        g_pre = g_act * (cdf + pre * pdf)
        both[0:pixels, sl] = g_pre.astype(BF16)
        both[pixels : 2 * pixels, sl] = (pre * cdf).astype(BF16)
        row = jnp.sum(g_pre, axis=0, keepdims=True)
        for l in range(BLOCKS):
            small[54 + f, l : l + 1, :] = row[:, LANES * l : LANES * (l + 1)]
    branch = matmul(both[pixels : 2 * pixels, :], wred_ref[...], 1, 0) + bred_ref[...]
    block = x_ref[...].astype(F32).reshape(pixels, D) + ls_ref[...] * branch
    block_ref[...] = block.astype(BF16).reshape(height, width, D)
    g_norm = matmul(both[0:pixels, :], wexp_ref[...], 1, 1)
    gx = g_norm * gain_ref[...]
    gconv = inv * (
        gx
        - jnp.mean(gx, axis=-1, keepdims=True)
        - xhat * jnp.mean(gx * xhat, axis=-1, keepdims=True)
    )
    gconv_ref[...] = gconv.reshape(height, width, D)
    sums = (gconv, g_norm * xhat, g_norm, scaled, grad * branch)
    for k, value in enumerate(sums):
        row = jnp.sum(value, axis=0, keepdims=True)
        for l in range(BLOCKS):
            small[49 + k, l : l + 1, :] = row[:, LANES * l : LANES * (l + 1)]
    for l in range(BLOCKS):
        ln = slice(LANES * l, LANES * (l + 1))
        g3 = gconv_ref[:, :, ln]
        for j in range(7):
            s = xp[:, j : j + width, ln]
            for i in range(7):
                part = jnp.sum(g3 * s[i : i + height], axis=0)
                small[7 * i + j, l : l + 1, :] = jnp.sum(part, axis=0, keepdims=True)
    value = small[:, 0:BLOCKS, :]
    low = value - value.astype(BF16).astype(F32)
    mine_ref[:, BIG:ROWS, :] = small[...]
    small[:, BLOCKS : 2 * BLOCKS, :] = low
    send_ref[:, BIG:ROWS, :] = small[...].astype(BF16)
    chan = lax.broadcasted_iota(jnp.int32, (D, D), 0)
    for other in range(2):
        shift = DROWS * core_ref[0] if other == 0 else DROWS * (1 - core_ref[0])
        pick_e = (chan == idx_ref[0:1, :] + shift).astype(F32).astype(BF16)
        pick_r = (chan == idx_ref[1:2, :] + shift).astype(F32).astype(BF16)
        right = jnp.concatenate(
            [matmul(normed, pick_e, 1, 0).astype(BF16), matmul(g_branch, pick_r, 1, 0).astype(BF16)],
            axis=0,
        )
        out = mine_ref if other == 0 else send_ref
        for f in range(4):
            g = matmul(both[:, D * f : D * (f + 1)], right, 0, 0).reshape(D // FROWS, FROWS, D)
            for l in range(BLOCKS):
                out[16 * f : 16 * (f + 1), FROWS * l : FROWS * (l + 1), :] = g[
                    :, :, LANES * l : LANES * (l + 1)
                ].astype(out.dtype)


def join_kernel(mine_ref, got_ref, out_ref):
    out_ref[:, 0:BIG, :] = (mine_ref[:, 0:BIG, :] + got_ref[:, 0:BIG, :].astype(F32)).astype(BF16)
    got = got_ref[:, BIG:ROWS, :].astype(F32)
    value = mine_ref[:, BIG : BIG + BLOCKS, :] + got[:, 0:BLOCKS] + got[:, BLOCKS : 2 * BLOCKS]
    low = value - value.astype(BF16).astype(F32)
    rest = jnp.zeros((value.shape[0], 8 - 2 * BLOCKS, LANES), F32)
    out_ref[:, BIG:ROWS, :] = jnp.concatenate([value, low, rest], axis=1).astype(BF16)


def tile_sum_kernel(got_ref, out_ref):
    total = jnp.sum(got_ref[...].astype(F32), axis=0)
    wide = jnp.concatenate(
        [total[FROWS * l : FROWS * (l + 1), :] for l in range(BLOCKS)], axis=1
    )
    small = total[BIG : BIG + BLOCKS, :] + total[BIG + BLOCKS : BIG + 2 * BLOCKS, :]
    for y in range(out_ref.shape[0]):
        out_ref[y, 0:FROWS, 0 : 2 * DROWS] = wide[:, 2 * DROWS * y : 2 * DROWS * (y + 1)]
        out_ref[y, 0:FROWS, 2 * DROWS :] = jnp.zeros((FROWS, LANES - 2 * DROWS), F32)
        out_ref[y, FROWS:, :] = jnp.zeros((8, LANES), F32)
        out_ref[y, FROWS : FROWS + BLOCKS, :] = small


def region_sum_kernel(scale, got_ref, ge_ref, gr_ref, small_ref):
    total = jnp.sum(got_ref[...], axis=0) * scale
    turned = jnp.transpose(total, (1, 0))
    ge_ref[...] = turned[0:DROWS, 0:FROWS]
    gr_ref[...] = turned[DROWS : 2 * DROWS, 0:FROWS]
    small_ref[...] = jnp.broadcast_to(total[FROWS : FROWS + BLOCKS, :], small_ref.shape)


def spread_kernel(got_ref, gker_ref, vec_ref, gbexp_ref):
    for l in range(BLOCKS):
        ln = slice(LANES * l, LANES * (l + 1))
        for i in range(7):
            for j in range(7):
                gker_ref[i, j : j + 1, ln] = got_ref[7 * i + j, l : l + 1, :]
        for k in range(5):
            vec_ref[k : k + 1, ln] = got_ref[49 + k, l : l + 1, :]
        for f in range(4):
            at = D * f + LANES * l
            gbexp_ref[0:1, at : at + LANES] = got_ref[54 + f, l : l + 1, :]


def input_grad_kernel(g_ref, top_ref, bot_ref, left_ref, right_ref, cot_ref, dwk_ref, out_ref, gp):
    height, width = g_ref.shape[0], g_ref.shape[1]
    gp[HALO : HALO + height, HALO : HALO + width, :] = g_ref[...]
    gp[0:HALO, HALO : HALO + width, :] = top_ref[...]
    gp[HALO + height :, HALO : HALO + width, :] = bot_ref[...]
    gp[:, 0:HALO, :] = left_ref[...]
    gp[:, HALO + width : 2 * HALO + width, :] = right_ref[...]
    for l in range(BLOCKS):
        ln = slice(LANES * l, LANES * (l + 1))
        acc = cot_ref[:, :, ln].astype(F32)
        for j in range(7):
            s = gp[:, 6 - j : 6 - j + width, ln]
            for i in range(7):
                acc = acc + dwk_ref[i, j : j + 1, ln] * s[6 - i : 6 - i + height]
        out_ref[:, :, ln] = acc.astype(BF16)


def shifted(cells, axis, dim):
    count = lax.axis_size(axis)
    size = cells.shape[dim]
    head = lax.slice_in_dim(cells, 0, HALO, axis=dim)
    tail = lax.slice_in_dim(cells, size - HALO, size, axis=dim)
    before = lax.ppermute(tail, axis, [(i, i + 1) for i in range(count - 1)])
    after = lax.ppermute(head, axis, [(i + 1, i) for i in range(count - 1)])
    return before, after


def column_halo(cells, top, bot):
    width = cells.shape[1]
    head = jnp.concatenate([a[:, 0:HALO] for a in (top, cells, bot)], axis=0)
    tail = jnp.concatenate([a[:, width - HALO :] for a in (top, cells, bot)], axis=0)
    count = lax.axis_size("cols")
    left = lax.ppermute(tail, "cols", [(i, i + 1) for i in range(count - 1)])
    right = lax.ppermute(head, "cols", [(i + 1, i) for i in range(count - 1)])
    return left, right


def per_device(
    scale,
    feature_map,
    dw_kernel,
    dw_bias,
    layer_norm_gain,
    layer_norm_bias,
    w_expand,
    b_expand,
    w_reduce,
    b_reduce,
    layer_scale,
    cotangent,
):
    x, cot = feature_map[0], cotangent[0]
    height, width = x.shape[0], x.shape[1]
    regions = lax.axis_size("y")
    core = lax.axis_index("core").astype(jnp.int32)
    top, bot = shifted(x, "rows", 0)
    left, right = column_halo(x, top, bot)

    column = jnp.arange(D, dtype=jnp.int32)
    block, kind, inside = column // (2 * DROWS), (column // DROWS) % 2, column % DROWS
    base = 2 * DROWS * block + inside
    away = jnp.int32(-4 * D)
    index = jnp.stack([jnp.where(kind == 0, base, away), jnp.where(kind == 1, base, away)])

    row = lambda v: v.reshape(1, -1)
    whole = lambda n: [pl.BlockSpec(memory_space=pltpu.VMEM)] * n
    block_out, gconv, mine, send = pl.pallas_call(
        front_kernel,
        out_shape=(
            jax.ShapeDtypeStruct((height, width, D), BF16),
            jax.ShapeDtypeStruct((height, width, D), F32),
            jax.ShapeDtypeStruct((PIECES, ROWS, LANES), F32),
            jax.ShapeDtypeStruct((PIECES, ROWS, LANES), BF16),
        ),
        in_specs=[pl.BlockSpec(memory_space=pltpu.SMEM)] + whole(16),
        out_specs=tuple(whole(4)),
        scratch_shapes=[
            pltpu.VMEM((height + 2 * HALO, width + 8, D), F32),
            pltpu.VMEM((height * width, D), F32),
            pltpu.VMEM((2 * height * width, FF), BF16),
            pltpu.VMEM((PIECES, 8, LANES), F32),
        ],
        compiler_params=LIMIT,
        name="front",
    )(
        core.reshape(1),
        x,
        top,
        bot,
        left,
        right,
        cot,
        dw_kernel,
        row(dw_bias),
        row(layer_norm_gain),
        row(layer_norm_bias),
        w_expand,
        row(b_expand),
        w_reduce,
        row(b_reduce),
        row(layer_scale),
        index,
    )

    got = lax.ppermute(send, "core", [(0, 1), (1, 0)])
    gtop, gbot = shifted(gconv, "rows", 0)
    gleft, gright = column_halo(gconv, gtop, gbot)

    step = 16
    spec = pl.BlockSpec((step, ROWS, LANES), lambda i: (i, 0, 0))
    joined = pl.pallas_call(
        join_kernel,
        out_shape=jax.ShapeDtypeStruct((PIECES, ROWS, LANES), BF16),
        grid=(PIECES // step,),
        in_specs=[spec, spec],
        out_specs=spec,
        compiler_params=LIMIT,
        name="join",
    )(mine, got)
    tiles = lax.all_to_all(joined, ("rows", "cols"), 0, 0, tiled=True)
    by_region = pl.pallas_call(
        tile_sum_kernel,
        out_shape=jax.ShapeDtypeStruct((regions, FROWS + 8, LANES), F32),
        in_specs=whole(1),
        out_specs=whole(1)[0],
        compiler_params=LIMIT,
        name="tile_sum",
    )(tiles)
    by_region = lax.all_to_all(by_region, "y", 0, 0, tiled=True)
    grad_expand, grad_reduce_t, small = pl.pallas_call(
        functools.partial(region_sum_kernel, scale),
        out_shape=(
            jax.ShapeDtypeStruct((DROWS, FROWS), F32),
            jax.ShapeDtypeStruct((DROWS, FROWS), F32),
            jax.ShapeDtypeStruct((PIECES, BLOCKS, LANES), F32),
        ),
        in_specs=whole(1),
        out_specs=tuple(whole(3)),
        compiler_params=LIMIT,
        name="region_sum",
    )(by_region)
    small = lax.all_to_all(small, ("rows", "cols"), 0, 0, tiled=True)
    gker, vectors, gbexp = pl.pallas_call(
        spread_kernel,
        out_shape=(
            jax.ShapeDtypeStruct((7, 7, D), F32),
            jax.ShapeDtypeStruct((5, D), F32),
            jax.ShapeDtypeStruct((1, FF), F32),
        ),
        in_specs=whole(1),
        out_specs=tuple(whole(3)),
        compiler_params=LIMIT,
        name="spread",
    )(small)
    grad_in = pl.pallas_call(
        input_grad_kernel,
        out_shape=jax.ShapeDtypeStruct((height, width, D), BF16),
        in_specs=whole(7),
        out_specs=whole(1)[0],
        scratch_shapes=[pltpu.VMEM((height + 2 * HALO, width + 8, D), F32)],
        compiler_params=LIMIT,
        name="input_grad",
    )(gconv, gtop, gbot, gleft, gright, cot, dw_kernel)
    return (
        block_out[None],
        grad_in[None],
        grad_expand,
        grad_reduce_t,
        gker,
        vectors,
        gbexp.reshape(FF),
    )


def solution(mesh):
    shape = dict(mesh.shape)
    fine = Mesh(
        mesh.devices.reshape(shape["rows"], shape["cols"], shape["rep"] // 2, 2),
        ("rows", "cols", "y", "core"),
    )
    tile = P(("y", "core"), "rows", "cols", None)
    grad = P(("y", "core"), ("rows", "cols"))
    pixels = 16 * 64 * 128
    scale = float(pixels) ** -0.5
    return jax.shard_map(
        functools.partial(per_device, scale),
        mesh=fine,
        in_specs=(tile,) + (P(),) * 9 + (tile,),
        out_specs=(tile, tile, grad, grad, P(), P(), P()),
        check_vma=False,
    )
```

time: 500 us -> 143 us (0.29)
  the two profiles are of different devices: /device:TPU:1 before, /device:TPU:6 now
where the time goes in v1:
time: 143 us; the launch traced here: 142 us
  starting transfers between devices  64.7 us (45%)
  waiting for transfers between devices  48.7 us (34%)
  Pallas kernels  16.1 us (11%)
  local copies, waits for them, and re-layouts  11.1 us (8%)
    all_to_all x1, waiting for transfers between devices, per_device(): tiles = lax.all_to_all(joined, ('rows', 'cols'), 0, 0, tiled=True)  29 us
    all_to_all x1, starting transfers between devices, per_device(): tiles = lax.all_to_all(joined, ('rows', 'cols'), 0, 0, tiled=True)  20.8 us
    ppermute x2, starting transfers between devices, shifted(): before = lax.ppermute(tail, axis, [(i, i + 1) for i in range(count - 1)])  10.5 us
    ppermute x2, starting transfers between devices, column_halo(): left = lax.ppermute(tail, 'cols', [(i, i + 1) for i in range(count - 1)])  9.19 us
    all_to_all x1, waiting for transfers between devices, per_device(): by_region = lax.all_to_all(by_region, 'y', 0, 0, tiled=True)  9.03 us
    all_to_all x1, starting transfers between devices, per_device(): small = lax.all_to_all(small, ('rows', 'cols'), 0, 0, tiled=True)  8.32 us
    pallas_call x1, Pallas kernels, per_device(): pl.pallas_call(front_kernel, out_shape=(jax.ShapeDtypeStruct((height, wid...  7.78 us
    all_to_all x1, starting transfers between devices, per_device(): by_region = lax.all_to_all(by_region, 'y', 0, 0, tiled=True)  7.57 us
  transfers between devices with their start and end apart: 12, of which 7 were waited for; matrix products, arithmetic and copies ran while one was open for 4% of the time, Pallas kernels for 2%

profile of v1, /device:TPU:6, one launch (start us, length us, event | category | flops | bytes accessed | tf_op | source)
XLA Modules:
  0.0 142.2 jit_solution(13393888641930734999)
XLA Ops:
  0.6 0.8 slice_bitcast_fusion
  1.4 1.3 collective-permute-start.1
  2.7 5.8 %collective-permute-start = (bf16[3,16,384]{2,1,0:T(8,128)(2,1)S(1)}, bf16[3,16,384]{2,1,0:T(8,128)(2,1)S(1)}, u32[]{:S(2)}, u32[]{:S(2)}) collective-permute-start(bf16[3,16,384]{2,1,0:T(8,128)(2,1)S(1)} %get-tuple-element.34), channel_id=1, source_target_pairs={{0,128},{128,256},{256,384},{384,512},{512,640},{640,768},{768,896... | collective-permute-start | bytes 110600 | tf_op jit(solution)/shard_map/ppermute | solution.py:208
  8.5 0.8 fusion.5
  9.4 0.0 collective-permute-done.1.bot_ref
  9.5 0.7 collective-permute-done.top_ref
  10.2 4.6 %collective-permute-start.2 = (bf16[14,3,384]{2,1,0:T(4,128)(2,1)S(1)}, bf16[14,3,384]{2,1,0:T(4,128)(2,1)S(1)}, u32[]{:S(2)}, u32[]{:S(2)}) collective-permute-start(bf16[14,3,384]{2,1,0:T(4,128)(2,1)S(1)} %pad_maximum_fusion.2), channel_id=1, source_target_pairs={{0,16},{16,32},{32,48},{48,64},{64,80},{80,96},{96,112},{1,17},{17... | collective-permute-start | bytes 96776 | tf_op jit(solution)/shard_map/ppermute | solution.py:218
  14.9 1.9 %collective-permute-start.3 = (bf16[14,3,384]{2,1,0:T(4,128)(2,1)S(1)}, bf16[14,3,384]{2,1,0:T(4,128)(2,1)S(1)}, u32[]{:S(2)}, u32[]{:S(2)}) collective-permute-start(bf16[14,3,384]{2,1,0:T(4,128)(2,1)S(1)} %pad_maximum_fusion.3), channel_id=1, source_target_pairs={{16,0},{32,16},{48,32},{64,48},{80,64},{96,80},{112,96},{17,1},{33... | collective-permute-start | bytes 96776 | tf_op jit(solution)/shard_map/ppermute | solution.py:219
  16.8 0.7 reshape.163.dwb_ref
  17.5 0.7 reshape.164.gain_ref
  18.2 0.7 reshape.165.lnb_ref
  18.9 0.7 reshape.167.bred_ref
  19.6 0.7 reshape.168.ls_ref
  20.3 0.7 reshape.166.bexp_ref
  21.0 0.0 collective-permute-done.2.left_ref
  21.0 1.1 collective-permute-done.3.right_ref
  22.0 0.0 copy-start
  22.0 1.3 copy-done
  23.3 0.0 copy-start.1
  23.3 1.3 copy-done.1
  24.6 0.0 copy-start.2
  24.6 0.9 copy-done.2
  25.4 0.0 copy-start.3
  25.5 0.9 copy-done.3
  26.3 0.0 copy-start.5
  26.3 0.9 copy-done.5
  27.2 7.8 %front.1 = (bf16[8,16,384]{2,1,0:T(8,128)(2,1)}, f32[8,16,384]{2,1,0:T(8,128)S(1)}, f32[64,80,128]{2,1,0:T(8,128)}, bf16[64,80,128]{2,1,0:T(8,128)(2,1)}) custom-call(s32[1]{0:T(128)} %bitcast.core_ref, bf16[8,16,384]{2,1,0:T(8,128)(2,1)S(1)} %bitcast.10, bf16[3,16,384]{2,1,0:T(8,128)(2,1)S(1)} %collective-permute-done.top_ref, ...), custom_call_target="tpu_custom_call" | custom-call | tf_op jit(solution)/shard_map/front/pallas_call | solution.py:252
  35.0 1.9 %collective-permute-start.8 = (bf16[64,80,128]{2,1,0:T(8,128)(2,1)}, bf16[64,80,128]{2,1,0:T(8,128)(2,1)S(1)}, u32[]{:S(2)}, u32[]{:S(2)}) collective-permute-start(bf16[64,80,128]{2,1,0:T(8,128)(2,1)} %get-tuple-element.20), channel_id=1, source_target_pairs={{0,1},{1,0},{2,3},{3,2},{4,5},{5,4},{6,7},{7,6},{8,9},{9,8},{10,11... | collective-permute-start | bytes 3932168 | tf_op jit(solution)/shard_map/ppermute | solution.py:290
  36.9 3.2 %collective-permute-done.8.got_ref = bf16[64,80,128]{2,1,0:T(8,128)(2,1)S(1)} collective-permute-done((bf16[64,80,128]{2,1,0:T(8,128)(2,1)}, bf16[64,80,128]{2,1,0:T(8,128)(2,1)S(1)}, u32[]{:S(2)}, u32[]{:S(2)}) %collective-permute-start.8) | collective-permute-done | bytes 1310752 | tf_op jit(solution)/shard_map/ppermute | solution.py:290
  40.1 3.8 %join.1 = bf16[64,80,128]{2,1,0:T(8,128)(2,1)} custom-call(f32[64,80,128]{2,1,0:T(8,128)} %get-tuple-element.19.mine_ref, bf16[64,80,128]{2,1,0:T(8,128)(2,1)S(1)} %collective-permute-done.8.got_ref), custom_call_target="tpu_custom_call" | custom-call | tf_op jit(solution)/shard_map/join/pallas_call | solution.py:296
  43.9 20.8 %all-to-all-start = ((bf16[64,80,128]{2,1,0:T(8,128)(2,1)}), bf16[64,80,128]{2,1,0:T(8,128)(2,1)S(1)}, u32[]{:S(2)}, u32[]{:S(2)}) async-start(bf16[64,80,128]{2,1,0:T(8,128)(2,1)} %join.1), calls=%async_computation | async-start | bytes 2621440 | tf_op jit(solution)/shard_map/all_to_all | solution.py:305
  64.8 1.3 collective-permute-start.5
  66.1 0.0 copy-start.4
  66.1 0.0 copy-start.6
  66.1 4.7 %collective-permute-start.4 = (f32[3,16,384]{2,1,0:T(8,128)S(1)}, f32[3,16,384]{2,1,0:T(8,128)S(1)}, u32[]{:S(2)}, u32[]{:S(2)}) collective-permute-start(f32[3,16,384]{2,1,0:T(8,128)S(1)} %get-tuple-element.30), channel_id=1, source_target_pairs={{0,128},{128,256},{256,384},{384,512},{512,640},{640,768},{768,896... | collective-permute-start | bytes 221192 | tf_op jit(solution)/shard_map/ppermute | solution.py:208
  70.8 29.0 %all-to-all-done.got_ref = bf16[64,80,128]{2,1,0:T(8,128)(2,1)S(1)} async-done(((bf16[64,80,128]{2,1,0:T(8,128)(2,1)}), bf16[64,80,128]{2,1,0:T(8,128)(2,1)S(1)}, u32[]{:S(2)}, u32[]{:S(2)}) %all-to-all-start) | async-done | bytes 1310752 | tf_op jit(solution)/shard_map/all_to_all | solution.py:305
  99.8 0.9 tile_sum.1
  100.7 7.6 %all-to-all-start.1 = ((f32[8,32,128]{2,1,0:T(8,128)}), f32[8,32,128]{2,1,0:T(8,128)S(1)}, u32[]{:S(2)}, u32[]{:S(2)}) async-start(f32[8,32,128]{2,1,0:T(8,128)} %tile_sum.1), calls=%async_computation.1 | async-start | bytes 262144 | tf_op jit(solution)/shard_map/all_to_all | solution.py:314
  108.3 0.0 collective-permute-done.5.bot_ref
  108.3 0.0 collective-permute-done.4.top_ref
  108.4 9.0 %all-to-all-done.1.got_ref = f32[8,32,128]{2,1,0:T(8,128)S(1)} async-done(((f32[8,32,128]{2,1,0:T(8,128)}), f32[8,32,128]{2,1,0:T(8,128)S(1)}, u32[]{:S(2)}, u32[]{:S(2)}) %all-to-all-start.1) | async-done | bytes 131104 | tf_op jit(solution)/shard_map/all_to_all | solution.py:314
  117.4 0.7 region_sum.1
  118.1 8.3 %all-to-all-start.2 = ((f32[64,3,128]{2,1,0:T(4,128)}), f32[64,3,128]{2,1,0:T(4,128)S(1)}, u32[]{:S(2)}, u32[]{:S(2)}) async-start(f32[64,3,128]{2,1,0:T(4,128)} %get-tuple-element.23), calls=%async_computation.2 | async-start | bytes 262144 | tf_op jit(solution)/shard_map/all_to_all | solution.py:327
  126.5 4.6 %collective-permute-start.6 = (f32[14,3,384]{2,1,0:T(4,128)S(1)}, f32[14,3,384]{2,1,0:T(4,128)S(1)}, u32[]{:S(2)}, u32[]{:S(2)}) collective-permute-start(f32[14,3,384]{2,1,0:T(4,128)S(1)} %pad_maximum_fusion), channel_id=1, source_target_pairs={{0,16},{16,32},{32,48},{48,64},{64,80},{80,96},{96,112},{1,17},{17... | collective-permute-start | bytes 193544 | tf_op jit(solution)/shard_map/ppermute | solution.py:218
  131.1 1.9 %collective-permute-start.7 = (f32[14,3,384]{2,1,0:T(4,128)S(1)}, f32[14,3,384]{2,1,0:T(4,128)S(1)}, u32[]{:S(2)}, u32[]{:S(2)}) collective-permute-start(f32[14,3,384]{2,1,0:T(4,128)S(1)} %pad_maximum_fusion.1), channel_id=1, source_target_pairs={{16,0},{32,16},{48,32},{64,48},{80,64},{96,80},{112,96},{17,1},{33... | collective-permute-start | bytes 193544 | tf_op jit(solution)/shard_map/ppermute | solution.py:219
  133.0 0.1 collective-permute-done.6.left_ref
  133.2 5.5 %collective-permute-done.7.right_ref = f32[14,3,384]{2,1,0:T(4,128)S(1)} collective-permute-done((f32[14,3,384]{2,1,0:T(4,128)S(1)}, f32[14,3,384]{2,1,0:T(4,128)S(1)}, u32[]{:S(2)}, u32[]{:S(2)}) %collective-permute-start.7) | collective-permute-done | bytes 64544 | tf_op jit(solution)/shard_map/ppermute | solution.py:219
  138.7 0.0 copy-done.4
  138.7 0.0 copy-done.6
  138.7 2.1 %input_grad.1 = bf16[8,16,384]{2,1,0:T(8,128)(2,1)} custom-call(f32[8,16,384]{2,1,0:T(8,128)S(1)} %get-tuple-element.18.g_ref, f32[3,16,384]{2,1,0:T(8,128)S(1)} %collective-permute-done.4.top_ref, f32[3,16,384]{2,1,0:T(8,128)S(1)} %collective-permute-done.5.bot_ref, f32[14,3,384]{2,1,0:T(4,128)S(1)} %collective-permute-done.6.left_ref, ...), custom_call_target="tpu_custom_call" | custom-call | tf_op jit(solution)/shard_map/input_grad/pallas_call | solution.py:340
  140.8 0.0 all-to-all-done.2.got_ref
  140.8 0.7 spread.1
  141.5 0.6 reduce
  (12 shorter events, 0.2 us)
Async XLA Ops:
  1.4 8.0 %collective-permute-start.1 = (bf16[3,16,384]{2,1,0:T(8,128)(2,1)S(1)}, bf16[3,16,384]{2,1,0:T(8,128)(2,1)S(1)}, u32[]{:S(2)}, u32[]{:S(2)}) collective-permute-start(bf16[3,16,384]{2,1,0:T(8,128)(2,1)S(1)} %get-tuple-element.33), channel_id=1, source_target_pairs={{128,0},{256,128},{384,256},{512,384},{640,512},{768,640},{896,768... | collective-permute-start | bytes 110600 | tf_op jit(solution)/shard_map/ppermute | solution.py:209
  2.7 7.4 %collective-permute-start = (bf16[3,16,384]{2,1,0:T(8,128)(2,1)S(1)}, bf16[3,16,384]{2,1,0:T(8,128)(2,1)S(1)}, u32[]{:S(2)}, u32[]{:S(2)}) collective-permute-start(bf16[3,16,384]{2,1,0:T(8,128)(2,1)S(1)} %get-tuple-element.34), channel_id=1, source_target_pairs={{0,128},{128,256},{256,384},{384,512},{512,640},{640,768},{768,896... | collective-permute-start | bytes 110600 | tf_op jit(solution)/shard_map/ppermute | solution.py:208
  10.2 10.7 %collective-permute-start.2 = (bf16[14,3,384]{2,1,0:T(4,128)(2,1)S(1)}, bf16[14,3,384]{2,1,0:T(4,128)(2,1)S(1)}, u32[]{:S(2)}, u32[]{:S(2)}) collective-permute-start(bf16[14,3,384]{2,1,0:T(4,128)(2,1)S(1)} %pad_maximum_fusion.2), channel_id=1, source_target_pairs={{0,16},{16,32},{32,48},{48,64},{64,80},{80,96},{96,112},{1,17},{17... | collective-permute-start | bytes 96776 | tf_op jit(solution)/shard_map/ppermute | solution.py:218
  14.9 7.1 %collective-permute-start.3 = (bf16[14,3,384]{2,1,0:T(4,128)(2,1)S(1)}, bf16[14,3,384]{2,1,0:T(4,128)(2,1)S(1)}, u32[]{:S(2)}, u32[]{:S(2)}) collective-permute-start(bf16[14,3,384]{2,1,0:T(4,128)(2,1)S(1)} %pad_maximum_fusion.3), channel_id=1, source_target_pairs={{16,0},{32,16},{48,32},{64,48},{80,64},{96,80},{112,96},{17,1},{33... | collective-permute-start | bytes 96776 | tf_op jit(solution)/shard_map/ppermute | solution.py:219
  22.0 1.3 copy-start
  23.3 1.3 copy-start.1
  24.6 0.9 copy-start.2
  25.4 0.9 copy-start.3
  26.3 0.9 copy-start.5
  35.0 5.1 %collective-permute-start.8 = (bf16[64,80,128]{2,1,0:T(8,128)(2,1)}, bf16[64,80,128]{2,1,0:T(8,128)(2,1)S(1)}, u32[]{:S(2)}, u32[]{:S(2)}) collective-permute-start(bf16[64,80,128]{2,1,0:T(8,128)(2,1)} %get-tuple-element.20), channel_id=1, source_target_pairs={{0,1},{1,0},{2,3},{3,2},{4,5},{5,4},{6,7},{7,6},{8,9},{9,8},{10,11... | collective-permute-start | bytes 3932168 | tf_op jit(solution)/shard_map/ppermute | solution.py:290
  43.9 55.8 %all-to-all-start = ((bf16[64,80,128]{2,1,0:T(8,128)(2,1)}), bf16[64,80,128]{2,1,0:T(8,128)(2,1)S(1)}, u32[]{:S(2)}, u32[]{:S(2)}) async-start(bf16[64,80,128]{2,1,0:T(8,128)(2,1)} %join.1), calls=%async_computation | async-start | bytes 2621440 | tf_op jit(solution)/shard_map/all_to_all | solution.py:305
  64.8 43.6 %collective-permute-start.5 = (f32[3,16,384]{2,1,0:T(8,128)S(1)}, f32[3,16,384]{2,1,0:T(8,128)S(1)}, u32[]{:S(2)}, u32[]{:S(2)}) collective-permute-start(f32[3,16,384]{2,1,0:T(8,128)S(1)} %get-tuple-element.29), channel_id=1, source_target_pairs={{128,0},{256,128},{384,256},{512,384},{640,512},{768,640},{896,768... | collective-permute-start | bytes 221192 | tf_op jit(solution)/shard_map/ppermute | solution.py:209
  66.1 72.6 %copy-start.4 = (bf16[1,8,16,384]{3,2,1,0:T(8,128)(2,1)S(1)}, bf16[1,8,16,384]{3,2,1,0:T(8,128)(2,1)}, u32[]{:S(2)}) copy-start(bf16[1,8,16,384]{3,2,1,0:T(8,128)(2,1)} %param.21) | copy-start | bytes 294916
  66.1 72.6 %copy-start.6 = (f32[7,7,384]{2,1,0:T(8,128)S(1)}, f32[7,7,384]{2,1,0:T(8,128)}, u32[]{:S(2)}) copy-start(f32[7,7,384]{2,1,0:T(8,128)} %dwk_ref.3) | copy-start | bytes 225796
  66.1 42.2 %collective-permute-start.4 = (f32[3,16,384]{2,1,0:T(8,128)S(1)}, f32[3,16,384]{2,1,0:T(8,128)S(1)}, u32[]{:S(2)}, u32[]{:S(2)}) collective-permute-start(f32[3,16,384]{2,1,0:T(8,128)S(1)} %get-tuple-element.30), channel_id=1, source_target_pairs={{0,128},{128,256},{256,384},{384,512},{512,640},{640,768},{768,896... | collective-permute-start | bytes 221192 | tf_op jit(solution)/shard_map/ppermute | solution.py:208
  100.7 16.6 %all-to-all-start.1 = ((f32[8,32,128]{2,1,0:T(8,128)}), f32[8,32,128]{2,1,0:T(8,128)S(1)}, u32[]{:S(2)}, u32[]{:S(2)}) async-start(f32[8,32,128]{2,1,0:T(8,128)} %tile_sum.1), calls=%async_computation.1 | async-start | bytes 262144 | tf_op jit(solution)/shard_map/all_to_all | solution.py:314
  118.1 22.7 %all-to-all-start.2 = ((f32[64,3,128]{2,1,0:T(4,128)}), f32[64,3,128]{2,1,0:T(4,128)S(1)}, u32[]{:S(2)}, u32[]{:S(2)}) async-start(f32[64,3,128]{2,1,0:T(4,128)} %get-tuple-element.23), calls=%async_computation.2 | async-start | bytes 262144 | tf_op jit(solution)/shard_map/all_to_all | solution.py:327
  126.5 6.7 %collective-permute-start.6 = (f32[14,3,384]{2,1,0:T(4,128)S(1)}, f32[14,3,384]{2,1,0:T(4,128)S(1)}, u32[]{:S(2)}, u32[]{:S(2)}) collective-permute-start(f32[14,3,384]{2,1,0:T(4,128)S(1)} %pad_maximum_fusion), channel_id=1, source_target_pairs={{0,16},{16,32},{32,48},{48,64},{64,80},{80,96},{96,112},{1,17},{17... | collective-permute-start | bytes 193544 | tf_op jit(solution)/shard_map/ppermute | solution.py:218
  131.1 7.6 %collective-permute-start.7 = (f32[14,3,384]{2,1,0:T(4,128)S(1)}, f32[14,3,384]{2,1,0:T(4,128)S(1)}, u32[]{:S(2)}, u32[]{:S(2)}) collective-permute-start(f32[14,3,384]{2,1,0:T(4,128)S(1)} %pad_maximum_fusion.1), channel_id=1, source_target_pairs={{16,0},{32,16},{48,32},{64,48},{80,64},{96,80},{112,96},{17,1},{33... | collective-permute-start | bytes 193544 | tf_op jit(solution)/shard_map/ppermute | solution.py:219

commit v2 on v1

--- a/solution.py
+++ b/solution.py
@@ -32,11 +32,26 @@
 
 def front_kernel(
     core_ref,
-    x_ref,
+    x_hbm,
     top_ref,
     bot_ref,
     left_ref,
     right_ref,
+    cot_hbm,
+    dwk_hbm,
+    dwb_hbm,
+    gain_hbm,
+    lnb_hbm,
+    wexp_hbm,
+    bexp_hbm,
+    wred_hbm,
+    bred_hbm,
+    ls_hbm,
+    block_ref,
+    gconv_ref,
+    mine_hbm,
+    send_hbm,
+    x_ref,
     cot_ref,
     dwk_ref,
     dwb_ref,
@@ -47,23 +62,41 @@
     wred_ref,
     bred_ref,
     ls_ref,
-    idx_ref,
-    block_ref,
-    gconv_ref,
-    mine_ref,
-    send_ref,
     xp,
     conv,
     both,
     small,
+    mine_ref,
+    send_ref,
+    sems,
 ):
+    pairs = (
+        (x_hbm, x_ref),
+        (dwk_hbm, dwk_ref),
+        (dwb_hbm, dwb_ref),
+        (gain_hbm, gain_ref),
+        (lnb_hbm, lnb_ref),
+        (cot_hbm, cot_ref),
+        (ls_hbm, ls_ref),
+        (bexp_hbm, bexp_ref),
+        (bred_hbm, bred_ref),
+        (wexp_hbm, wexp_ref),
+        (wred_hbm, wred_ref),
+    )
+    copies = [pltpu.make_async_copy(a, b, sems.at[k]) for k, (a, b) in enumerate(pairs)]
+    for c in copies:
+        c.start()
     height, width = x_ref.shape[0], x_ref.shape[1]
     pixels = height * width
-    xp[HALO : HALO + height, HALO : HALO + width, :] = x_ref[...].astype(F32)
+    row = lambda ref: ref[...].reshape(1, -1)
     xp[0:HALO, HALO : HALO + width, :] = top_ref[...].astype(F32)
     xp[HALO + height :, HALO : HALO + width, :] = bot_ref[...].astype(F32)
     xp[:, 0:HALO, :] = left_ref[...].astype(F32)
     xp[:, HALO + width : 2 * HALO + width, :] = right_ref[...].astype(F32)
+    small[...] = jnp.zeros_like(small)
+    for c in copies[0:2]:
+        c.wait()
+    xp[HALO : HALO + height, HALO : HALO + width, :] = x_ref[...].astype(F32)
     for l in range(BLOCKS):
         ln = slice(LANES * l, LANES * (l + 1))
         acc = jnp.zeros((height, width, LANES), F32)
@@ -72,32 +105,34 @@
             for i in range(7):
                 acc = acc + dwk_ref[i, j : j + 1, ln] * s[i : i + height]
         conv[:, ln] = acc.reshape(pixels, LANES)
-    flat = conv[...] + dwb_ref[...]
+    for c in copies[2:]:
+        c.wait()
+    flat = conv[...] + row(dwb_ref)
     centered = flat - jnp.mean(flat, axis=-1, keepdims=True)
     inv = lax.rsqrt(jnp.mean(centered * centered, axis=-1, keepdims=True) + EPS)
     xhat = centered * inv
-    normed = (xhat * gain_ref[...] + lnb_ref[...]).astype(BF16)
+    gain = row(gain_ref)
+    normed = (xhat * gain + row(lnb_ref)).astype(BF16)
     grad = cot_ref[...].astype(F32).reshape(pixels, D)
-    scaled = grad * ls_ref[...]
+    scaled = grad * row(ls_ref)
     g_branch = scaled.astype(BF16)
-    small[...] = jnp.zeros_like(small)
     for f in range(4):
         sl = slice(D * f, D * (f + 1))
-        pre = matmul(normed, wexp_ref[:, sl], 1, 0) + bexp_ref[:, sl]
+        pre = matmul(normed, wexp_ref[:, sl], 1, 0) + bexp_ref[sl].reshape(1, D)
         cdf = 0.5 * (1.0 + lax.erf(pre * INV_ROOT_TWO))
         pdf = jnp.exp(-0.5 * pre * pre) * INV_ROOT_TWO_PI
         g_act = matmul(g_branch, wred_ref[sl, :], 1, 1)
         g_pre = g_act * (cdf + pre * pdf)
         both[0:pixels, sl] = g_pre.astype(BF16)
         both[pixels : 2 * pixels, sl] = (pre * cdf).astype(BF16)
-        row = jnp.sum(g_pre, axis=0, keepdims=True)
+        total = jnp.sum(g_pre, axis=0, keepdims=True)
         for l in range(BLOCKS):
-            small[54 + f, l : l + 1, :] = row[:, LANES * l : LANES * (l + 1)]
-    branch = matmul(both[pixels : 2 * pixels, :], wred_ref[...], 1, 0) + bred_ref[...]
-    block = x_ref[...].astype(F32).reshape(pixels, D) + ls_ref[...] * branch
+            small[54 + f, l : l + 1, :] = total[:, LANES * l : LANES * (l + 1)]
+    branch = matmul(both[pixels : 2 * pixels, :], wred_ref[...], 1, 0) + row(bred_ref)
+    block = x_ref[...].astype(F32).reshape(pixels, D) + row(ls_ref) * branch
     block_ref[...] = block.astype(BF16).reshape(height, width, D)
     g_norm = matmul(both[0:pixels, :], wexp_ref[...], 1, 1)
-    gx = g_norm * gain_ref[...]
+    gx = g_norm * gain
     gconv = inv * (
         gx
         - jnp.mean(gx, axis=-1, keepdims=True)
@@ -106,9 +141,9 @@
     gconv_ref[...] = gconv.reshape(height, width, D)
     sums = (gconv, g_norm * xhat, g_norm, scaled, grad * branch)
     for k, value in enumerate(sums):
-        row = jnp.sum(value, axis=0, keepdims=True)
+        total = jnp.sum(value, axis=0, keepdims=True)
         for l in range(BLOCKS):
-            small[49 + k, l : l + 1, :] = row[:, LANES * l : LANES * (l + 1)]
+            small[49 + k, l : l + 1, :] = total[:, LANES * l : LANES * (l + 1)]
     for l in range(BLOCKS):
         ln = slice(LANES * l, LANES * (l + 1))
         g3 = gconv_ref[:, :, ln]
@@ -118,38 +153,49 @@
                 part = jnp.sum(g3 * s[i : i + height], axis=0)
                 small[7 * i + j, l : l + 1, :] = jnp.sum(part, axis=0, keepdims=True)
     value = small[:, 0:BLOCKS, :]
-    low = value - value.astype(BF16).astype(F32)
-    mine_ref[:, BIG:ROWS, :] = small[...]
-    small[:, BLOCKS : 2 * BLOCKS, :] = low
-    send_ref[:, BIG:ROWS, :] = small[...].astype(BF16)
+    small[:, BLOCKS : 2 * BLOCKS, :] = value - value.astype(BF16).astype(F32)
+    packed = small[...].astype(BF16)
     chan = lax.broadcasted_iota(jnp.int32, (D, D), 0)
-    for other in range(2):
-        shift = DROWS * core_ref[0] if other == 0 else DROWS * (1 - core_ref[0])
-        pick_e = (chan == idx_ref[0:1, :] + shift).astype(F32).astype(BF16)
-        pick_r = (chan == idx_ref[1:2, :] + shift).astype(F32).astype(BF16)
+    column = lax.broadcasted_iota(jnp.int32, (1, D), 1)
+    block = (column * 1366) >> 16
+    inside = column - 2 * DROWS * block
+    of_e = 2 * DROWS * block + jnp.where(inside < DROWS, inside, -4 * D)
+    of_r = 2 * DROWS * block + jnp.where(inside < DROWS, -4 * D, inside - DROWS)
+    outputs = []
+    for which, (out, hbm) in enumerate(((send_ref, send_hbm), (mine_ref, mine_hbm))):
+        shift = DROWS * core_ref[0] if which == 1 else DROWS * (1 - core_ref[0])
+        out[:, BIG:ROWS, :] = packed
+        pick_e = (chan == of_e + shift).astype(F32).astype(BF16)
+        pick_r = (chan == of_r + shift).astype(F32).astype(BF16)
         right = jnp.concatenate(
             [matmul(normed, pick_e, 1, 0).astype(BF16), matmul(g_branch, pick_r, 1, 0).astype(BF16)],
             axis=0,
         )
-        out = mine_ref if other == 0 else send_ref
         for f in range(4):
             g = matmul(both[:, D * f : D * (f + 1)], right, 0, 0).reshape(D // FROWS, FROWS, D)
+            at = slice(16 * f, 16 * (f + 1))
             for l in range(BLOCKS):
-                out[16 * f : 16 * (f + 1), FROWS * l : FROWS * (l + 1), :] = g[
+                out[at, FROWS * l : FROWS * (l + 1), :] = g[
                     :, :, LANES * l : LANES * (l + 1)
-                ].astype(out.dtype)
+                ].astype(BF16)
+            c = pltpu.make_async_copy(out.at[at], hbm.at[at], sems.at[11 + 4 * which + f])
+            c.start()
+            outputs.append(c)
+    for c in outputs:
+        c.wait()
 
 
 def join_kernel(mine_ref, got_ref, out_ref):
-    out_ref[:, 0:BIG, :] = (mine_ref[:, 0:BIG, :] + got_ref[:, 0:BIG, :].astype(F32)).astype(BF16)
-    got = got_ref[:, BIG:ROWS, :].astype(F32)
-    value = mine_ref[:, BIG : BIG + BLOCKS, :] + got[:, 0:BLOCKS] + got[:, BLOCKS : 2 * BLOCKS]
+    big = mine_ref[:, 0:BIG, :].astype(F32) + got_ref[:, 0:BIG, :].astype(F32)
+    out_ref[:, 0:BIG, :] = big.astype(BF16)
+    both = mine_ref[:, BIG:ROWS, :].astype(F32) + got_ref[:, BIG:ROWS, :].astype(F32)
+    value = both[:, 0:BLOCKS] + both[:, BLOCKS : 2 * BLOCKS]
     low = value - value.astype(BF16).astype(F32)
     rest = jnp.zeros((value.shape[0], 8 - 2 * BLOCKS, LANES), F32)
     out_ref[:, BIG:ROWS, :] = jnp.concatenate([value, low, rest], axis=1).astype(BF16)
 
 
-def tile_sum_kernel(got_ref, out_ref):
+def tile_sum_kernel(got_ref, after_hbm, out_ref):
     total = jnp.sum(got_ref[...].astype(F32), axis=0)
     wide = jnp.concatenate(
         [total[FROWS * l : FROWS * (l + 1), :] for l in range(BLOCKS)], axis=1
@@ -180,7 +226,7 @@
             vec_ref[k : k + 1, ln] = got_ref[49 + k, l : l + 1, :]
         for f in range(4):
             at = D * f + LANES * l
-            gbexp_ref[0:1, at : at + LANES] = got_ref[54 + f, l : l + 1, :]
+            gbexp_ref[at : at + LANES] = got_ref[54 + f, l, :]
 
 
 def input_grad_kernel(g_ref, top_ref, bot_ref, left_ref, right_ref, cot_ref, dwk_ref, out_ref, gp):
@@ -241,50 +287,58 @@
     top, bot = shifted(x, "rows", 0)
     left, right = column_halo(x, top, bot)
 
-    column = jnp.arange(D, dtype=jnp.int32)
-    block, kind, inside = column // (2 * DROWS), (column // DROWS) % 2, column % DROWS
-    base = 2 * DROWS * block + inside
-    away = jnp.int32(-4 * D)
-    index = jnp.stack([jnp.where(kind == 0, base, away), jnp.where(kind == 1, base, away)])
-
-    row = lambda v: v.reshape(1, -1)
     whole = lambda n: [pl.BlockSpec(memory_space=pltpu.VMEM)] * n
+    away = lambda v: pltpu.with_memory_space_constraint(v, pltpu.HBM)
+    hbm = lambda n: [pl.BlockSpec(memory_space=pltpu.HBM)] * n
     block_out, gconv, mine, send = pl.pallas_call(
         front_kernel,
         out_shape=(
             jax.ShapeDtypeStruct((height, width, D), BF16),
             jax.ShapeDtypeStruct((height, width, D), F32),
-            jax.ShapeDtypeStruct((PIECES, ROWS, LANES), F32),
+            jax.ShapeDtypeStruct((PIECES, ROWS, LANES), BF16),
             jax.ShapeDtypeStruct((PIECES, ROWS, LANES), BF16),
         ),
-        in_specs=[pl.BlockSpec(memory_space=pltpu.SMEM)] + whole(16),
-        out_specs=tuple(whole(4)),
+        in_specs=[pl.BlockSpec(memory_space=pltpu.SMEM)] + hbm(1) + whole(4) + hbm(10),
+        out_specs=tuple(whole(2) + hbm(2)),
         scratch_shapes=[
+            pltpu.VMEM((height, width, D), BF16),
+            pltpu.VMEM((height, width, D), BF16),
+            pltpu.VMEM((7, 7, D), F32),
+            pltpu.VMEM((D,), F32),
+            pltpu.VMEM((D,), F32),
+            pltpu.VMEM((D,), F32),
+            pltpu.VMEM((D, FF), BF16),
+            pltpu.VMEM((FF,), F32),
+            pltpu.VMEM((FF, D), BF16),
+            pltpu.VMEM((D,), F32),
+            pltpu.VMEM((D,), F32),
             pltpu.VMEM((height + 2 * HALO, width + 8, D), F32),
             pltpu.VMEM((height * width, D), F32),
             pltpu.VMEM((2 * height * width, FF), BF16),
             pltpu.VMEM((PIECES, 8, LANES), F32),
+            pltpu.VMEM((PIECES, ROWS, LANES), BF16),
+            pltpu.VMEM((PIECES, ROWS, LANES), BF16),
+            pltpu.SemaphoreType.DMA((19,)),
         ],
         compiler_params=LIMIT,
         name="front",
     )(
         core.reshape(1),
-        x,
+        away(x),
         top,
         bot,
         left,
         right,
-        cot,
-        dw_kernel,
-        row(dw_bias),
-        row(layer_norm_gain),
-        row(layer_norm_bias),
-        w_expand,
-        row(b_expand),
-        w_reduce,
-        row(b_reduce),
-        row(layer_scale),
-        index,
+        away(cot),
+        away(dw_kernel),
+        away(dw_bias),
+        away(layer_norm_gain),
+        away(layer_norm_bias),
+        away(w_expand),
+        away(b_expand),
+        away(w_reduce),
+        away(b_reduce),
+        away(layer_scale),
     )
 
     got = lax.ppermute(send, "core", [(0, 1), (1, 0)])
@@ -303,14 +357,23 @@
         name="join",
     )(mine, got)
     tiles = lax.all_to_all(joined, ("rows", "cols"), 0, 0, tiled=True)
+    grad_in = pl.pallas_call(
+        input_grad_kernel,
+        out_shape=jax.ShapeDtypeStruct((height, width, D), BF16),
+        in_specs=whole(7),
+        out_specs=whole(1)[0],
+        scratch_shapes=[pltpu.VMEM((height + 2 * HALO, width + 8, D), F32)],
+        compiler_params=LIMIT,
+        name="input_grad",
+    )(gconv, gtop, gbot, gleft, gright, cot, dw_kernel)
     by_region = pl.pallas_call(
         tile_sum_kernel,
         out_shape=jax.ShapeDtypeStruct((regions, FROWS + 8, LANES), F32),
-        in_specs=whole(1),
+        in_specs=whole(1) + hbm(1),
         out_specs=whole(1)[0],
         compiler_params=LIMIT,
         name="tile_sum",
-    )(tiles)
+    )(tiles, away(grad_in))
     by_region = lax.all_to_all(by_region, "y", 0, 0, tiled=True)
     grad_expand, grad_reduce_t, small = pl.pallas_call(
         functools.partial(region_sum_kernel, scale),
@@ -330,22 +393,13 @@
         out_shape=(
             jax.ShapeDtypeStruct((7, 7, D), F32),
             jax.ShapeDtypeStruct((5, D), F32),
-            jax.ShapeDtypeStruct((1, FF), F32),
+            jax.ShapeDtypeStruct((FF,), F32),
         ),
         in_specs=whole(1),
         out_specs=tuple(whole(3)),
         compiler_params=LIMIT,
         name="spread",
     )(small)
-    grad_in = pl.pallas_call(
-        input_grad_kernel,
-        out_shape=jax.ShapeDtypeStruct((height, width, D), BF16),
-        in_specs=whole(7),
-        out_specs=whole(1)[0],
-        scratch_shapes=[pltpu.VMEM((height + 2 * HALO, width + 8, D), F32)],
-        compiler_params=LIMIT,
-        name="input_grad",
-    )(gconv, gtop, gbot, gleft, gright, cot, dw_kernel)
     return (
         block_out[None],
         grad_in[None],
@@ -353,7 +407,7 @@
         grad_reduce_t,
         gker,
         vectors,
-        gbexp.reshape(FF),
+        gbexp,
     )
 
 

time: 143 us -> 143 us (level)
  the two profiles are of different devices: /device:TPU:6 before, /device:TPU:2 now
where the time goes in v2:
time: 143 us
  starting transfers between devices  51.2 us (36%)
  blocking collectives  46.4 us (32%)
  waiting for transfers between devices  27.5 us (19%)
  Pallas kernels  15 us (10%)
  local copies, waits for them, and re-layouts  1.72 us (1%)
    all_to_all x1, blocking collectives, per_device(): small = lax.all_to_all(small, ('rows', 'cols'), 0, 0, tiled=True)  29.9 us
    ppermute x2, waiting for transfers between devices, shifted(): after = lax.ppermute(head, axis, [(i + 1, i) for i in range(count - 1)])  19 us
    all_to_all x1, blocking collectives, per_device(): by_region = lax.all_to_all(by_region, 'y', 0, 0, tiled=True)  16.4 us
    ppermute x2, starting transfers between devices, column_halo(): right = lax.ppermute(head, 'cols', [(i + 1, i) for i in range(count - 1)])  15 us
    all_to_all x1, starting transfers between devices, per_device(): tiles = lax.all_to_all(joined, ('rows', 'cols'), 0, 0, tiled=True)  14.3 us
    ppermute x2, starting transfers between devices, shifted(): before = lax.ppermute(tail, axis, [(i, i + 1) for i in range(count - 1)])  10.4 us
    pallas_call x1, Pallas kernels, per_device(): pl.pallas_call(front_kernel, out_shape=(jax.ShapeDtypeStruct((height, wid...  9.41 us
    ppermute x2, starting transfers between devices, column_halo(): left = lax.ppermute(tail, 'cols', [(i, i + 1) for i in range(count - 1)])  7.08 us
  transfers between devices with their start and end apart: 10, of which 6 were waited for; matrix products, arithmetic and copies ran while one was open for 1% of the time, Pallas kernels for 1%

profile of v2, /device:TPU:2, one launch (start us, length us, event | category | flops | bytes accessed | tf_op | source)
XLA Modules:
  0.0 142.8 jit_solution(6294386724572422621)
XLA Ops:
  0.6 0.8 slice_bitcast_fusion
  1.4 1.3 collective-permute-start.1
  2.7 5.8 %collective-permute-start = (bf16[3,16,384]{2,1,0:T(8,128)(2,1)S(1)}, bf16[3,16,384]{2,1,0:T(8,128)(2,1)S(1)}, u32[]{:S(2)}, u32[]{:S(2)}) collective-permute-start(bf16[3,16,384]{2,1,0:T(8,128)(2,1)S(1)} %get-tuple-element.34), channel_id=1, source_target_pairs={{0,128},{128,256},{256,384},{384,512},{512,640},{640,768},{768,896... | collective-permute-start | bytes 110600 | tf_op jit(solution)/shard_map/ppermute | solution.py:254
  8.5 0.8 fusion.2
  9.4 0.0 collective-permute-done.1.bot_ref
  9.4 0.7 collective-permute-done.top_ref
  10.2 3.4 %collective-permute-start.2 = (bf16[14,3,384]{2,1,0:T(4,128)(2,1)S(1)}, bf16[14,3,384]{2,1,0:T(4,128)(2,1)S(1)}, u32[]{:S(2)}, u32[]{:S(2)}) collective-permute-start(bf16[14,3,384]{2,1,0:T(4,128)(2,1)S(1)} %pad_maximum_fusion.2), channel_id=1, source_target_pairs={{0,16},{16,32},{32,48},{48,64},{64,80},{80,96},{96,112},{1,17},{17... | collective-permute-start | bytes 96776 | tf_op jit(solution)/shard_map/ppermute | solution.py:264
  13.7 11.7 %collective-permute-start.3 = (bf16[14,3,384]{2,1,0:T(4,128)(2,1)S(1)}, bf16[14,3,384]{2,1,0:T(4,128)(2,1)S(1)}, u32[]{:S(2)}, u32[]{:S(2)}) collective-permute-start(bf16[14,3,384]{2,1,0:T(4,128)(2,1)S(1)} %pad_maximum_fusion.3), channel_id=1, source_target_pairs={{16,0},{32,16},{48,32},{64,48},{80,64},{96,80},{112,96},{17,1},{33... | collective-permute-start | bytes 96776 | tf_op jit(solution)/shard_map/ppermute | solution.py:265
  25.4 0.0 collective-permute-done.2.left_ref
  25.4 1.7 %collective-permute-done.3.right_ref = bf16[14,3,384]{2,1,0:T(4,128)(2,1)S(1)} collective-permute-done((bf16[14,3,384]{2,1,0:T(4,128)(2,1)S(1)}, bf16[14,3,384]{2,1,0:T(4,128)(2,1)S(1)}, u32[]{:S(2)}, u32[]{:S(2)}) %collective-permute-start.3) | collective-permute-done | bytes 32288 | tf_op jit(solution)/shard_map/ppermute | solution.py:265
  27.1 9.4 %front.1 = (bf16[8,16,384]{2,1,0:T(8,128)(2,1)}, f32[8,16,384]{2,1,0:T(8,128)S(1)}, bf16[64,80,128]{2,1,0:T(8,128)(2,1)S(1)}, bf16[64,80,128]{2,1,0:T(8,128)(2,1)S(1)}) custom-call(s32[1]{0:T(128)} %bitcast.core_ref, bf16[8,16,384]{2,1,0:T(8,128)(2,1)} %bitcast.12, bf16[3,16,384]{2,1,0:T(8,128)(2,1)S(1)} %collective-permute-done.top_ref, ...), custom_call_target="tpu_custom_call" | custom-call | tf_op jit(solution)/shard_map/front/pallas_call | solution.py:293
  36.5 1.9 %collective-permute-start.8 = (bf16[64,80,128]{2,1,0:T(8,128)(2,1)S(1)}, bf16[64,80,128]{2,1,0:T(8,128)(2,1)S(1)}, u32[]{:S(2)}, u32[]{:S(2)}) collective-permute-start(bf16[64,80,128]{2,1,0:T(8,128)(2,1)S(1)} %get-tuple-element.20), channel_id=1, source_target_pairs={{0,1},{1,0},{2,3},{3,2},{4,5},{5,4},{6,7},{7,6},{8,9},{9,8},{10,11... | collective-permute-start | bytes 3932168 | tf_op jit(solution)/shard_map/ppermute | solution.py:344
  38.4 3.0 %collective-permute-done.8.got_ref = bf16[64,80,128]{2,1,0:T(8,128)(2,1)S(1)} collective-permute-done((bf16[64,80,128]{2,1,0:T(8,128)(2,1)S(1)}, bf16[64,80,128]{2,1,0:T(8,128)(2,1)S(1)}, u32[]{:S(2)}, u32[]{:S(2)}) %collective-permute-start.8) | collective-permute-done | bytes 1310752 | tf_op jit(solution)/shard_map/ppermute | solution.py:344
  41.4 1.8 %join.1 = bf16[64,80,128]{2,1,0:T(8,128)(2,1)} custom-call(bf16[64,80,128]{2,1,0:T(8,128)(2,1)S(1)} %get-tuple-element.19.mine_ref, bf16[64,80,128]{2,1,0:T(8,128)(2,1)S(1)} %collective-permute-done.8.got_ref), custom_call_target="tpu_custom_call" | custom-call | tf_op jit(solution)/shard_map/join/pallas_call | solution.py:350
  43.2 0.0 copy-start
  43.2 0.0 copy-start.1
  43.2 14.3 %all-to-all-start = ((bf16[64,80,128]{2,1,0:T(8,128)(2,1)}), bf16[64,80,128]{2,1,0:T(8,128)(2,1)S(1)}, u32[]{:S(2)}, u32[]{:S(2)}) async-start(bf16[64,80,128]{2,1,0:T(8,128)(2,1)} %join.1), calls=%async_computation | async-start | bytes 2621440 | tf_op jit(solution)/shard_map/all_to_all | solution.py:359
  57.5 1.3 collective-permute-start.5
  58.9 4.5 %collective-permute-start.4 = (f32[3,16,384]{2,1,0:T(8,128)S(1)}, f32[3,16,384]{2,1,0:T(8,128)S(1)}, u32[]{:S(2)}, u32[]{:S(2)}) collective-permute-start(f32[3,16,384]{2,1,0:T(8,128)S(1)} %get-tuple-element.30), channel_id=1, source_target_pairs={{0,128},{128,256},{256,384},{384,512},{512,640},{640,768},{768,896... | collective-permute-start | bytes 221192 | tf_op jit(solution)/shard_map/ppermute | solution.py:254
  63.4 19.0 %collective-permute-done.5.bot_ref = f32[3,16,384]{2,1,0:T(8,128)S(1)} collective-permute-done((f32[3,16,384]{2,1,0:T(8,128)S(1)}, f32[3,16,384]{2,1,0:T(8,128)S(1)}, u32[]{:S(2)}, u32[]{:S(2)}) %collective-permute-start.5) | collective-permute-done | bytes 73760 | tf_op jit(solution)/shard_map/ppermute | solution.py:255
  82.4 0.0 collective-permute-done.4.top_ref
  82.5 3.7 %collective-permute-start.6 = (f32[14,3,384]{2,1,0:T(4,128)S(1)}, f32[14,3,384]{2,1,0:T(4,128)S(1)}, u32[]{:S(2)}, u32[]{:S(2)}) collective-permute-start(f32[14,3,384]{2,1,0:T(4,128)S(1)} %pad_maximum_fusion), channel_id=1, source_target_pairs={{0,16},{16,32},{32,48},{48,64},{64,80},{80,96},{96,112},{1,17},{17... | collective-permute-start | bytes 193544 | tf_op jit(solution)/shard_map/ppermute | solution.py:264
  86.2 3.2 %collective-permute-start.7 = (f32[14,3,384]{2,1,0:T(4,128)S(1)}, f32[14,3,384]{2,1,0:T(4,128)S(1)}, u32[]{:S(2)}, u32[]{:S(2)}) collective-permute-start(f32[14,3,384]{2,1,0:T(4,128)S(1)} %pad_maximum_fusion.1), channel_id=1, source_target_pairs={{16,0},{32,16},{48,32},{64,48},{80,64},{96,80},{112,96},{17,1},{33... | collective-permute-start | bytes 193544 | tf_op jit(solution)/shard_map/ppermute | solution.py:265
  89.5 0.7 collective-permute-done.6.left_ref
  90.1 2.4 %collective-permute-done.7.right_ref = f32[14,3,384]{2,1,0:T(4,128)S(1)} collective-permute-done((f32[14,3,384]{2,1,0:T(4,128)S(1)}, f32[14,3,384]{2,1,0:T(4,128)S(1)}, u32[]{:S(2)}, u32[]{:S(2)}) %collective-permute-start.7) | collective-permute-done | bytes 64544 | tf_op jit(solution)/shard_map/ppermute | solution.py:265
  92.6 0.0 copy-done
  92.6 0.0 copy-done.1
  92.6 2.1 %input_grad.1.after_hbm = bf16[8,16,384]{2,1,0:T(8,128)(2,1)} custom-call(f32[8,16,384]{2,1,0:T(8,128)S(1)} %get-tuple-element.18.g_ref, f32[3,16,384]{2,1,0:T(8,128)S(1)} %collective-permute-done.4.top_ref, f32[3,16,384]{2,1,0:T(8,128)S(1)} %collective-permute-done.5.bot_ref, f32[14,3,384]{2,1,0:T(4,128)S(1)} %collective-permute-done.6.left_ref, ...), custom_call_target="tpu_custom_call" | custom-call | tf_op jit(solution)/shard_map/input_grad/pallas_call | solution.py:360
  94.7 0.0 all-to-all-done.got_ref
  94.7 0.3 tile_sum.1
  95.0 16.4 %all_to_all.15.got_ref = f32[8,32,128]{2,1,0:T(8,128)S(1)} all-to-all(f32[8,32,128]{2,1,0:T(8,128)S(1)} %tile_sum.1), channel_id=1, replica_groups=mesh['rows'=8,'cols'=8,'y'=8,'core'=2] {'y'}, dimensions={0} | all-to-all | bytes 262144 | tf_op jit(solution)/shard_map/all_to_all | solution.py:377
  111.5 0.7 region_sum.1
  112.2 29.9 %all_to_all.16.got_ref = f32[64,3,128]{2,1,0:T(4,128)S(1)} all-to-all(f32[64,3,128]{2,1,0:T(4,128)S(1)} %get-tuple-element.23), channel_id=1, replica_groups=mesh['rows'=8,'cols'=8,'y'=8,'core'=2] {'rows','cols'}, dimensions={0} | all-to-all | bytes 196608 | tf_op jit(solution)/shard_map/all_to_all | solution.py:390
  142.1 0.7 spread.1
  (10 shorter events, 0.2 us)
Async XLA Ops:
  1.4 8.0 %collective-permute-start.1 = (bf16[3,16,384]{2,1,0:T(8,128)(2,1)S(1)}, bf16[3,16,384]{2,1,0:T(8,128)(2,1)S(1)}, u32[]{:S(2)}, u32[]{:S(2)}) collective-permute-start(bf16[3,16,384]{2,1,0:T(8,128)(2,1)S(1)} %get-tuple-element.33), channel_id=1, source_target_pairs={{128,0},{256,128},{384,256},{512,384},{640,512},{768,640},{896,768... | collective-permute-start | bytes 110600 | tf_op jit(solution)/shard_map/ppermute | solution.py:255
  2.7 7.4 %collective-permute-start = (bf16[3,16,384]{2,1,0:T(8,128)(2,1)S(1)}, bf16[3,16,384]{2,1,0:T(8,128)(2,1)S(1)}, u32[]{:S(2)}, u32[]{:S(2)}) collective-permute-start(bf16[3,16,384]{2,1,0:T(8,128)(2,1)S(1)} %get-tuple-element.34), channel_id=1, source_target_pairs={{0,128},{128,256},{256,384},{384,512},{512,640},{640,768},{768,896... | collective-permute-start | bytes 110600 | tf_op jit(solution)/shard_map/ppermute | solution.py:254
  10.2 15.2 %collective-permute-start.2 = (bf16[14,3,384]{2,1,0:T(4,128)(2,1)S(1)}, bf16[14,3,384]{2,1,0:T(4,128)(2,1)S(1)}, u32[]{:S(2)}, u32[]{:S(2)}) collective-permute-start(bf16[14,3,384]{2,1,0:T(4,128)(2,1)S(1)} %pad_maximum_fusion.2), channel_id=1, source_target_pairs={{0,16},{16,32},{32,48},{48,64},{64,80},{80,96},{96,112},{1,17},{17... | collective-permute-start | bytes 96776 | tf_op jit(solution)/shard_map/ppermute | solution.py:264
  13.7 13.4 %collective-permute-start.3 = (bf16[14,3,384]{2,1,0:T(4,128)(2,1)S(1)}, bf16[14,3,384]{2,1,0:T(4,128)(2,1)S(1)}, u32[]{:S(2)}, u32[]{:S(2)}) collective-permute-start(bf16[14,3,384]{2,1,0:T(4,128)(2,1)S(1)} %pad_maximum_fusion.3), channel_id=1, source_target_pairs={{16,0},{32,16},{48,32},{64,48},{80,64},{96,80},{112,96},{17,1},{33... | collective-permute-start | bytes 96776 | tf_op jit(solution)/shard_map/ppermute | solution.py:265
  36.5 4.9 %collective-permute-start.8 = (bf16[64,80,128]{2,1,0:T(8,128)(2,1)S(1)}, bf16[64,80,128]{2,1,0:T(8,128)(2,1)S(1)}, u32[]{:S(2)}, u32[]{:S(2)}) collective-permute-start(bf16[64,80,128]{2,1,0:T(8,128)(2,1)S(1)} %get-tuple-element.20), channel_id=1, source_target_pairs={{0,1},{1,0},{2,3},{3,2},{4,5},{5,4},{6,7},{7,6},{8,9},{9,8},{10,11... | collective-permute-start | bytes 3932168 | tf_op jit(solution)/shard_map/ppermute | solution.py:344
  43.2 49.4 %copy-start = (bf16[1,8,16,384]{3,2,1,0:T(8,128)(2,1)S(1)}, bf16[1,8,16,384]{3,2,1,0:T(8,128)(2,1)}, u32[]{:S(2)}) copy-start(bf16[1,8,16,384]{3,2,1,0:T(8,128)(2,1)} %param.21) | copy-start | bytes 294916
  43.2 49.4 %copy-start.1 = (f32[7,7,384]{2,1,0:T(8,128)S(1)}, f32[7,7,384]{2,1,0:T(8,128)}, u32[]{:S(2)}) copy-start(f32[7,7,384]{2,1,0:T(8,128)} %dwk_ref.1) | copy-start | bytes 225796
  43.2 51.5 %all-to-all-start = ((bf16[64,80,128]{2,1,0:T(8,128)(2,1)}), bf16[64,80,128]{2,1,0:T(8,128)(2,1)S(1)}, u32[]{:S(2)}, u32[]{:S(2)}) async-start(bf16[64,80,128]{2,1,0:T(8,128)(2,1)} %join.1), calls=%async_computation | async-start | bytes 2621440 | tf_op jit(solution)/shard_map/all_to_all | solution.py:359
  57.5 24.9 %collective-permute-start.5 = (f32[3,16,384]{2,1,0:T(8,128)S(1)}, f32[3,16,384]{2,1,0:T(8,128)S(1)}, u32[]{:S(2)}, u32[]{:S(2)}) collective-permute-start(f32[3,16,384]{2,1,0:T(8,128)S(1)} %get-tuple-element.29), channel_id=1, source_target_pairs={{128,0},{256,128},{384,256},{512,384},{640,512},{768,640},{896,768... | collective-permute-start | bytes 221192 | tf_op jit(solution)/shard_map/ppermute | solution.py:255
  58.9 23.6 %collective-permute-start.4 = (f32[3,16,384]{2,1,0:T(8,128)S(1)}, f32[3,16,384]{2,1,0:T(8,128)S(1)}, u32[]{:S(2)}, u32[]{:S(2)}) collective-permute-start(f32[3,16,384]{2,1,0:T(8,128)S(1)} %get-tuple-element.30), channel_id=1, source_target_pairs={{0,128},{128,256},{256,384},{384,512},{512,640},{640,768},{768,896... | collective-permute-start | bytes 221192 | tf_op jit(solution)/shard_map/ppermute | solution.py:254
  82.5 7.7 %collective-permute-start.6 = (f32[14,3,384]{2,1,0:T(4,128)S(1)}, f32[14,3,384]{2,1,0:T(4,128)S(1)}, u32[]{:S(2)}, u32[]{:S(2)}) collective-permute-start(f32[14,3,384]{2,1,0:T(4,128)S(1)} %pad_maximum_fusion), channel_id=1, source_target_pairs={{0,16},{16,32},{32,48},{48,64},{64,80},{80,96},{96,112},{1,17},{17... | collective-permute-start | bytes 193544 | tf_op jit(solution)/shard_map/ppermute | solution.py:264
  86.2 6.4 %collective-permute-start.7 = (f32[14,3,384]{2,1,0:T(4,128)S(1)}, f32[14,3,384]{2,1,0:T(4,128)S(1)}, u32[]{:S(2)}, u32[]{:S(2)}) collective-permute-start(f32[14,3,384]{2,1,0:T(4,128)S(1)} %pad_maximum_fusion.1), channel_id=1, source_target_pairs={{16,0},{32,16},{48,32},{64,48},{80,64},{96,80},{112,96},{17,1},{33... | collective-permute-start | bytes 193544 | tf_op jit(solution)/shard_map/ppermute | solution.py:265

commit v3 on v2

--- a/solution.py
+++ b/solution.py
@@ -18,11 +18,15 @@
 LANES = 128
 BLOCKS = D // LANES
 HALO = 3
-PIECES = 64
-FROWS = FF // PIECES
+FROWS = 24
 DROWS = 24
-BIG = BLOCKS * FROWS
-ROWS = BIG + 8
+PIECES = 8
+FAR = 64
+BIG = BLOCKS * 8 * FROWS
+SHARE = 12
+ROWS = BIG + 2 * SHARE
+TALL = ("zh", "zl")
+WIDE = ("xh", "xl")
 LIMIT = pltpu.CompilerParams(vmem_limit_bytes=50 * 1024 * 1024)
 
 
@@ -94,6 +98,11 @@
     xp[:, 0:HALO, :] = left_ref[...].astype(F32)
     xp[:, HALO + width : 2 * HALO + width, :] = right_ref[...].astype(F32)
     small[...] = jnp.zeros_like(small)
+
+    def put(p, l, value):
+        at = BLOCKS * (p % 4) + l
+        small[p // 4, at : at + 1, :] = value
+
     for c in copies[0:2]:
         c.wait()
     xp[HALO : HALO + height, HALO : HALO + width, :] = x_ref[...].astype(F32)
@@ -127,7 +136,7 @@
         both[pixels : 2 * pixels, sl] = (pre * cdf).astype(BF16)
         total = jnp.sum(g_pre, axis=0, keepdims=True)
         for l in range(BLOCKS):
-            small[54 + f, l : l + 1, :] = total[:, LANES * l : LANES * (l + 1)]
+            put(54 + f, l, total[:, LANES * l : LANES * (l + 1)])
     branch = matmul(both[pixels : 2 * pixels, :], wred_ref[...], 1, 0) + row(bred_ref)
     block = x_ref[...].astype(F32).reshape(pixels, D) + row(ls_ref) * branch
     block_ref[...] = block.astype(BF16).reshape(height, width, D)
@@ -143,7 +152,7 @@
     for k, value in enumerate(sums):
         total = jnp.sum(value, axis=0, keepdims=True)
         for l in range(BLOCKS):
-            small[49 + k, l : l + 1, :] = total[:, LANES * l : LANES * (l + 1)]
+            put(49 + k, l, total[:, LANES * l : LANES * (l + 1)])
     for l in range(BLOCKS):
         ln = slice(LANES * l, LANES * (l + 1))
         g3 = gconv_ref[:, :, ln]
@@ -151,82 +160,128 @@
             s = xp[:, j : j + width, ln]
             for i in range(7):
                 part = jnp.sum(g3 * s[i : i + height], axis=0)
-                small[7 * i + j, l : l + 1, :] = jnp.sum(part, axis=0, keepdims=True)
-    value = small[:, 0:BLOCKS, :]
-    small[:, BLOCKS : 2 * BLOCKS, :] = value - value.astype(BF16).astype(F32)
-    packed = small[...].astype(BF16)
+                put(7 * i + j, l, jnp.sum(part, axis=0, keepdims=True))
+    value = small[:, 0:SHARE, :]
+    small[:, SHARE : 2 * SHARE, :] = value - value.astype(BF16).astype(F32)
     chan = lax.broadcasted_iota(jnp.int32, (D, D), 0)
     column = lax.broadcasted_iota(jnp.int32, (1, D), 1)
-    block = (column * 1366) >> 16
-    inside = column - 2 * DROWS * block
-    of_e = 2 * DROWS * block + jnp.where(inside < DROWS, inside, -4 * D)
-    of_r = 2 * DROWS * block + jnp.where(inside < DROWS, -4 * D, inside - DROWS)
+    half = (column >= D // 2).astype(jnp.int32)
+    rest = column - (D // 2) * half
+    block = (rest * 1366) >> 16
+    inside = rest - 2 * DROWS * block
+    of_e = inside < DROWS
+    base = 4 * DROWS * block + jnp.where(of_e, inside, inside - DROWS)
+    pixel = lax.broadcasted_iota(jnp.int32, (2 * pixels, 1), 0)
+    keep = jnp.where(pixel < pixels, 1, 0) == jnp.where(of_e, 1, 0)
+    stack = jnp.concatenate([normed, g_branch], axis=0)
+    lane = lax.broadcasted_iota(jnp.int32, (1, 1, LANES), 2)
     outputs = []
+
+    def flush(out, hbm, rows):
+        c = pltpu.make_async_copy(out.at[:, rows], hbm.at[:, rows], sems.at[11 + len(outputs)])
+        c.start()
+        outputs.append(c)
+
     for which, (out, hbm) in enumerate(((send_ref, send_hbm), (mine_ref, mine_hbm))):
-        shift = DROWS * core_ref[0] if which == 1 else DROWS * (1 - core_ref[0])
-        out[:, BIG:ROWS, :] = packed
-        pick_e = (chan == of_e + shift).astype(F32).astype(BF16)
-        pick_r = (chan == of_r + shift).astype(F32).astype(BF16)
-        right = jnp.concatenate(
-            [matmul(normed, pick_e, 1, 0).astype(BF16), matmul(g_branch, pick_r, 1, 0).astype(BF16)],
-            axis=0,
-        )
-        for f in range(4):
-            g = matmul(both[:, D * f : D * (f + 1)], right, 0, 0).reshape(D // FROWS, FROWS, D)
-            at = slice(16 * f, 16 * (f + 1))
+        core = core_ref[0] if which == 1 else 1 - core_ref[0]
+        out[:, BIG:ROWS, :] = small[pl.ds(PIECES * core, PIECES)].astype(BF16)
+        flush(out, hbm, slice(BIG, ROWS))
+        right = []
+        for order in range(2):
+            turn = half if order == 0 else 1 - half
+            pick = (chan == base + 2 * DROWS * turn + DROWS * core).astype(F32).astype(BF16)
+            right.append(jnp.where(keep, matmul(stack, pick, 1, 0), 0.0).astype(BF16))
+        for low in range(2):
+            g = []
+            for order in range(2):
+                f = low + 2 * order
+                part = matmul(both[:, D * f : D * (f + 1)], right[order], 0, 0)
+                g.append(part.reshape(2, 4, 2, FROWS, D))
+            for zl in range(2):
+                for xl in range(2):
+                    for yl in range(2):
+                        one, two = g[yl][zl, :, xl], g[1 - yl][zl, :, xl]
+                        pieces = (
+                            one[:, :, 0:LANES],
+                            jnp.where(
+                                lane < LANES // 2,
+                                one[:, :, LANES : 2 * LANES],
+                                two[:, :, LANES : 2 * LANES],
+                            ),
+                            two[:, :, 2 * LANES : D],
+                        )
+                        for l, piece in enumerate(pieces):
+                            at = 8 * FROWS * l + 4 * FROWS * low
+                            out[4 * zl + 2 * xl + yl, at : at + 4 * FROWS, :] = piece.reshape(
+                                4 * FROWS, LANES
+                            ).astype(BF16)
             for l in range(BLOCKS):
-                out[at, FROWS * l : FROWS * (l + 1), :] = g[
-                    :, :, LANES * l : LANES * (l + 1)
-                ].astype(BF16)
-            c = pltpu.make_async_copy(out.at[at], hbm.at[at], sems.at[11 + 4 * which + f])
-            c.start()
-            outputs.append(c)
+                at = 8 * FROWS * l + 4 * FROWS * low
+                flush(out, hbm, slice(at, at + 4 * FROWS))
     for c in outputs:
         c.wait()
 
 
-def join_kernel(mine_ref, got_ref, out_ref):
+def join_kernel(mine_ref, got_ref, top_hbm, bot_hbm, out_ref):
     big = mine_ref[:, 0:BIG, :].astype(F32) + got_ref[:, 0:BIG, :].astype(F32)
     out_ref[:, 0:BIG, :] = big.astype(BF16)
     both = mine_ref[:, BIG:ROWS, :].astype(F32) + got_ref[:, BIG:ROWS, :].astype(F32)
-    value = both[:, 0:BLOCKS] + both[:, BLOCKS : 2 * BLOCKS]
+    value = both[:, 0:SHARE] + both[:, SHARE : 2 * SHARE]
     low = value - value.astype(BF16).astype(F32)
-    rest = jnp.zeros((value.shape[0], 8 - 2 * BLOCKS, LANES), F32)
-    out_ref[:, BIG:ROWS, :] = jnp.concatenate([value, low, rest], axis=1).astype(BF16)
-
-
-def tile_sum_kernel(got_ref, after_hbm, out_ref):
-    total = jnp.sum(got_ref[...].astype(F32), axis=0)
-    wide = jnp.concatenate(
-        [total[FROWS * l : FROWS * (l + 1), :] for l in range(BLOCKS)], axis=1
-    )
-    small = total[BIG : BIG + BLOCKS, :] + total[BIG + BLOCKS : BIG + 2 * BLOCKS, :]
-    for y in range(out_ref.shape[0]):
-        out_ref[y, 0:FROWS, 0 : 2 * DROWS] = wide[:, 2 * DROWS * y : 2 * DROWS * (y + 1)]
-        out_ref[y, 0:FROWS, 2 * DROWS :] = jnp.zeros((FROWS, LANES - 2 * DROWS), F32)
-        out_ref[y, FROWS:, :] = jnp.zeros((8, LANES), F32)
-        out_ref[y, FROWS : FROWS + BLOCKS, :] = small
-
-
-def region_sum_kernel(scale, got_ref, ge_ref, gr_ref, small_ref):
-    total = jnp.sum(got_ref[...], axis=0) * scale
+    out_ref[:, BIG:ROWS, :] = jnp.concatenate([value, low], axis=1).astype(BF16)
+
+
+def block_sum_kernel(yl_ref, got_ref, left_hbm, right_hbm, out_ref, total):
+    total[...] = jnp.sum(got_ref[...].astype(F32), axis=0)
+    small = total[BIG : BIG + SHARE, :] + total[BIG + SHARE : ROWS, :]
+    side = LANES // 2
+    folded = jnp.concatenate([small[:, 0:side], small[:, side:]], axis=0)
+    gap = jnp.zeros((FROWS, side - 2 * DROWS), F32)
+    tail = jnp.concatenate([gap, folded], axis=1)
+    for low in range(2):
+        for xh in range(4):
+            at = 4 * FROWS * low + FROWS * xh
+            wide = jnp.concatenate(
+                [
+                    total[8 * FROWS * l + at : 8 * FROWS * l + at + FROWS, :]
+                    for l in range(BLOCKS)
+                ],
+                axis=1,
+            )
+            for half in range(2):
+                turn = yl_ref[0] if half == 0 else 1 - yl_ref[0]
+                zh = low + 2 * turn
+                for yh in range(4):
+                    start = D // 2 * half + 2 * DROWS * yh
+                    piece = jnp.concatenate([wide[:, start : start + 2 * DROWS], tail], axis=1)
+                    out_ref[16 * zh + 4 * xh + yh] = piece.astype(BF16)
+
+
+def far_sum_kernel(scale, got_ref, ge_ref, gr_ref, small_ref):
+    total = jnp.sum(got_ref[...].astype(F32), axis=0) * scale
     turned = jnp.transpose(total, (1, 0))
     ge_ref[...] = turned[0:DROWS, 0:FROWS]
     gr_ref[...] = turned[DROWS : 2 * DROWS, 0:FROWS]
-    small_ref[...] = jnp.broadcast_to(total[FROWS : FROWS + BLOCKS, :], small_ref.shape)
+    side = LANES // 2
+    small = jnp.concatenate([total[0:SHARE, side:], total[SHARE:FROWS, side:]], axis=1)
+    small_ref[...] = jnp.broadcast_to(small, small_ref.shape)
 
 
 def spread_kernel(got_ref, gker_ref, vec_ref, gbexp_ref):
+    def take(p, l):
+        share, at = p // 4, BLOCKS * (p % 4) + l
+        return got_ref[2 * (share % PIECES) + share // PIECES, at : at + 1, :]
+
     for l in range(BLOCKS):
         ln = slice(LANES * l, LANES * (l + 1))
         for i in range(7):
             for j in range(7):
-                gker_ref[i, j : j + 1, ln] = got_ref[7 * i + j, l : l + 1, :]
+                gker_ref[i, j : j + 1, ln] = take(7 * i + j, l)
         for k in range(5):
-            vec_ref[k : k + 1, ln] = got_ref[49 + k, l : l + 1, :]
+            vec_ref[k : k + 1, ln] = take(49 + k, l)
         for f in range(4):
             at = D * f + LANES * l
-            gbexp_ref[at : at + LANES] = got_ref[54 + f, l, :]
+            gbexp_ref[at : at + LANES] = take(54 + f, l).reshape(LANES)
 
 
 def input_grad_kernel(g_ref, top_ref, bot_ref, left_ref, right_ref, cot_ref, dwk_ref, out_ref, gp):
@@ -260,9 +315,9 @@
     width = cells.shape[1]
     head = jnp.concatenate([a[:, 0:HALO] for a in (top, cells, bot)], axis=0)
     tail = jnp.concatenate([a[:, width - HALO :] for a in (top, cells, bot)], axis=0)
-    count = lax.axis_size("cols")
-    left = lax.ppermute(tail, "cols", [(i, i + 1) for i in range(count - 1)])
-    right = lax.ppermute(head, "cols", [(i + 1, i) for i in range(count - 1)])
+    count = lax.axis_size(WIDE)
+    left = lax.ppermute(tail, WIDE, [(i, i + 1) for i in range(count - 1)])
+    right = lax.ppermute(head, WIDE, [(i + 1, i) for i in range(count - 1)])
     return left, right
 
 
@@ -282,9 +337,9 @@
 ):
     x, cot = feature_map[0], cotangent[0]
     height, width = x.shape[0], x.shape[1]
-    regions = lax.axis_size("y")
     core = lax.axis_index("core").astype(jnp.int32)
-    top, bot = shifted(x, "rows", 0)
+    yl = lax.axis_index("yl").astype(jnp.int32)
+    top, bot = shifted(x, TALL, 0)
     left, right = column_halo(x, top, bot)
 
     whole = lambda n: [pl.BlockSpec(memory_space=pltpu.VMEM)] * n
@@ -315,10 +370,10 @@
             pltpu.VMEM((height + 2 * HALO, width + 8, D), F32),
             pltpu.VMEM((height * width, D), F32),
             pltpu.VMEM((2 * height * width, FF), BF16),
-            pltpu.VMEM((PIECES, 8, LANES), F32),
+            pltpu.VMEM((2 * PIECES, 2 * SHARE, LANES), F32),
             pltpu.VMEM((PIECES, ROWS, LANES), BF16),
             pltpu.VMEM((PIECES, ROWS, LANES), BF16),
-            pltpu.SemaphoreType.DMA((19,)),
+            pltpu.SemaphoreType.DMA((25,)),
         ],
         compiler_params=LIMIT,
         name="front",
@@ -342,21 +397,32 @@
     )
 
     got = lax.ppermute(send, "core", [(0, 1), (1, 0)])
-    gtop, gbot = shifted(gconv, "rows", 0)
+    gtop, gbot = shifted(gconv, TALL, 0)
     gleft, gright = column_halo(gconv, gtop, gbot)
 
-    step = 16
+    step = 2
     spec = pl.BlockSpec((step, ROWS, LANES), lambda i: (i, 0, 0))
+    free = lambda n: [pl.BlockSpec(memory_space=pl.ANY)] * n
+    smem = [pl.BlockSpec(memory_space=pltpu.SMEM)]
     joined = pl.pallas_call(
         join_kernel,
         out_shape=jax.ShapeDtypeStruct((PIECES, ROWS, LANES), BF16),
         grid=(PIECES // step,),
-        in_specs=[spec, spec],
+        in_specs=[spec, spec] + free(2),
         out_specs=spec,
         compiler_params=LIMIT,
         name="join",
-    )(mine, got)
-    tiles = lax.all_to_all(joined, ("rows", "cols"), 0, 0, tiled=True)
+    )(mine, got, gtop, gbot)
+    near = lax.all_to_all(joined, ("zl", "xl", "yl"), 0, 0, tiled=True)
+    by_block = pl.pallas_call(
+        block_sum_kernel,
+        out_shape=jax.ShapeDtypeStruct((FAR, FROWS, LANES), BF16),
+        in_specs=smem + whole(1) + free(2),
+        out_specs=whole(1)[0],
+        scratch_shapes=[pltpu.VMEM((ROWS, LANES), F32)],
+        compiler_params=LIMIT,
+        name="block_sum",
+    )(yl.reshape(1), near, gleft, gright)
     grad_in = pl.pallas_call(
         input_grad_kernel,
         out_shape=jax.ShapeDtypeStruct((height, width, D), BF16),
@@ -366,28 +432,20 @@
         compiler_params=LIMIT,
         name="input_grad",
     )(gconv, gtop, gbot, gleft, gright, cot, dw_kernel)
-    by_region = pl.pallas_call(
-        tile_sum_kernel,
-        out_shape=jax.ShapeDtypeStruct((regions, FROWS + 8, LANES), F32),
-        in_specs=whole(1) + hbm(1),
-        out_specs=whole(1)[0],
-        compiler_params=LIMIT,
-        name="tile_sum",
-    )(tiles, away(grad_in))
-    by_region = lax.all_to_all(by_region, "y", 0, 0, tiled=True)
+    by_block = lax.all_to_all(by_block, ("zh", "xh", "yh"), 0, 0, tiled=True)
     grad_expand, grad_reduce_t, small = pl.pallas_call(
-        functools.partial(region_sum_kernel, scale),
+        functools.partial(far_sum_kernel, scale),
         out_shape=(
             jax.ShapeDtypeStruct((DROWS, FROWS), F32),
             jax.ShapeDtypeStruct((DROWS, FROWS), F32),
-            jax.ShapeDtypeStruct((PIECES, BLOCKS, LANES), F32),
+            jax.ShapeDtypeStruct((2 * PIECES, SHARE, LANES), F32),
         ),
         in_specs=whole(1),
         out_specs=tuple(whole(3)),
         compiler_params=LIMIT,
-        name="region_sum",
-    )(by_region)
-    small = lax.all_to_all(small, ("rows", "cols"), 0, 0, tiled=True)
+        name="far_sum",
+    )(by_block)
+    small = lax.all_to_all(small, ("zl", "xl", "yl", "core"), 0, 0, tiled=True)
     gker, vectors, gbexp = pl.pallas_call(
         spread_kernel,
         out_shape=(
@@ -413,12 +471,10 @@
 
 def solution(mesh):
     shape = dict(mesh.shape)
-    fine = Mesh(
-        mesh.devices.reshape(shape["rows"], shape["cols"], shape["rep"] // 2, 2),
-        ("rows", "cols", "y", "core"),
-    )
-    tile = P(("y", "core"), "rows", "cols", None)
-    grad = P(("y", "core"), ("rows", "cols"))
+    sizes = (shape["rows"] // 2, 2, shape["cols"] // 2, 2, shape["rep"] // 4, 2, 2)
+    fine = Mesh(mesh.devices.reshape(sizes), TALL + WIDE + ("yh", "yl", "core"))
+    tile = P(("yh", "yl", "core"), TALL, WIDE, None)
+    grad = P(("yh", "yl", "core"), TALL + WIDE)
     pixels = 16 * 64 * 128
     scale = float(pixels) ** -0.5
     return jax.shard_map(

time: 143 us -> 126 us (0.88)
  the two profiles are of different devices: /device:TPU:2 before, /device:TPU:1 now
where the time goes in v3:
time: 126 us
  starting transfers between devices  47.9 us (38%)
  blocking collectives  37.2 us (30%)
  waiting for transfers between devices  23.6 us (19%)
  Pallas kernels  14.2 us (11%)
  local copies, waits for them, and re-layouts  1.73 us (1%)
    all_to_all x1, blocking collectives, per_device(): by_block = lax.all_to_all(by_block, ('zh', 'xh', 'yh'), 0, 0, tiled=True)  37.2 us
    ppermute x1, starting transfers between devices, per_device(): got = lax.ppermute(send, 'core', [(0, 1), (1, 0)])  12.4 us
    ppermute x2, waiting for transfers between devices, column_halo(): right = lax.ppermute(head, WIDE, [(i + 1, i) for i in range(count - 1)])  11 us
    all_to_all x1, starting transfers between devices, per_device(): small = lax.all_to_all(small, ('zl', 'xl', 'yl', 'core'), 0, 0, tiled=True)  9.05 us
    pallas_call x1, Pallas kernels, per_device(): pl.pallas_call(front_kernel, out_shape=(jax.ShapeDtypeStruct((height, wid...  8.47 us
    ppermute x2, starting transfers between devices, column_halo(): left = lax.ppermute(tail, WIDE, [(i, i + 1) for i in range(count - 1)])  7.99 us
    ppermute x2, waiting for transfers between devices, shifted(): after = lax.ppermute(head, axis, [(i + 1, i) for i in range(count - 1)])  7.87 us
    ppermute x2, starting transfers between devices, shifted(): before = lax.ppermute(tail, axis, [(i, i + 1) for i in range(count - 1)])  7.06 us
  transfers between devices with their start and end apart: 11, of which 6 were waited for; matrix products, arithmetic and copies ran while one was open for 1% of the time, Pallas kernels for 2%

profile of v3, /device:TPU:1, one launch (start us, length us, event | category | flops | bytes accessed | tf_op | source)
XLA Modules:
  0.0 125.5 jit_solution(16801455049778615833)
XLA Ops:
  0.6 0.8 slice_bitcast_fusion
  1.4 5.7 %collective-permute-start = (bf16[3,16,384]{2,1,0:T(8,128)(2,1)S(1)}, bf16[3,16,384]{2,1,0:T(8,128)(2,1)S(1)}, u32[]{:S(2)}, u32[]{:S(2)}) collective-permute-start(bf16[3,16,384]{2,1,0:T(8,128)(2,1)S(1)} %get-tuple-element.34), channel_id=1, source_target_pairs={{0,128},{128,256},{256,384},{384,512},{512,640},{640,768},{768,896... | collective-permute-start | bytes 110600 | tf_op jit(solution)/shard_map/ppermute | solution.py:309
  7.2 1.3 %collective-permute-start.1 = (bf16[3,16,384]{2,1,0:T(8,128)(2,1)S(1)}, bf16[3,16,384]{2,1,0:T(8,128)(2,1)S(1)}, u32[]{:S(2)}, u32[]{:S(2)}) collective-permute-start(bf16[3,16,384]{2,1,0:T(8,128)(2,1)S(1)} %get-tuple-element.33), channel_id=1, source_target_pairs={{128,0},{256,128},{384,256},{512,384},{640,512},{768,640},{896,768... | collective-permute-start | bytes 110600 | tf_op jit(solution)/shard_map/ppermute | solution.py:310
  8.5 0.8 fusion.2
  9.3 0.0 collective-permute-done.top_ref
  9.3 4.1 %collective-permute-done.1.bot_ref = bf16[3,16,384]{2,1,0:T(8,128)(2,1)S(1)} collective-permute-done((bf16[3,16,384]{2,1,0:T(8,128)(2,1)S(1)}, bf16[3,16,384]{2,1,0:T(8,128)(2,1)S(1)}, u32[]{:S(2)}, u32[]{:S(2)}) %collective-permute-start.1) | collective-permute-done | bytes 36896 | tf_op jit(solution)/shard_map/ppermute | solution.py:310
  13.5 1.3 %collective-permute-start.3 = (bf16[14,3,384]{2,1,0:T(4,128)(2,1)S(1)}, bf16[14,3,384]{2,1,0:T(4,128)(2,1)S(1)}, u32[]{:S(2)}, u32[]{:S(2)}) collective-permute-start(bf16[14,3,384]{2,1,0:T(4,128)(2,1)S(1)} %pad_maximum_fusion.3), channel_id=1, source_target_pairs={{16,0},{32,16},{48,32},{64,48},{80,64},{96,80},{112,96},{17,1},{33... | collective-permute-start | bytes 96776 | tf_op jit(solution)/shard_map/ppermute | solution.py:320
  14.8 4.0 %collective-permute-start.2 = (bf16[14,3,384]{2,1,0:T(4,128)(2,1)S(1)}, bf16[14,3,384]{2,1,0:T(4,128)(2,1)S(1)}, u32[]{:S(2)}, u32[]{:S(2)}) collective-permute-start(bf16[14,3,384]{2,1,0:T(4,128)(2,1)S(1)} %pad_maximum_fusion.2), channel_id=1, source_target_pairs={{0,16},{16,32},{32,48},{48,64},{64,80},{80,96},{96,112},{1,17},{17... | collective-permute-start | bytes 96776 | tf_op jit(solution)/shard_map/ppermute | solution.py:319
  18.8 0.0 collective-permute-done.3.right_ref
  18.8 1.1 collective-permute-done.2.left_ref
  19.9 8.5 %front.1 = (bf16[8,16,384]{2,1,0:T(8,128)(2,1)}, f32[8,16,384]{2,1,0:T(8,128)S(1)}, bf16[8,600,128]{2,1,0:T(8,128)(2,1)S(1)}, bf16[8,600,128]{2,1,0:T(8,128)(2,1)S(1)}) custom-call(s32[1]{0:T(128)} %bitcast.core_ref, bf16[8,16,384]{2,1,0:T(8,128)(2,1)} %bitcast.13, bf16[3,16,384]{2,1,0:T(8,128)(2,1)S(1)} %collective-permute-done.top_ref, ...), custom_call_target="tpu_custom_call" | custom-call | tf_op jit(solution)/shard_map/front/pallas_call | solution.py:348
  28.4 12.4 %collective-permute-start.8 = (bf16[8,600,128]{2,1,0:T(8,128)(2,1)S(1)}, bf16[8,600,128]{2,1,0:T(8,128)(2,1)S(1)}, u32[]{:S(2)}, u32[]{:S(2)}) collective-permute-start(bf16[8,600,128]{2,1,0:T(8,128)(2,1)S(1)} %get-tuple-element.20), channel_id=1, source_target_pairs={{0,1},{1,0},{2,3},{3,2},{4,5},{5,4},{6,7},{7,6},{8,9},{9,8},{10,11... | collective-permute-start | bytes 3686408 | tf_op jit(solution)/shard_map/ppermute | solution.py:399
  40.8 1.3 %collective-permute-start.4 = (f32[3,16,384]{2,1,0:T(8,128)S(1)}, f32[3,16,384]{2,1,0:T(8,128)S(1)}, u32[]{:S(2)}, u32[]{:S(2)}) collective-permute-start(f32[3,16,384]{2,1,0:T(8,128)S(1)} %get-tuple-element.30), channel_id=1, source_target_pairs={{0,128},{128,256},{256,384},{384,512},{512,640},{640,768},{768,896... | collective-permute-start | bytes 221192 | tf_op jit(solution)/shard_map/ppermute | solution.py:309
  42.1 1.3 %collective-permute-start.5 = (f32[3,16,384]{2,1,0:T(8,128)S(1)}, f32[3,16,384]{2,1,0:T(8,128)S(1)}, u32[]{:S(2)}, u32[]{:S(2)}) collective-permute-start(f32[3,16,384]{2,1,0:T(8,128)S(1)} %get-tuple-element.29), channel_id=1, source_target_pairs={{128,0},{256,128},{384,256},{512,384},{640,512},{768,640},{896,768... | collective-permute-start | bytes 221192 | tf_op jit(solution)/shard_map/ppermute | solution.py:310
  43.4 0.4 collective-permute-done.4.top_ref.top_hbm
  43.8 3.8 %collective-permute-done.5.bot_ref.bot_hbm = f32[3,16,384]{2,1,0:T(8,128)S(1)} collective-permute-done((f32[3,16,384]{2,1,0:T(8,128)S(1)}, f32[3,16,384]{2,1,0:T(8,128)S(1)}, u32[]{:S(2)}, u32[]{:S(2)}) %collective-permute-start.5) | collective-permute-done | bytes 73760 | tf_op jit(solution)/shard_map/ppermute | solution.py:310
  47.6 0.0 collective-permute-done.8.got_ref
  47.6 1.8 %join.1 = bf16[8,600,128]{2,1,0:T(8,128)(2,1)} custom-call(bf16[8,600,128]{2,1,0:T(8,128)(2,1)S(1)} %get-tuple-element.19.mine_ref, bf16[8,600,128]{2,1,0:T(8,128)(2,1)S(1)} %collective-permute-done.8.got_ref, f32[3,16,384]{2,1,0:T(8,128)S(1)} %collective-permute-done.4.top_ref.top_hbm, f32[3,16,384]{2,1,0:T(8,128)S(1)} %collective-permute-done.5.bot_ref.bot_hbm), custom_call_target="tpu_custom_call" | custom-call | tf_op jit(solution)/shard_map/join/pallas_call | solution.py:407
  49.3 6.3 %all-to-all-start = ((bf16[8,600,128]{2,1,0:T(8,128)(2,1)}), bf16[8,600,128]{2,1,0:T(8,128)(2,1)S(1)}, u32[]{:S(2)}, u32[]{:S(2)}) async-start(bf16[8,600,128]{2,1,0:T(8,128)(2,1)} %join.1), calls=%async_computation | async-start | bytes 2457600 | tf_op jit(solution)/shard_map/all_to_all | solution.py:416
  55.7 1.3 %collective-permute-start.7 = (f32[14,3,384]{2,1,0:T(4,128)S(1)}, f32[14,3,384]{2,1,0:T(4,128)S(1)}, u32[]{:S(2)}, u32[]{:S(2)}) collective-permute-start(f32[14,3,384]{2,1,0:T(4,128)S(1)} %pad_maximum_fusion.1), channel_id=1, source_target_pairs={{16,0},{32,16},{48,32},{64,48},{80,64},{96,80},{112,96},{17,1},{33... | collective-permute-start | bytes 193544 | tf_op jit(solution)/shard_map/ppermute | solution.py:320
  57.0 4.0 %collective-permute-start.6 = (f32[14,3,384]{2,1,0:T(4,128)S(1)}, f32[14,3,384]{2,1,0:T(4,128)S(1)}, u32[]{:S(2)}, u32[]{:S(2)}) collective-permute-start(f32[14,3,384]{2,1,0:T(4,128)S(1)} %pad_maximum_fusion), channel_id=1, source_target_pairs={{0,16},{16,32},{32,48},{48,64},{64,80},{80,96},{96,112},{1,17},{17... | collective-permute-start | bytes 193544 | tf_op jit(solution)/shard_map/ppermute | solution.py:319
  61.0 11.0 %collective-permute-done.7.right_ref.right_hbm = f32[14,3,384]{2,1,0:T(4,128)S(1)} collective-permute-done((f32[14,3,384]{2,1,0:T(4,128)S(1)}, f32[14,3,384]{2,1,0:T(4,128)S(1)}, u32[]{:S(2)}, u32[]{:S(2)}) %collective-permute-start.7) | collective-permute-done | bytes 64544 | tf_op jit(solution)/shard_map/ppermute | solution.py:320
  72.0 0.0 collective-permute-done.6.left_ref.left_hbm
  72.0 0.0 all-to-all-done.got_ref
  72.0 0.0 copy-start
  72.0 0.0 copy-start.1
  72.1 0.3 block_sum.1
  72.4 37.2 %all_to_all.15.got_ref = bf16[64,24,128]{2,1,0:T(8,128)(2,1)S(1)} all-to-all(bf16[64,24,128]{2,1,0:T(8,128)(2,1)S(1)} %block_sum.1), channel_id=1, replica_groups=mesh['zh'=4,'zl'=2,'xh'=4,'xl'=2,'yh'=4,'yl'=2,'core'=2] {'zh','xh','yh'}, dimensions={0} | all-to-all | bytes 786432 | tf_op jit(solution)/shard_map/all_to_all | solution.py:435
  109.6 0.8 far_sum.1
  110.4 9.1 %all-to-all-start.2 = ((f32[16,12,128]{2,1,0:T(8,128)}), f32[16,12,128]{2,1,0:T(8,128)S(1)}, u32[]{:S(2)}, u32[]{:S(2)}) async-start(f32[16,12,128]{2,1,0:T(8,128)} %get-tuple-element.23), calls=%async_computation.2 | async-start | bytes 262144 | tf_op jit(solution)/shard_map/all_to_all | solution.py:448
  119.4 0.0 copy-done
  119.5 0.0 copy-done.1
  119.5 2.1 %input_grad.1 = bf16[8,16,384]{2,1,0:T(8,128)(2,1)} custom-call(f32[8,16,384]{2,1,0:T(8,128)S(1)} %get-tuple-element.18.g_ref, f32[3,16,384]{2,1,0:T(8,128)S(1)} %collective-permute-done.4.top_ref.top_hbm, f32[3,16,384]{2,1,0:T(8,128)S(1)} %collective-permute-done.5.bot_ref.bot_hbm, f32[14,3,384]{2,1,0:T(4,128)S(1)} %collective-permute-done.6.left_ref.left_hbm, ...), custom_call_target="tpu_custom_call" | custom-call | tf_op jit(solution)/shard_map/input_grad/pallas_call | solution.py:426
  121.6 3.2 %all-to-all-done.2.got_ref = f32[16,12,128]{2,1,0:T(8,128)S(1)} async-done(((f32[16,12,128]{2,1,0:T(8,128)}), f32[16,12,128]{2,1,0:T(8,128)S(1)}, u32[]{:S(2)}, u32[]{:S(2)}) %all-to-all-start.2) | async-done | bytes 98336 | tf_op jit(solution)/shard_map/all_to_all | solution.py:448
  124.8 0.7 spread.1
  (10 shorter events, 0.2 us)
Async XLA Ops:
  1.4 7.9 %collective-permute-start = (bf16[3,16,384]{2,1,0:T(8,128)(2,1)S(1)}, bf16[3,16,384]{2,1,0:T(8,128)(2,1)S(1)}, u32[]{:S(2)}, u32[]{:S(2)}) collective-permute-start(bf16[3,16,384]{2,1,0:T(8,128)(2,1)S(1)} %get-tuple-element.34), channel_id=1, source_target_pairs={{0,128},{128,256},{256,384},{384,512},{512,640},{640,768},{768,896... | collective-permute-start | bytes 110600 | tf_op jit(solution)/shard_map/ppermute | solution.py:309
  7.2 6.3 %collective-permute-start.1 = (bf16[3,16,384]{2,1,0:T(8,128)(2,1)S(1)}, bf16[3,16,384]{2,1,0:T(8,128)(2,1)S(1)}, u32[]{:S(2)}, u32[]{:S(2)}) collective-permute-start(bf16[3,16,384]{2,1,0:T(8,128)(2,1)S(1)} %get-tuple-element.33), channel_id=1, source_target_pairs={{128,0},{256,128},{384,256},{512,384},{640,512},{768,640},{896,768... | collective-permute-start | bytes 110600 | tf_op jit(solution)/shard_map/ppermute | solution.py:310
  13.5 5.3 %collective-permute-start.3 = (bf16[14,3,384]{2,1,0:T(4,128)(2,1)S(1)}, bf16[14,3,384]{2,1,0:T(4,128)(2,1)S(1)}, u32[]{:S(2)}, u32[]{:S(2)}) collective-permute-start(bf16[14,3,384]{2,1,0:T(4,128)(2,1)S(1)} %pad_maximum_fusion.3), channel_id=1, source_target_pairs={{16,0},{32,16},{48,32},{64,48},{80,64},{96,80},{112,96},{17,1},{33... | collective-permute-start | bytes 96776 | tf_op jit(solution)/shard_map/ppermute | solution.py:320
  14.8 5.1 %collective-permute-start.2 = (bf16[14,3,384]{2,1,0:T(4,128)(2,1)S(1)}, bf16[14,3,384]{2,1,0:T(4,128)(2,1)S(1)}, u32[]{:S(2)}, u32[]{:S(2)}) collective-permute-start(bf16[14,3,384]{2,1,0:T(4,128)(2,1)S(1)} %pad_maximum_fusion.2), channel_id=1, source_target_pairs={{0,16},{16,32},{32,48},{48,64},{64,80},{80,96},{96,112},{1,17},{17... | collective-permute-start | bytes 96776 | tf_op jit(solution)/shard_map/ppermute | solution.py:319
  28.4 19.2 %collective-permute-start.8 = (bf16[8,600,128]{2,1,0:T(8,128)(2,1)S(1)}, bf16[8,600,128]{2,1,0:T(8,128)(2,1)S(1)}, u32[]{:S(2)}, u32[]{:S(2)}) collective-permute-start(bf16[8,600,128]{2,1,0:T(8,128)(2,1)S(1)} %get-tuple-element.20), channel_id=1, source_target_pairs={{0,1},{1,0},{2,3},{3,2},{4,5},{5,4},{6,7},{7,6},{8,9},{9,8},{10,11... | collective-permute-start | bytes 3686408 | tf_op jit(solution)/shard_map/ppermute | solution.py:399
  40.8 3.0 %collective-permute-start.4 = (f32[3,16,384]{2,1,0:T(8,128)S(1)}, f32[3,16,384]{2,1,0:T(8,128)S(1)}, u32[]{:S(2)}, u32[]{:S(2)}) collective-permute-start(f32[3,16,384]{2,1,0:T(8,128)S(1)} %get-tuple-element.30), channel_id=1, source_target_pairs={{0,128},{128,256},{256,384},{384,512},{512,640},{640,768},{768,896... | collective-permute-start | bytes 221192 | tf_op jit(solution)/shard_map/ppermute | solution.py:309
  42.1 5.5 %collective-permute-start.5 = (f32[3,16,384]{2,1,0:T(8,128)S(1)}, f32[3,16,384]{2,1,0:T(8,128)S(1)}, u32[]{:S(2)}, u32[]{:S(2)}) collective-permute-start(f32[3,16,384]{2,1,0:T(8,128)S(1)} %get-tuple-element.29), channel_id=1, source_target_pairs={{128,0},{256,128},{384,256},{512,384},{640,512},{768,640},{896,768... | collective-permute-start | bytes 221192 | tf_op jit(solution)/shard_map/ppermute | solution.py:310
  49.3 22.7 %all-to-all-start = ((bf16[8,600,128]{2,1,0:T(8,128)(2,1)}), bf16[8,600,128]{2,1,0:T(8,128)(2,1)S(1)}, u32[]{:S(2)}, u32[]{:S(2)}) async-start(bf16[8,600,128]{2,1,0:T(8,128)(2,1)} %join.1), calls=%async_computation | async-start | bytes 2457600 | tf_op jit(solution)/shard_map/all_to_all | solution.py:416
  55.7 16.3 %collective-permute-start.7 = (f32[14,3,384]{2,1,0:T(4,128)S(1)}, f32[14,3,384]{2,1,0:T(4,128)S(1)}, u32[]{:S(2)}, u32[]{:S(2)}) collective-permute-start(f32[14,3,384]{2,1,0:T(4,128)S(1)} %pad_maximum_fusion.1), channel_id=1, source_target_pairs={{16,0},{32,16},{48,32},{64,48},{80,64},{96,80},{112,96},{17,1},{33... | collective-permute-start | bytes 193544 | tf_op jit(solution)/shard_map/ppermute | solution.py:320
  57.0 15.0 %collective-permute-start.6 = (f32[14,3,384]{2,1,0:T(4,128)S(1)}, f32[14,3,384]{2,1,0:T(4,128)S(1)}, u32[]{:S(2)}, u32[]{:S(2)}) collective-permute-start(f32[14,3,384]{2,1,0:T(4,128)S(1)} %pad_maximum_fusion), channel_id=1, source_target_pairs={{0,16},{16,32},{32,48},{48,64},{64,80},{80,96},{96,112},{1,17},{17... | collective-permute-start | bytes 193544 | tf_op jit(solution)/shard_map/ppermute | solution.py:319
  72.0 47.4 %copy-start = (bf16[1,8,16,384]{3,2,1,0:T(8,128)(2,1)S(1)}, bf16[1,8,16,384]{3,2,1,0:T(8,128)(2,1)}, u32[]{:S(2)}) copy-start(bf16[1,8,16,384]{3,2,1,0:T(8,128)(2,1)} %param.21) | copy-start | bytes 294916
  72.0 47.4 %copy-start.1 = (f32[7,7,384]{2,1,0:T(8,128)S(1)}, f32[7,7,384]{2,1,0:T(8,128)}, u32[]{:S(2)}) copy-start(f32[7,7,384]{2,1,0:T(8,128)} %dwk_ref.1) | copy-start | bytes 225796
  110.4 14.4 %all-to-all-start.2 = ((f32[16,12,128]{2,1,0:T(8,128)}), f32[16,12,128]{2,1,0:T(8,128)S(1)}, u32[]{:S(2)}, u32[]{:S(2)}) async-start(f32[16,12,128]{2,1,0:T(8,128)} %get-tuple-element.23), calls=%async_computation.2 | async-start | bytes 262144 | tf_op jit(solution)/shard_map/all_to_all | solution.py:448

commit v4 on v3

--- a/solution.py
+++ b/solution.py
@@ -21,12 +21,12 @@
 FROWS = 24
 DROWS = 24
 PIECES = 8
-FAR = 64
 BIG = BLOCKS * 8 * FROWS
 SHARE = 12
 ROWS = BIG + 2 * SHARE
-TALL = ("zh", "zl")
-WIDE = ("xh", "xl")
+TALL = ("zh", "zm", "zl")
+WIDE = ("xh", "xm", "xl")
+DEEP = ("yh", "ym", "yl", "core")
 LIMIT = pltpu.CompilerParams(vmem_limit_bytes=50 * 1024 * 1024)
 
 
@@ -231,34 +231,60 @@
     out_ref[:, BIG:ROWS, :] = jnp.concatenate([value, low], axis=1).astype(BF16)
 
 
-def block_sum_kernel(yl_ref, got_ref, left_hbm, right_hbm, out_ref, total):
+def block_sum_kernel(got_ref, left_hbm, right_hbm, out_ref, total):
     total[...] = jnp.sum(got_ref[...].astype(F32), axis=0)
     small = total[BIG : BIG + SHARE, :] + total[BIG + SHARE : ROWS, :]
+    high = small.astype(BF16).astype(F32)
+    both = jnp.concatenate([high, small - high], axis=0)
+    width = LANES - 4 * DROWS
+    for zm in range(2):
+        for xh in range(2):
+            for xm in range(2):
+                at = 4 * FROWS * zm + FROWS * (2 * xh + xm)
+                wide = jnp.concatenate(
+                    [
+                        total[8 * FROWS * l + at : 8 * FROWS * l + at + FROWS, :]
+                        for l in range(BLOCKS)
+                    ],
+                    axis=1,
+                )
+                for half in range(2):
+                    group = 2 * half + xh
+                    tail = both[:, width * group : width * (group + 1)]
+                    for ym in range(2):
+                        start = D // 2 * half + 2 * DROWS * ym
+                        piece = jnp.concatenate(
+                            [
+                                wide[:, start : start + 2 * DROWS],
+                                wide[:, start + 4 * DROWS : start + 6 * DROWS],
+                                tail,
+                            ],
+                            axis=1,
+                        )
+                        rows = slice(FROWS * group, FROWS * (group + 1))
+                        out_ref[4 * zm + 2 * xm + ym, rows, :] = piece.astype(BF16)
+
+
+def middle_sum_kernel(yl_ref, got_ref, out_ref):
+    total = jnp.sum(got_ref[...].astype(F32), axis=0)
+    both = jnp.concatenate(
+        [total[FROWS * k : FROWS * (k + 1), 4 * DROWS :] for k in range(4)], axis=1
+    )
+    small = both[0:SHARE] + both[SHARE : 2 * SHARE]
     side = LANES // 2
     folded = jnp.concatenate([small[:, 0:side], small[:, side:]], axis=0)
     gap = jnp.zeros((FROWS, side - 2 * DROWS), F32)
-    tail = jnp.concatenate([gap, folded], axis=1)
-    for low in range(2):
-        for xh in range(4):
-            at = 4 * FROWS * low + FROWS * xh
-            wide = jnp.concatenate(
-                [
-                    total[8 * FROWS * l + at : 8 * FROWS * l + at + FROWS, :]
-                    for l in range(BLOCKS)
-                ],
-                axis=1,
-            )
-            for half in range(2):
-                turn = yl_ref[0] if half == 0 else 1 - yl_ref[0]
-                zh = low + 2 * turn
-                for yh in range(4):
-                    start = D // 2 * half + 2 * DROWS * yh
-                    piece = jnp.concatenate([wide[:, start : start + 2 * DROWS], tail], axis=1)
-                    out_ref[16 * zh + 4 * xh + yh] = piece.astype(BF16)
+    for half in range(2):
+        zh = yl_ref[0] if half == 0 else 1 - yl_ref[0]
+        for xh in range(2):
+            rows = slice(FROWS * (2 * half + xh), FROWS * (2 * half + xh + 1))
+            for yh in range(2):
+                own = total[rows, 2 * DROWS * yh : 2 * DROWS * (yh + 1)]
+                out_ref[4 * zh + 2 * xh + yh] = jnp.concatenate([own, gap, folded], axis=1)
 
 
 def far_sum_kernel(scale, got_ref, ge_ref, gr_ref, small_ref):
-    total = jnp.sum(got_ref[...].astype(F32), axis=0) * scale
+    total = jnp.sum(got_ref[...], axis=0) * scale
     turned = jnp.transpose(total, (1, 0))
     ge_ref[...] = turned[0:DROWS, 0:FROWS]
     gr_ref[...] = turned[DROWS : 2 * DROWS, 0:FROWS]
@@ -416,13 +442,23 @@
     near = lax.all_to_all(joined, ("zl", "xl", "yl"), 0, 0, tiled=True)
     by_block = pl.pallas_call(
         block_sum_kernel,
-        out_shape=jax.ShapeDtypeStruct((FAR, FROWS, LANES), BF16),
-        in_specs=smem + whole(1) + free(2),
+        out_shape=jax.ShapeDtypeStruct((PIECES, 4 * FROWS, LANES), BF16),
+        in_specs=whole(1) + free(2),
         out_specs=whole(1)[0],
         scratch_shapes=[pltpu.VMEM((ROWS, LANES), F32)],
         compiler_params=LIMIT,
         name="block_sum",
-    )(yl.reshape(1), near, gleft, gright)
+    )(near, gleft, gright)
+    middle = lax.all_to_all(by_block, ("zm", "xm", "ym"), 0, 0, tiled=True)
+    by_middle = pl.pallas_call(
+        middle_sum_kernel,
+        out_shape=jax.ShapeDtypeStruct((PIECES, FROWS, LANES), F32),
+        in_specs=smem + whole(1),
+        out_specs=whole(1)[0],
+        compiler_params=LIMIT,
+        name="middle_sum",
+    )(yl.reshape(1), middle)
+    far = lax.all_to_all(by_middle, ("zh", "xh", "yh"), 0, 0, tiled=True)
     grad_in = pl.pallas_call(
         input_grad_kernel,
         out_shape=jax.ShapeDtypeStruct((height, width, D), BF16),
@@ -432,7 +468,6 @@
         compiler_params=LIMIT,
         name="input_grad",
     )(gconv, gtop, gbot, gleft, gright, cot, dw_kernel)
-    by_block = lax.all_to_all(by_block, ("zh", "xh", "yh"), 0, 0, tiled=True)
     grad_expand, grad_reduce_t, small = pl.pallas_call(
         functools.partial(far_sum_kernel, scale),
         out_shape=(
@@ -444,7 +479,7 @@
         out_specs=tuple(whole(3)),
         compiler_params=LIMIT,
         name="far_sum",
-    )(by_block)
+    )(far)
     small = lax.all_to_all(small, ("zl", "xl", "yl", "core"), 0, 0, tiled=True)
     gker, vectors, gbexp = pl.pallas_call(
         spread_kernel,
@@ -471,10 +506,10 @@
 
 def solution(mesh):
     shape = dict(mesh.shape)
-    sizes = (shape["rows"] // 2, 2, shape["cols"] // 2, 2, shape["rep"] // 4, 2, 2)
-    fine = Mesh(mesh.devices.reshape(sizes), TALL + WIDE + ("yh", "yl", "core"))
-    tile = P(("yh", "yl", "core"), TALL, WIDE, None)
-    grad = P(("yh", "yl", "core"), TALL + WIDE)
+    sizes = (shape["rows"] // 4, 2, 2, shape["cols"] // 4, 2, 2, shape["rep"] // 8, 2, 2, 2)
+    fine = Mesh(mesh.devices.reshape(sizes), TALL + WIDE + DEEP)
+    tile = P(DEEP, TALL, WIDE, None)
+    grad = P(DEEP, TALL + WIDE)
     pixels = 16 * 64 * 128
     scale = float(pixels) ** -0.5
     return jax.shard_map(

time: 126 us -> 137 us (1.087)
  starting transfers between devices: 47.9 us -> 57.9 us
  blocking collectives: 37.2 us -> 28.2 us
  waiting for transfers between devices: 23.6 us -> 32.6 us
    all_to_all x0 -> x1, waiting for transfers between devices: none -> 9.26 us  [per_device(): middle = lax.all_to_all(by_block, ('zm', 'xm', 'ym'), 0, 0, tiled=True)]
    all_to_all x1, blocking collectives: 37.2 us -> 28.2 us  [per_device(): far = lax.all_to_all(by_middle, ('zh', 'xh', 'yh'), 0, 0, tiled=True)]
    all_to_all x0 -> x1, starting transfers between devices: none -> 8.76 us  [per_device(): middle = lax.all_to_all(by_block, ('zm', 'xm', 'ym'), 0, 0, tiled=True)]
  transfers between devices with their start and end apart: 11 -> 12, of which waited for: 6 -> 7; matrix products, arithmetic and copies ran while one was open for 1% -> 1% of each run, Pallas kernels for 2% -> 2%
where the time goes in v4:
time: 137 us; the launch traced here: 136 us
  starting transfers between devices  57.9 us (42%)
  waiting for transfers between devices  32.6 us (24%)
  blocking collectives  28.2 us (21%)
  Pallas kernels  15 us (11%)
  local copies, waits for them, and re-layouts  1.73 us (1%)
    all_to_all x1, blocking collectives, per_device(): far = lax.all_to_all(by_middle, ('zh', 'xh', 'yh'), 0, 0, tiled=True)  28.2 us
    ppermute x1, starting transfers between devices, per_device(): got = lax.ppermute(send, 'core', [(0, 1), (1, 0)])  12.4 us
    ppermute x2, waiting for transfers between devices, column_halo(): right = lax.ppermute(head, WIDE, [(i + 1, i) for i in range(count - 1)])  10.8 us
    all_to_all x1, starting transfers between devices, per_device(): small = lax.all_to_all(small, ('zl', 'xl', 'yl', 'core'), 0, 0, tiled=True)  10.1 us
    all_to_all x1, waiting for transfers between devices, per_device(): middle = lax.all_to_all(by_block, ('zm', 'xm', 'ym'), 0, 0, tiled=True)  9.26 us
    all_to_all x1, starting transfers between devices, per_device(): middle = lax.all_to_all(by_block, ('zm', 'xm', 'ym'), 0, 0, tiled=True)  8.76 us
    pallas_call x1, Pallas kernels, per_device(): pl.pallas_call(front_kernel, out_shape=(jax.ShapeDtypeStruct((height, wid...  8.47 us
    ppermute x2, starting transfers between devices, column_halo(): left = lax.ppermute(tail, WIDE, [(i, i + 1) for i in range(count - 1)])  8.12 us
  transfers between devices with their start and end apart: 12, of which 7 were waited for; matrix products, arithmetic and copies ran while one was open for 1% of the time, Pallas kernels for 2%

profile of v4, /device:TPU:1, one launch (start us, length us, event | category | flops | bytes accessed | tf_op | source)
XLA Modules:
  0.0 136.3 jit_solution(14525518392546503917)
XLA Ops:
  0.6 0.8 slice_bitcast_fusion
  1.4 5.7 %collective-permute-start = (bf16[3,16,384]{2,1,0:T(8,128)(2,1)S(1)}, bf16[3,16,384]{2,1,0:T(8,128)(2,1)S(1)}, u32[]{:S(2)}, u32[]{:S(2)}) collective-permute-start(bf16[3,16,384]{2,1,0:T(8,128)(2,1)S(1)} %get-tuple-element.34), channel_id=1, source_target_pairs={{0,128},{128,256},{256,384},{384,512},{512,640},{640,768},{768,896... | collective-permute-start | bytes 110600 | tf_op jit(solution)/shard_map/ppermute | solution.py:335
  7.2 1.3 collective-permute-start.1
  8.5 0.8 fusion.2
  9.3 0.0 collective-permute-done.top_ref
  9.3 4.1 %collective-permute-done.1.bot_ref = bf16[3,16,384]{2,1,0:T(8,128)(2,1)S(1)} collective-permute-done((bf16[3,16,384]{2,1,0:T(8,128)(2,1)S(1)}, bf16[3,16,384]{2,1,0:T(8,128)(2,1)S(1)}, u32[]{:S(2)}, u32[]{:S(2)}) %collective-permute-start.1) | collective-permute-done | bytes 36896 | tf_op jit(solution)/shard_map/ppermute | solution.py:336
  13.5 1.3 collective-permute-start.3
  14.8 4.0 %collective-permute-start.2 = (bf16[14,3,384]{2,1,0:T(4,128)(2,1)S(1)}, bf16[14,3,384]{2,1,0:T(4,128)(2,1)S(1)}, u32[]{:S(2)}, u32[]{:S(2)}) collective-permute-start(bf16[14,3,384]{2,1,0:T(4,128)(2,1)S(1)} %pad_maximum_fusion.2), channel_id=1, source_target_pairs={{0,16},{16,32},{32,48},{48,64},{64,80},{80,96},{96,112},{1,17},{17... | collective-permute-start | bytes 96776 | tf_op jit(solution)/shard_map/ppermute | solution.py:345
  18.8 0.0 collective-permute-done.3.right_ref
  18.8 1.1 collective-permute-done.2.left_ref
  19.9 8.5 %front.1 = (bf16[8,16,384]{2,1,0:T(8,128)(2,1)}, f32[8,16,384]{2,1,0:T(8,128)S(1)}, bf16[8,600,128]{2,1,0:T(8,128)(2,1)S(1)}, bf16[8,600,128]{2,1,0:T(8,128)(2,1)S(1)}) custom-call(s32[1]{0:T(128)} %bitcast.core_ref, bf16[8,16,384]{2,1,0:T(8,128)(2,1)} %bitcast.13, bf16[3,16,384]{2,1,0:T(8,128)(2,1)S(1)} %collective-permute-done.top_ref, ...), custom_call_target="tpu_custom_call" | custom-call | tf_op jit(solution)/shard_map/front/pallas_call | solution.py:374
  28.4 12.4 %collective-permute-start.8 = (bf16[8,600,128]{2,1,0:T(8,128)(2,1)S(1)}, bf16[8,600,128]{2,1,0:T(8,128)(2,1)S(1)}, u32[]{:S(2)}, u32[]{:S(2)}) collective-permute-start(bf16[8,600,128]{2,1,0:T(8,128)(2,1)S(1)} %get-tuple-element.20), channel_id=1, source_target_pairs={{0,1},{1,0},{2,3},{3,2},{4,5},{5,4},{6,7},{7,6},{8,9},{9,8},{10,11... | collective-permute-start | bytes 3686408 | tf_op jit(solution)/shard_map/ppermute | solution.py:425
  40.8 1.3 collective-permute-start.4
  42.1 1.3 collective-permute-start.5
  43.4 0.4 collective-permute-done.4.top_ref.top_hbm
  43.8 3.8 %collective-permute-done.5.bot_ref.bot_hbm = f32[3,16,384]{2,1,0:T(8,128)S(1)} collective-permute-done((f32[3,16,384]{2,1,0:T(8,128)S(1)}, f32[3,16,384]{2,1,0:T(8,128)S(1)}, u32[]{:S(2)}, u32[]{:S(2)}) %collective-permute-start.5) | collective-permute-done | bytes 73760 | tf_op jit(solution)/shard_map/ppermute | solution.py:336
  47.6 0.0 collective-permute-done.8.got_ref
  47.6 1.7 %join.1 = bf16[8,600,128]{2,1,0:T(8,128)(2,1)} custom-call(bf16[8,600,128]{2,1,0:T(8,128)(2,1)S(1)} %get-tuple-element.19.mine_ref, bf16[8,600,128]{2,1,0:T(8,128)(2,1)S(1)} %collective-permute-done.8.got_ref, f32[3,16,384]{2,1,0:T(8,128)S(1)} %collective-permute-done.4.top_ref.top_hbm, f32[3,16,384]{2,1,0:T(8,128)S(1)} %collective-permute-done.5.bot_ref.bot_hbm), custom_call_target="tpu_custom_call" | custom-call | tf_op jit(solution)/shard_map/join/pallas_call | solution.py:433
  49.3 6.3 %all-to-all-start = ((bf16[8,600,128]{2,1,0:T(8,128)(2,1)}), bf16[8,600,128]{2,1,0:T(8,128)(2,1)S(1)}, u32[]{:S(2)}, u32[]{:S(2)}) async-start(bf16[8,600,128]{2,1,0:T(8,128)(2,1)} %join.1), calls=%async_computation | async-start | bytes 2457600 | tf_op jit(solution)/shard_map/all_to_all | solution.py:442
  55.7 1.3 collective-permute-start.7
  57.0 0.0 copy-start
  57.0 0.0 copy-start.1
  57.0 4.1 %collective-permute-start.6 = (f32[14,3,384]{2,1,0:T(4,128)S(1)}, f32[14,3,384]{2,1,0:T(4,128)S(1)}, u32[]{:S(2)}, u32[]{:S(2)}) collective-permute-start(f32[14,3,384]{2,1,0:T(4,128)S(1)} %pad_maximum_fusion), channel_id=1, source_target_pairs={{0,16},{16,32},{32,48},{48,64},{64,80},{80,96},{96,112},{1,17},{17... | collective-permute-start | bytes 193544 | tf_op jit(solution)/shard_map/ppermute | solution.py:345
  61.2 10.8 %collective-permute-done.7.right_ref.right_hbm = f32[14,3,384]{2,1,0:T(4,128)S(1)} collective-permute-done((f32[14,3,384]{2,1,0:T(4,128)S(1)}, f32[14,3,384]{2,1,0:T(4,128)S(1)}, u32[]{:S(2)}, u32[]{:S(2)}) %collective-permute-start.7) | collective-permute-done | bytes 64544 | tf_op jit(solution)/shard_map/ppermute | solution.py:346
  72.0 0.0 collective-permute-done.6.left_ref.left_hbm
  72.0 0.0 all-to-all-done.got_ref
  72.0 0.9 block_sum.1
  72.9 8.8 %all-to-all-start.1 = ((bf16[8,96,128]{2,1,0:T(8,128)(2,1)}), bf16[8,96,128]{2,1,0:T(8,128)(2,1)S(1)}, u32[]{:S(2)}, u32[]{:S(2)}) async-start(bf16[8,96,128]{2,1,0:T(8,128)(2,1)} %block_sum.1), calls=%async_computation.1 | async-start | bytes 393216 | tf_op jit(solution)/shard_map/all_to_all | solution.py:452
  81.7 9.3 %all-to-all-done.1.got_ref = bf16[8,96,128]{2,1,0:T(8,128)(2,1)S(1)} async-done(((bf16[8,96,128]{2,1,0:T(8,128)(2,1)}), bf16[8,96,128]{2,1,0:T(8,128)(2,1)S(1)}, u32[]{:S(2)}, u32[]{:S(2)}) %all-to-all-start.1) | async-done | bytes 196640 | tf_op jit(solution)/shard_map/all_to_all | solution.py:452
  91.0 0.2 middle_sum.1
  91.2 28.2 %all_to_all.20.got_ref = f32[8,24,128]{2,1,0:T(8,128)S(1)} all-to-all(f32[8,24,128]{2,1,0:T(8,128)S(1)} %middle_sum.1), channel_id=1, replica_groups=mesh['zh'=2,'zm'=2,'zl'=2,'xh'=2,'xm'=2,'xl'=2,'yh'=2,'ym'=2,'yl'=2,'cor..., dimensions={0} | all-to-all | bytes 196608 | tf_op jit(solution)/shard_map/all_to_all | solution.py:461
  119.4 0.7 far_sum.1
  120.1 10.1 %all-to-all-start.3 = ((f32[16,12,128]{2,1,0:T(8,128)}), f32[16,12,128]{2,1,0:T(8,128)S(1)}, u32[]{:S(2)}, u32[]{:S(2)}) async-start(f32[16,12,128]{2,1,0:T(8,128)} %get-tuple-element.23), calls=%async_computation.3 | async-start | bytes 262144 | tf_op jit(solution)/shard_map/all_to_all | solution.py:483
  130.2 0.0 copy-done
  130.2 0.0 copy-done.1
  130.2 2.2 %input_grad.1 = bf16[8,16,384]{2,1,0:T(8,128)(2,1)} custom-call(f32[8,16,384]{2,1,0:T(8,128)S(1)} %get-tuple-element.18.g_ref, f32[3,16,384]{2,1,0:T(8,128)S(1)} %collective-permute-done.4.top_ref.top_hbm, f32[3,16,384]{2,1,0:T(8,128)S(1)} %collective-permute-done.5.bot_ref.bot_hbm, f32[14,3,384]{2,1,0:T(4,128)S(1)} %collective-permute-done.6.left_ref.left_hbm, ...), custom_call_target="tpu_custom_call" | custom-call | tf_op jit(solution)/shard_map/input_grad/pallas_call | solution.py:462
  132.4 3.2 %all-to-all-done.3.got_ref = f32[16,12,128]{2,1,0:T(8,128)S(1)} async-done(((f32[16,12,128]{2,1,0:T(8,128)}), f32[16,12,128]{2,1,0:T(8,128)S(1)}, u32[]{:S(2)}, u32[]{:S(2)}) %all-to-all-start.3) | async-done | bytes 98336 | tf_op jit(solution)/shard_map/all_to_all | solution.py:483
  135.6 0.7 spread.1
  (10 shorter events, 0.2 us)
Async XLA Ops:
  1.4 7.9 %collective-permute-start = (bf16[3,16,384]{2,1,0:T(8,128)(2,1)S(1)}, bf16[3,16,384]{2,1,0:T(8,128)(2,1)S(1)}, u32[]{:S(2)}, u32[]{:S(2)}) collective-permute-start(bf16[3,16,384]{2,1,0:T(8,128)(2,1)S(1)} %get-tuple-element.34), channel_id=1, source_target_pairs={{0,128},{128,256},{256,384},{384,512},{512,640},{640,768},{768,896... | collective-permute-start | bytes 110600 | tf_op jit(solution)/shard_map/ppermute | solution.py:335
  7.2 6.3 %collective-permute-start.1 = (bf16[3,16,384]{2,1,0:T(8,128)(2,1)S(1)}, bf16[3,16,384]{2,1,0:T(8,128)(2,1)S(1)}, u32[]{:S(2)}, u32[]{:S(2)}) collective-permute-start(bf16[3,16,384]{2,1,0:T(8,128)(2,1)S(1)} %get-tuple-element.33), channel_id=1, source_target_pairs={{128,0},{256,128},{384,256},{512,384},{640,512},{768,640},{896,768... | collective-permute-start | bytes 110600 | tf_op jit(solution)/shard_map/ppermute | solution.py:336
  13.5 5.3 %collective-permute-start.3 = (bf16[14,3,384]{2,1,0:T(4,128)(2,1)S(1)}, bf16[14,3,384]{2,1,0:T(4,128)(2,1)S(1)}, u32[]{:S(2)}, u32[]{:S(2)}) collective-permute-start(bf16[14,3,384]{2,1,0:T(4,128)(2,1)S(1)} %pad_maximum_fusion.3), channel_id=1, source_target_pairs={{16,0},{32,16},{48,32},{64,48},{80,64},{96,80},{112,96},{17,1},{33... | collective-permute-start | bytes 96776 | tf_op jit(solution)/shard_map/ppermute | solution.py:346
  14.8 5.1 %collective-permute-start.2 = (bf16[14,3,384]{2,1,0:T(4,128)(2,1)S(1)}, bf16[14,3,384]{2,1,0:T(4,128)(2,1)S(1)}, u32[]{:S(2)}, u32[]{:S(2)}) collective-permute-start(bf16[14,3,384]{2,1,0:T(4,128)(2,1)S(1)} %pad_maximum_fusion.2), channel_id=1, source_target_pairs={{0,16},{16,32},{32,48},{48,64},{64,80},{80,96},{96,112},{1,17},{17... | collective-permute-start | bytes 96776 | tf_op jit(solution)/shard_map/ppermute | solution.py:345
  28.4 19.2 %collective-permute-start.8 = (bf16[8,600,128]{2,1,0:T(8,128)(2,1)S(1)}, bf16[8,600,128]{2,1,0:T(8,128)(2,1)S(1)}, u32[]{:S(2)}, u32[]{:S(2)}) collective-permute-start(bf16[8,600,128]{2,1,0:T(8,128)(2,1)S(1)} %get-tuple-element.20), channel_id=1, source_target_pairs={{0,1},{1,0},{2,3},{3,2},{4,5},{5,4},{6,7},{7,6},{8,9},{9,8},{10,11... | collective-permute-start | bytes 3686408 | tf_op jit(solution)/shard_map/ppermute | solution.py:425
  40.8 3.0 %collective-permute-start.4 = (f32[3,16,384]{2,1,0:T(8,128)S(1)}, f32[3,16,384]{2,1,0:T(8,128)S(1)}, u32[]{:S(2)}, u32[]{:S(2)}) collective-permute-start(f32[3,16,384]{2,1,0:T(8,128)S(1)} %get-tuple-element.30), channel_id=1, source_target_pairs={{0,128},{128,256},{256,384},{384,512},{512,640},{640,768},{768,896... | collective-permute-start | bytes 221192 | tf_op jit(solution)/shard_map/ppermute | solution.py:335
  42.1 5.5 %collective-permute-start.5 = (f32[3,16,384]{2,1,0:T(8,128)S(1)}, f32[3,16,384]{2,1,0:T(8,128)S(1)}, u32[]{:S(2)}, u32[]{:S(2)}) collective-permute-start(f32[3,16,384]{2,1,0:T(8,128)S(1)} %get-tuple-element.29), channel_id=1, source_target_pairs={{128,0},{256,128},{384,256},{512,384},{640,512},{768,640},{896,768... | collective-permute-start | bytes 221192 | tf_op jit(solution)/shard_map/ppermute | solution.py:336
  49.3 22.7 %all-to-all-start = ((bf16[8,600,128]{2,1,0:T(8,128)(2,1)}), bf16[8,600,128]{2,1,0:T(8,128)(2,1)S(1)}, u32[]{:S(2)}, u32[]{:S(2)}) async-start(bf16[8,600,128]{2,1,0:T(8,128)(2,1)} %join.1), calls=%async_computation | async-start | bytes 2457600 | tf_op jit(solution)/shard_map/all_to_all | solution.py:442
  55.7 16.3 %collective-permute-start.7 = (f32[14,3,384]{2,1,0:T(4,128)S(1)}, f32[14,3,384]{2,1,0:T(4,128)S(1)}, u32[]{:S(2)}, u32[]{:S(2)}) collective-permute-start(f32[14,3,384]{2,1,0:T(4,128)S(1)} %pad_maximum_fusion.1), channel_id=1, source_target_pairs={{16,0},{32,16},{48,32},{64,48},{80,64},{96,80},{112,96},{17,1},{33... | collective-permute-start | bytes 193544 | tf_op jit(solution)/shard_map/ppermute | solution.py:346
  57.0 73.2 %copy-start = (bf16[1,8,16,384]{3,2,1,0:T(8,128)(2,1)S(1)}, bf16[1,8,16,384]{3,2,1,0:T(8,128)(2,1)}, u32[]{:S(2)}) copy-start(bf16[1,8,16,384]{3,2,1,0:T(8,128)(2,1)} %param.21) | copy-start | bytes 294916
  57.0 73.2 %copy-start.1 = (f32[7,7,384]{2,1,0:T(8,128)S(1)}, f32[7,7,384]{2,1,0:T(8,128)}, u32[]{:S(2)}) copy-start(f32[7,7,384]{2,1,0:T(8,128)} %dwk_ref.1) | copy-start | bytes 225796
  57.0 15.0 %collective-permute-start.6 = (f32[14,3,384]{2,1,0:T(4,128)S(1)}, f32[14,3,384]{2,1,0:T(4,128)S(1)}, u32[]{:S(2)}, u32[]{:S(2)}) collective-permute-start(f32[14,3,384]{2,1,0:T(4,128)S(1)} %pad_maximum_fusion), channel_id=1, source_target_pairs={{0,16},{16,32},{32,48},{48,64},{64,80},{80,96},{96,112},{1,17},{17... | collective-permute-start | bytes 193544 | tf_op jit(solution)/shard_map/ppermute | solution.py:345
  72.9 18.0 %all-to-all-start.1 = ((bf16[8,96,128]{2,1,0:T(8,128)(2,1)}), bf16[8,96,128]{2,1,0:T(8,128)(2,1)S(1)}, u32[]{:S(2)}, u32[]{:S(2)}) async-start(bf16[8,96,128]{2,1,0:T(8,128)(2,1)} %block_sum.1), calls=%async_computation.1 | async-start | bytes 393216 | tf_op jit(solution)/shard_map/all_to_all | solution.py:452
  120.1 15.5 %all-to-all-start.3 = ((f32[16,12,128]{2,1,0:T(8,128)}), f32[16,12,128]{2,1,0:T(8,128)S(1)}, u32[]{:S(2)}, u32[]{:S(2)}) async-start(f32[16,12,128]{2,1,0:T(8,128)} %get-tuple-element.23), calls=%async_computation.3 | async-start | bytes 262144 | tf_op jit(solution)/shard_map/all_to_all | solution.py:483

commit v5 on v3

--- a/solution.py
+++ b/solution.py
@@ -34,58 +34,60 @@
     return lax.dot_general(a, b, (((ca,), (cb,)), ((), ())), preferred_element_type=F32)
 
 
+def fetch_kernel(*refs):
+    count = len(refs) // 2
+    copies = [
+        pltpu.make_async_copy(refs[k], refs[count + k], refs[-1].at[k]) for k in range(count)
+    ]
+    for c in copies:
+        c.start()
+    for c in copies:
+        c.wait()
+
+
 def front_kernel(
     core_ref,
-    x_hbm,
+    x_ref,
     top_ref,
     bot_ref,
     left_ref,
     right_ref,
-    cot_hbm,
-    dwk_hbm,
+    cot_ref,
+    dwk_ref,
     dwb_hbm,
     gain_hbm,
     lnb_hbm,
-    wexp_hbm,
+    wexp_ref,
     bexp_hbm,
-    wred_hbm,
+    wred_ref,
     bred_hbm,
     ls_hbm,
     block_ref,
     gconv_ref,
-    mine_hbm,
     send_hbm,
-    x_ref,
-    cot_ref,
-    dwk_ref,
+    both,
+    stack_ref,
+    own_ref,
     dwb_ref,
     gain_ref,
     lnb_ref,
-    wexp_ref,
     bexp_ref,
-    wred_ref,
     bred_ref,
     ls_ref,
     xp,
     conv,
-    both,
     small,
-    mine_ref,
     send_ref,
     sems,
+    out_sems,
 ):
     pairs = (
-        (x_hbm, x_ref),
-        (dwk_hbm, dwk_ref),
         (dwb_hbm, dwb_ref),
         (gain_hbm, gain_ref),
         (lnb_hbm, lnb_ref),
-        (cot_hbm, cot_ref),
         (ls_hbm, ls_ref),
         (bexp_hbm, bexp_ref),
         (bred_hbm, bred_ref),
-        (wexp_hbm, wexp_ref),
-        (wred_hbm, wred_ref),
     )
     copies = [pltpu.make_async_copy(a, b, sems.at[k]) for k, (a, b) in enumerate(pairs)]
     for c in copies:
@@ -103,8 +105,6 @@
         at = BLOCKS * (p % 4) + l
         small[p // 4, at : at + 1, :] = value
 
-    for c in copies[0:2]:
-        c.wait()
     xp[HALO : HALO + height, HALO : HALO + width, :] = x_ref[...].astype(F32)
     for l in range(BLOCKS):
         ln = slice(LANES * l, LANES * (l + 1))
@@ -114,7 +114,7 @@
             for i in range(7):
                 acc = acc + dwk_ref[i, j : j + 1, ln] * s[i : i + height]
         conv[:, ln] = acc.reshape(pixels, LANES)
-    for c in copies[2:]:
+    for c in copies:
         c.wait()
     flat = conv[...] + row(dwb_ref)
     centered = flat - jnp.mean(flat, axis=-1, keepdims=True)
@@ -163,6 +163,24 @@
                 put(7 * i + j, l, jnp.sum(part, axis=0, keepdims=True))
     value = small[:, 0:SHARE, :]
     small[:, SHARE : 2 * SHARE, :] = value - value.astype(BF16).astype(F32)
+    stack_ref[0:pixels, :] = normed
+    stack_ref[pixels : 2 * pixels, :] = g_branch
+    core = core_ref[0]
+    own_ref[...] = small[pl.ds(PIECES * core, PIECES)]
+    send_ref[:, BIG:ROWS, :] = small[pl.ds(PIECES * (1 - core), PIECES)].astype(BF16)
+    products(1 - core, both, stack_ref[...], send_ref, send_hbm, out_sems)
+
+
+def products(core, both, stack, out, hbm, sems):
+    pixels = stack.shape[0] // 2
+    copies = []
+
+    def flush(rows):
+        c = pltpu.make_async_copy(out.at[:, rows], hbm.at[:, rows], sems.at[len(copies)])
+        c.start()
+        copies.append(c)
+
+    flush(slice(BIG, ROWS))
     chan = lax.broadcasted_iota(jnp.int32, (D, D), 0)
     column = lax.broadcasted_iota(jnp.int32, (1, D), 1)
     half = (column >= D // 2).astype(jnp.int32)
@@ -173,56 +191,49 @@
     base = 4 * DROWS * block + jnp.where(of_e, inside, inside - DROWS)
     pixel = lax.broadcasted_iota(jnp.int32, (2 * pixels, 1), 0)
     keep = jnp.where(pixel < pixels, 1, 0) == jnp.where(of_e, 1, 0)
-    stack = jnp.concatenate([normed, g_branch], axis=0)
     lane = lax.broadcasted_iota(jnp.int32, (1, 1, LANES), 2)
-    outputs = []
-
-    def flush(out, hbm, rows):
-        c = pltpu.make_async_copy(out.at[:, rows], hbm.at[:, rows], sems.at[11 + len(outputs)])
-        c.start()
-        outputs.append(c)
-
-    for which, (out, hbm) in enumerate(((send_ref, send_hbm), (mine_ref, mine_hbm))):
-        core = core_ref[0] if which == 1 else 1 - core_ref[0]
-        out[:, BIG:ROWS, :] = small[pl.ds(PIECES * core, PIECES)].astype(BF16)
-        flush(out, hbm, slice(BIG, ROWS))
-        right = []
+    right = []
+    for order in range(2):
+        turn = half if order == 0 else 1 - half
+        pick = (chan == base + 2 * DROWS * turn + DROWS * core).astype(F32).astype(BF16)
+        right.append(jnp.where(keep, matmul(stack, pick, 1, 0), 0.0).astype(BF16))
+    for low in range(2):
+        g = []
         for order in range(2):
-            turn = half if order == 0 else 1 - half
-            pick = (chan == base + 2 * DROWS * turn + DROWS * core).astype(F32).astype(BF16)
-            right.append(jnp.where(keep, matmul(stack, pick, 1, 0), 0.0).astype(BF16))
-        for low in range(2):
-            g = []
-            for order in range(2):
-                f = low + 2 * order
-                part = matmul(both[:, D * f : D * (f + 1)], right[order], 0, 0)
-                g.append(part.reshape(2, 4, 2, FROWS, D))
-            for zl in range(2):
-                for xl in range(2):
-                    for yl in range(2):
-                        one, two = g[yl][zl, :, xl], g[1 - yl][zl, :, xl]
-                        pieces = (
-                            one[:, :, 0:LANES],
-                            jnp.where(
-                                lane < LANES // 2,
-                                one[:, :, LANES : 2 * LANES],
-                                two[:, :, LANES : 2 * LANES],
-                            ),
-                            two[:, :, 2 * LANES : D],
-                        )
-                        for l, piece in enumerate(pieces):
-                            at = 8 * FROWS * l + 4 * FROWS * low
-                            out[4 * zl + 2 * xl + yl, at : at + 4 * FROWS, :] = piece.reshape(
-                                4 * FROWS, LANES
-                            ).astype(BF16)
-            for l in range(BLOCKS):
-                at = 8 * FROWS * l + 4 * FROWS * low
-                flush(out, hbm, slice(at, at + 4 * FROWS))
-    for c in outputs:
+            f = low + 2 * order
+            part = matmul(both[:, D * f : D * (f + 1)], right[order], 0, 0)
+            g.append(part.reshape(2, 4, 2, FROWS, D))
+        for zl in range(2):
+            for xl in range(2):
+                for yl in range(2):
+                    one, two = g[yl][zl, :, xl], g[1 - yl][zl, :, xl]
+                    pieces = (
+                        one[:, :, 0:LANES],
+                        jnp.where(
+                            lane < LANES // 2,
+                            one[:, :, LANES : 2 * LANES],
+                            two[:, :, LANES : 2 * LANES],
+                        ),
+                        two[:, :, 2 * LANES : D],
+                    )
+                    for l, piece in enumerate(pieces):
+                        at = 8 * FROWS * l + 4 * FROWS * low
+                        out[4 * zl + 2 * xl + yl, at : at + 4 * FROWS, :] = piece.reshape(
+                            4 * FROWS, LANES
+                        ).astype(BF16)
+        for l in range(BLOCKS):
+            at = 8 * FROWS * l + 4 * FROWS * low
+            flush(slice(at, at + 4 * FROWS))
+    for c in copies:
         c.wait()
 
 
-def join_kernel(mine_ref, got_ref, top_hbm, bot_hbm, out_ref):
+def own_kernel(core_ref, both_ref, stack_ref, small_ref, out_hbm, out_ref, sems):
+    out_ref[:, BIG:ROWS, :] = small_ref[...].astype(BF16)
+    products(core_ref[0], both_ref, stack_ref[...], out_ref, out_hbm, sems)
+
+
+def join_kernel(mine_ref, got_ref, out_ref):
     big = mine_ref[:, 0:BIG, :].astype(F32) + got_ref[:, 0:BIG, :].astype(F32)
     out_ref[:, 0:BIG, :] = big.astype(BF16)
     both = mine_ref[:, BIG:ROWS, :].astype(F32) + got_ref[:, BIG:ROWS, :].astype(F32)
@@ -231,7 +242,7 @@
     out_ref[:, BIG:ROWS, :] = jnp.concatenate([value, low], axis=1).astype(BF16)
 
 
-def block_sum_kernel(yl_ref, got_ref, left_hbm, right_hbm, out_ref, total):
+def block_sum_kernel(yl_ref, got_ref, top_any, bot_any, out_ref, total):
     total[...] = jnp.sum(got_ref[...].astype(F32), axis=0)
     small = total[BIG : BIG + SHARE, :] + total[BIG + SHARE : ROWS, :]
     side = LANES // 2
@@ -257,7 +268,7 @@
                     out_ref[16 * zh + 4 * xh + yh] = piece.astype(BF16)
 
 
-def far_sum_kernel(scale, got_ref, ge_ref, gr_ref, small_ref):
+def far_sum_kernel(scale, got_ref, left_any, right_any, ge_ref, gr_ref, small_ref):
     total = jnp.sum(got_ref[...].astype(F32), axis=0) * scale
     turned = jnp.transpose(total, (1, 0))
     ge_ref[...] = turned[0:DROWS, 0:FROWS]
@@ -287,10 +298,10 @@
 def input_grad_kernel(g_ref, top_ref, bot_ref, left_ref, right_ref, cot_ref, dwk_ref, out_ref, gp):
     height, width = g_ref.shape[0], g_ref.shape[1]
     gp[HALO : HALO + height, HALO : HALO + width, :] = g_ref[...]
-    gp[0:HALO, HALO : HALO + width, :] = top_ref[...]
-    gp[HALO + height :, HALO : HALO + width, :] = bot_ref[...]
-    gp[:, 0:HALO, :] = left_ref[...]
-    gp[:, HALO + width : 2 * HALO + width, :] = right_ref[...]
+    gp[0:HALO, HALO : HALO + width, :] = top_ref[...].astype(F32)
+    gp[HALO + height :, HALO : HALO + width, :] = bot_ref[...].astype(F32)
+    gp[:, 0:HALO, :] = left_ref[...].astype(F32)
+    gp[:, HALO + width : 2 * HALO + width, :] = right_ref[...].astype(F32)
     for l in range(BLOCKS):
         ln = slice(LANES * l, LANES * (l + 1))
         acc = cot_ref[:, :, ln].astype(F32)
@@ -345,74 +356,94 @@
     whole = lambda n: [pl.BlockSpec(memory_space=pltpu.VMEM)] * n
     away = lambda v: pltpu.with_memory_space_constraint(v, pltpu.HBM)
     hbm = lambda n: [pl.BlockSpec(memory_space=pltpu.HBM)] * n
-    block_out, gconv, mine, send = pl.pallas_call(
+    fetched = (x, cot, dw_kernel, w_expand, w_reduce)
+    x_near, cot_near, dwk_near, wexp_near, wred_near = pl.pallas_call(
+        fetch_kernel,
+        out_shape=tuple(jax.ShapeDtypeStruct(v.shape, v.dtype) for v in fetched),
+        in_specs=hbm(5),
+        out_specs=tuple(whole(5)),
+        scratch_shapes=[pltpu.SemaphoreType.DMA((5,))],
+        compiler_params=LIMIT,
+        name="fetch",
+    )(*[away(v) for v in fetched])
+    smem = [pl.BlockSpec(memory_space=pltpu.SMEM)]
+    pixels = height * width
+    block_out, gconv, send, both, stack, own = pl.pallas_call(
         front_kernel,
         out_shape=(
             jax.ShapeDtypeStruct((height, width, D), BF16),
             jax.ShapeDtypeStruct((height, width, D), F32),
             jax.ShapeDtypeStruct((PIECES, ROWS, LANES), BF16),
-            jax.ShapeDtypeStruct((PIECES, ROWS, LANES), BF16),
+            jax.ShapeDtypeStruct((2 * pixels, FF), BF16),
+            jax.ShapeDtypeStruct((2 * pixels, D), BF16),
+            jax.ShapeDtypeStruct((PIECES, 2 * SHARE, LANES), F32),
         ),
-        in_specs=[pl.BlockSpec(memory_space=pltpu.SMEM)] + hbm(1) + whole(4) + hbm(10),
-        out_specs=tuple(whole(2) + hbm(2)),
+        in_specs=smem + whole(7) + hbm(3) + whole(1) + hbm(1) + whole(1) + hbm(2),
+        out_specs=tuple(whole(2) + hbm(1) + whole(3)),
         scratch_shapes=[
-            pltpu.VMEM((height, width, D), BF16),
-            pltpu.VMEM((height, width, D), BF16),
-            pltpu.VMEM((7, 7, D), F32),
             pltpu.VMEM((D,), F32),
             pltpu.VMEM((D,), F32),
             pltpu.VMEM((D,), F32),
-            pltpu.VMEM((D, FF), BF16),
             pltpu.VMEM((FF,), F32),
-            pltpu.VMEM((FF, D), BF16),
             pltpu.VMEM((D,), F32),
             pltpu.VMEM((D,), F32),
             pltpu.VMEM((height + 2 * HALO, width + 8, D), F32),
-            pltpu.VMEM((height * width, D), F32),
-            pltpu.VMEM((2 * height * width, FF), BF16),
+            pltpu.VMEM((pixels, D), F32),
             pltpu.VMEM((2 * PIECES, 2 * SHARE, LANES), F32),
             pltpu.VMEM((PIECES, ROWS, LANES), BF16),
-            pltpu.VMEM((PIECES, ROWS, LANES), BF16),
-            pltpu.SemaphoreType.DMA((25,)),
+            pltpu.SemaphoreType.DMA((6,)),
+            pltpu.SemaphoreType.DMA((7,)),
         ],
         compiler_params=LIMIT,
         name="front",
     )(
         core.reshape(1),
-        away(x),
+        x_near,
         top,
         bot,
         left,
         right,
-        away(cot),
-        away(dw_kernel),
+        cot_near,
+        dwk_near,
         away(dw_bias),
         away(layer_norm_gain),
         away(layer_norm_bias),
-        away(w_expand),
+        wexp_near,
         away(b_expand),
-        away(w_reduce),
+        wred_near,
         away(b_reduce),
         away(layer_scale),
     )
 
     got = lax.ppermute(send, "core", [(0, 1), (1, 0)])
-    gtop, gbot = shifted(gconv, TALL, 0)
-    gleft, gright = column_halo(gconv, gtop, gbot)
+    mine = pl.pallas_call(
+        own_kernel,
+        out_shape=jax.ShapeDtypeStruct((PIECES, ROWS, LANES), BF16),
+        in_specs=smem + whole(3),
+        out_specs=hbm(1)[0],
+        scratch_shapes=[
+            pltpu.VMEM((PIECES, ROWS, LANES), BF16),
+            pltpu.SemaphoreType.DMA((7,)),
+        ],
+        compiler_params=LIMIT,
+        name="own",
+    )(core.reshape(1), both, stack, own)
+    edges = gconv.astype(BF16)
+    gtop, gbot = shifted(edges, TALL, 0)
+    gleft, gright = column_halo(edges, gtop, gbot)
 
     step = 2
     spec = pl.BlockSpec((step, ROWS, LANES), lambda i: (i, 0, 0))
     free = lambda n: [pl.BlockSpec(memory_space=pl.ANY)] * n
-    smem = [pl.BlockSpec(memory_space=pltpu.SMEM)]
     joined = pl.pallas_call(
         join_kernel,
         out_shape=jax.ShapeDtypeStruct((PIECES, ROWS, LANES), BF16),
         grid=(PIECES // step,),
-        in_specs=[spec, spec] + free(2),
+        in_specs=[spec, spec],
         out_specs=spec,
         compiler_params=LIMIT,
         name="join",
-    )(mine, got, gtop, gbot)
+    )(mine, got)
     near = lax.all_to_all(joined, ("zl", "xl", "yl"), 0, 0, tiled=True)
     by_block = pl.pallas_call(
         block_sum_kernel,
@@ -422,7 +453,7 @@
         scratch_shapes=[pltpu.VMEM((ROWS, LANES), F32)],
         compiler_params=LIMIT,
         name="block_sum",
-    )(yl.reshape(1), near, gleft, gright)
+    )(yl.reshape(1), near, gtop, gbot)
     grad_in = pl.pallas_call(
         input_grad_kernel,
         out_shape=jax.ShapeDtypeStruct((height, width, D), BF16),
@@ -431,7 +462,7 @@
         scratch_shapes=[pltpu.VMEM((height + 2 * HALO, width + 8, D), F32)],
         compiler_params=LIMIT,
         name="input_grad",
-    )(gconv, gtop, gbot, gleft, gright, cot, dw_kernel)
+    )(gconv, gtop, gbot, gleft, gright, cot_near, dwk_near)
     by_block = lax.all_to_all(by_block, ("zh", "xh", "yh"), 0, 0, tiled=True)
     grad_expand, grad_reduce_t, small = pl.pallas_call(
         functools.partial(far_sum_kernel, scale),
@@ -440,11 +471,11 @@
             jax.ShapeDtypeStruct((DROWS, FROWS), F32),
             jax.ShapeDtypeStruct((2 * PIECES, SHARE, LANES), F32),
         ),
-        in_specs=whole(1),
+        in_specs=whole(1) + free(2),
         out_specs=tuple(whole(3)),
         compiler_params=LIMIT,
         name="far_sum",
-    )(by_block)
+    )(by_block, gleft, gright)
     small = lax.all_to_all(small, ("zl", "xl", "yl", "core"), 0, 0, tiled=True)
     gker, vectors, gbexp = pl.pallas_call(
         spread_kernel,

time: 126 us -> 117 us (0.929)
  blocking collectives: 37.2 us -> 0 us
  starting transfers between devices: 47.9 us -> 62.2 us
  waiting for transfers between devices: 23.6 us -> 35.3 us
  Pallas kernels: 14.2 us -> 16 us
    all_to_all x1 -> x0, blocking collectives: 37.2 us -> none  [per_device(): by_block = lax.all_to_all(by_block, ('zh', 'xh', 'yh'), 0, 0, tiled=True)]
    all_to_all x0 -> x1, starting transfers between devices: none -> 16.8 us  [per_device(): by_block = lax.all_to_all(by_block, ('zh', 'xh', 'yh'), 0, 0, tiled=True)]
    all_to_all x0 -> x1, waiting for transfers between devices: none -> 10.8 us  [per_device(): by_block = lax.all_to_all(by_block, ('zh', 'xh', 'yh'), 0, 0, tiled=True)]
    all_to_all x1, waiting for transfers between devices: 0.01 us -> 9.94 us  [per_device(): near = lax.all_to_all(joined, ('zl', 'xl', 'yl'), 0, 0, tiled=True)]
    ppermute x2, waiting for transfers between devices: 11 us -> 4.05 us  [column_halo(): right = lax.ppermute(head, WIDE, [(i + 1, i) for i in range(count - 1)])]
    ppermute x2, waiting for transfers between devices: 7.87 us -> 2.09 us  [shifted(): after = lax.ppermute(head, axis, [(i + 1, i) for i in range(count - 1)])]
    ppermute x2, starting transfers between devices: 7.06 us -> 10.9 us  [shifted(): before = lax.ppermute(tail, axis, [(i, i + 1) for i in range(count - 1)])]
    pallas_call x0 -> x2, Pallas kernels: none -> 3.16 us  [the longest x1 1.83 us: per_device(): pl.pallas_call(fetch_kernel, out_shape=tuple((jax.ShapeDtypeStruct(v.shap...]
  transfers between devices with their start and end apart: 11 -> 12, of which waited for: 6 -> 10; matrix products, arithmetic and copies ran while one was open for 1% -> 1% of each run, Pallas kernels for 2% -> 5%
where the time goes in v5:
time: 117 us; the launch traced here: 116 us
  starting transfers between devices  62.2 us (53%)
  waiting for transfers between devices  35.3 us (30%)
  Pallas kernels  16 us (14%)
  local copies, waits for them, and re-layouts  1.73 us (1%)
    all_to_all x1, starting transfers between devices, per_device(): by_block = lax.all_to_all(by_block, ('zh', 'xh', 'yh'), 0, 0, tiled=True)  16.8 us
    ppermute x1, starting transfers between devices, per_device(): got = lax.ppermute(send, 'core', [(0, 1), (1, 0)])  14.1 us
    ppermute x2, starting transfers between devices, shifted(): before = lax.ppermute(tail, axis, [(i, i + 1) for i in range(count - 1)])  10.9 us
    all_to_all x1, waiting for transfers between devices, per_device(): by_block = lax.all_to_all(by_block, ('zh', 'xh', 'yh'), 0, 0, tiled=True)  10.8 us
    all_to_all x1, waiting for transfers between devices, per_device(): near = lax.all_to_all(joined, ('zl', 'xl', 'yl'), 0, 0, tiled=True)  9.94 us
    all_to_all x1, starting transfers between devices, per_device(): small = lax.all_to_all(small, ('zl', 'xl', 'yl', 'core'), 0, 0, tiled=True)  6.58 us
    pallas_call x1, Pallas kernels, per_device(): pl.pallas_call(front_kernel, out_shape=(jax.ShapeDtypeStruct((height, wid...  6.34 us
    ppermute x2, starting transfers between devices, column_halo(): left = lax.ppermute(tail, WIDE, [(i, i + 1) for i in range(count - 1)])  5.1 us
  transfers between devices with their start and end apart: 12, of which 10 were waited for; matrix products, arithmetic and copies ran while one was open for 1% of the time, Pallas kernels for 5%

profile of v5, /device:TPU:1, one launch (start us, length us, event | category | flops | bytes accessed | tf_op | source)
XLA Modules:
  0.0 116.2 jit_solution(4998364982049892978)
XLA Ops:
  0.6 0.8 slice_bitcast_fusion
  1.4 1.3 %collective-permute-start.1 = (bf16[3,16,384]{2,1,0:T(8,128)(2,1)S(1)}, bf16[3,16,384]{2,1,0:T(8,128)(2,1)S(1)}, u32[]{:S(2)}, u32[]{:S(2)}) collective-permute-start(bf16[3,16,384]{2,1,0:T(8,128)(2,1)S(1)} %get-tuple-element.47), channel_id=1, source_target_pairs={{128,0},{256,128},{384,256},{512,384},{640,512},{768,640},{896,768... | collective-permute-start | bytes 110600 | tf_op jit(solution)/shard_map/ppermute | solution.py:321
  2.7 6.4 %collective-permute-start = (bf16[3,16,384]{2,1,0:T(8,128)(2,1)S(1)}, bf16[3,16,384]{2,1,0:T(8,128)(2,1)S(1)}, u32[]{:S(2)}, u32[]{:S(2)}) collective-permute-start(bf16[3,16,384]{2,1,0:T(8,128)(2,1)S(1)} %get-tuple-element.48), channel_id=1, source_target_pairs={{0,128},{128,256},{256,384},{384,512},{512,640},{640,768},{768,896... | collective-permute-start | bytes 110600 | tf_op jit(solution)/shard_map/ppermute | solution.py:320
  9.1 0.8 fusion.2
  9.9 0.0 collective-permute-done.1.bot_ref
  10.0 0.2 collective-permute-done.top_ref
  10.2 3.1 %collective-permute-start.2 = (bf16[14,3,384]{2,1,0:T(4,128)(2,1)S(1)}, bf16[14,3,384]{2,1,0:T(4,128)(2,1)S(1)}, u32[]{:S(2)}, u32[]{:S(2)}) collective-permute-start(bf16[14,3,384]{2,1,0:T(4,128)(2,1)S(1)} %pad_maximum_fusion), channel_id=1, source_target_pairs={{0,16},{16,32},{32,48},{48,64},{64,80},{80,96},{96,112},{1,17},{17... | collective-permute-start | bytes 96776 | tf_op jit(solution)/shard_map/ppermute | solution.py:330
  13.4 1.3 %collective-permute-start.3 = (bf16[14,3,384]{2,1,0:T(4,128)(2,1)S(1)}, bf16[14,3,384]{2,1,0:T(4,128)(2,1)S(1)}, u32[]{:S(2)}, u32[]{:S(2)}) collective-permute-start(bf16[14,3,384]{2,1,0:T(4,128)(2,1)S(1)} %pad_maximum_fusion.1), channel_id=1, source_target_pairs={{16,0},{32,16},{48,32},{64,48},{80,64},{96,80},{112,96},{17,1},{33... | collective-permute-start | bytes 96776 | tf_op jit(solution)/shard_map/ppermute | solution.py:331
  14.7 1.8 %fetch.1 = (bf16[8,16,384]{2,1,0:T(8,128)(2,1)S(1)}, bf16[8,16,384]{2,1,0:T(8,128)(2,1)S(1)}, f32[7,7,384]{2,1,0:T(8,128)S(1)}, bf16[384,1536]{1,0:T(8,128)(2,1)S(1)}, bf16[1536,384]{1,0:T(8,128)(2,1)S(1)}) custom-call(bf16[8,16,384]{2,1,0:T(8,128)(2,1)} %bitcast.11, bf16[8,16,384]{2,1,0:T(8,128)(2,1)} %bitcast.12, f32[7,7,384]{2,1,0:T(8,128)} %refs_2_.1, ...), custom_call_target="tpu_custom_call" | custom-call | tf_op jit(solution)/shard_map/fetch/pallas_call | solution.py:360
  16.5 0.0 collective-permute-done.2.left_ref
  16.5 1.6 %collective-permute-done.3.right_ref = bf16[14,3,384]{2,1,0:T(4,128)(2,1)S(1)} collective-permute-done((bf16[14,3,384]{2,1,0:T(4,128)(2,1)S(1)}, bf16[14,3,384]{2,1,0:T(4,128)(2,1)S(1)}, u32[]{:S(2)}, u32[]{:S(2)}) %collective-permute-start.3) | collective-permute-done | bytes 32288 | tf_op jit(solution)/shard_map/ppermute | solution.py:331
  18.1 6.3 %front.1 = (bf16[8,16,384]{2,1,0:T(8,128)(2,1)}, f32[8,16,384]{2,1,0:T(8,128)S(1)}, bf16[8,600,128]{2,1,0:T(8,128)(2,1)}, bf16[256,1536]{1,0:T(8,128)(2,1)S(1)},...) custom-call(s32[1]{0:T(128)} %bitcast.core_ref, bf16[8,16,384]{2,1,0:T(8,128)(2,1)S(1)} %get-tuple-element.24.x_ref, ...), custom_call_target="tpu_custom_call" | custom-call | tf_op jit(solution)/shard_map/front/pallas_call | solution.py:371
  24.5 14.1 %collective-permute-start.8 = (bf16[8,600,128]{2,1,0:T(8,128)(2,1)}, bf16[8,600,128]{2,1,0:T(8,128)(2,1)S(1)}, u32[]{:S(2)}, u32[]{:S(2)}) collective-permute-start(bf16[8,600,128]{2,1,0:T(8,128)(2,1)} %get-tuple-element.34), channel_id=1, source_target_pairs={{0,1},{1,0},{2,3},{3,2},{4,5},{5,4},{6,7},{7,6},{8,9},{9,8},{10,11... | collective-permute-start | bytes 3686408 | tf_op jit(solution)/shard_map/ppermute | solution.py:418
  38.6 1.3 %own.1.mine_ref = bf16[8,600,128]{2,1,0:T(8,128)(2,1)S(1)} custom-call(s32[1]{0:T(128)} %bitcast.core_ref, bf16[256,1536]{1,0:T(8,128)(2,1)S(1)} %get-tuple-element.31.both_ref, bf16[256,384]{1,0:T(8,128)(2,1)S(1)} %get-tuple-element.32.stack_ref, f32[8,24,128]{2,1,0:T(8,128)S(1)} %get-tuple-element.33.small_ref), custom_call_target="tpu_custom_call" | custom-call | tf_op jit(solution)/shard_map/own/pallas_call | solution.py:419
  40.0 1.4 %collective-permute-done.8.got_ref = bf16[8,600,128]{2,1,0:T(8,128)(2,1)S(1)} collective-permute-done((bf16[8,600,128]{2,1,0:T(8,128)(2,1)}, bf16[8,600,128]{2,1,0:T(8,128)(2,1)S(1)}, u32[]{:S(2)}, u32[]{:S(2)}) %collective-permute-start.8) | collective-permute-done | bytes 1228832 | tf_op jit(solution)/shard_map/ppermute | solution.py:418
  41.4 1.7 %join.1 = bf16[8,600,128]{2,1,0:T(8,128)(2,1)} custom-call(bf16[8,600,128]{2,1,0:T(8,128)(2,1)S(1)} %own.1.mine_ref, bf16[8,600,128]{2,1,0:T(8,128)(2,1)S(1)} %collective-permute-done.8.got_ref), custom_call_target="tpu_custom_call" | custom-call | tf_op jit(solution)/shard_map/join/pallas_call | solution.py:438
  43.1 3.6 %all-to-all-start = ((bf16[8,600,128]{2,1,0:T(8,128)(2,1)}), bf16[8,600,128]{2,1,0:T(8,128)(2,1)S(1)}, u32[]{:S(2)}, u32[]{:S(2)}) async-start(bf16[8,600,128]{2,1,0:T(8,128)(2,1)} %join.1), calls=%async_computation | async-start | bytes 2457600 | tf_op jit(solution)/shard_map/all_to_all | solution.py:447
  46.7 1.3 %collective-permute-start.5 = (bf16[3,16,384]{2,1,0:T(8,128)(2,1)S(1)}, bf16[3,16,384]{2,1,0:T(8,128)(2,1)S(1)}, u32[]{:S(2)}, u32[]{:S(2)}) collective-permute-start(bf16[3,16,384]{2,1,0:T(8,128)(2,1)S(1)} %get-tuple-element.43), channel_id=1, source_target_pairs={{128,0},{256,128},{384,256},{512,384},{640,512},{768,640},{896,768... | collective-permute-start | bytes 110600 | tf_op jit(solution)/shard_map/ppermute | solution.py:321
  48.0 4.5 %collective-permute-start.4 = (bf16[3,16,384]{2,1,0:T(8,128)(2,1)S(1)}, bf16[3,16,384]{2,1,0:T(8,128)(2,1)S(1)}, u32[]{:S(2)}, u32[]{:S(2)}) collective-permute-start(bf16[3,16,384]{2,1,0:T(8,128)(2,1)S(1)} %get-tuple-element.44), channel_id=1, source_target_pairs={{0,128},{128,256},{256,384},{384,512},{512,640},{640,768},{768,896... | collective-permute-start | bytes 110600 | tf_op jit(solution)/shard_map/ppermute | solution.py:320
  52.6 2.1 %collective-permute-done.5.bot_ref.bot_any = bf16[3,16,384]{2,1,0:T(8,128)(2,1)S(1)} collective-permute-done((bf16[3,16,384]{2,1,0:T(8,128)(2,1)S(1)}, bf16[3,16,384]{2,1,0:T(8,128)(2,1)S(1)}, u32[]{:S(2)}, u32[]{:S(2)}) %collective-permute-start.5) | collective-permute-done | bytes 36896 | tf_op jit(solution)/shard_map/ppermute | solution.py:321
  54.7 1.0 collective-permute-done.4.top_ref.top_any
  55.6 9.9 %all-to-all-done.got_ref = bf16[8,600,128]{2,1,0:T(8,128)(2,1)S(1)} async-done(((bf16[8,600,128]{2,1,0:T(8,128)(2,1)}), bf16[8,600,128]{2,1,0:T(8,128)(2,1)S(1)}, u32[]{:S(2)}, u32[]{:S(2)}) %all-to-all-start) | async-done | bytes 1228832 | tf_op jit(solution)/shard_map/all_to_all | solution.py:447
  65.6 1.1 block_sum.1
  66.7 16.8 %all-to-all-start.1 = ((bf16[64,24,128]{2,1,0:T(8,128)(2,1)}), bf16[64,24,128]{2,1,0:T(8,128)(2,1)S(1)}, u32[]{:S(2)}, u32[]{:S(2)}) async-start(bf16[64,24,128]{2,1,0:T(8,128)(2,1)} %block_sum.1), calls=%async_computation.1 | async-start | bytes 786432 | tf_op jit(solution)/shard_map/all_to_all | solution.py:466
  83.5 2.0 %collective-permute-start.6 = (bf16[14,3,384]{2,1,0:T(4,128)(2,1)S(1)}, bf16[14,3,384]{2,1,0:T(4,128)(2,1)S(1)}, u32[]{:S(2)}, u32[]{:S(2)}) collective-permute-start(bf16[14,3,384]{2,1,0:T(4,128)(2,1)S(1)} %pad_maximum_fusion.2), channel_id=1, source_target_pairs={{0,16},{16,32},{32,48},{48,64},{64,80},{80,96},{96,112},{1,17},{17... | collective-permute-start | bytes 96776 | tf_op jit(solution)/shard_map/ppermute | solution.py:330
  85.6 1.3 %collective-permute-start.7 = (bf16[14,3,384]{2,1,0:T(4,128)(2,1)S(1)}, bf16[14,3,384]{2,1,0:T(4,128)(2,1)S(1)}, u32[]{:S(2)}, u32[]{:S(2)}) collective-permute-start(bf16[14,3,384]{2,1,0:T(4,128)(2,1)S(1)} %pad_maximum_fusion.3), channel_id=1, source_target_pairs={{16,0},{32,16},{48,32},{64,48},{80,64},{96,80},{112,96},{17,1},{33... | collective-permute-start | bytes 96776 | tf_op jit(solution)/shard_map/ppermute | solution.py:331
  86.9 2.5 %collective-permute-done.6.left_ref.left_any = bf16[14,3,384]{2,1,0:T(4,128)(2,1)S(1)} collective-permute-done((bf16[14,3,384]{2,1,0:T(4,128)(2,1)S(1)}, bf16[14,3,384]{2,1,0:T(4,128)(2,1)S(1)}, u32[]{:S(2)}, u32[]{:S(2)}) %collective-permute-start.6) | collective-permute-done | bytes 32288 | tf_op jit(solution)/shard_map/ppermute | solution.py:330
  89.4 2.4 %collective-permute-done.7.right_ref.right_any = bf16[14,3,384]{2,1,0:T(4,128)(2,1)S(1)} collective-permute-done((bf16[14,3,384]{2,1,0:T(4,128)(2,1)S(1)}, bf16[14,3,384]{2,1,0:T(4,128)(2,1)S(1)}, u32[]{:S(2)}, u32[]{:S(2)}) %collective-permute-start.7) | collective-permute-done | bytes 32288 | tf_op jit(solution)/shard_map/ppermute | solution.py:331
  91.8 10.8 %all-to-all-done.1.got_ref = bf16[64,24,128]{2,1,0:T(8,128)(2,1)S(1)} async-done(((bf16[64,24,128]{2,1,0:T(8,128)(2,1)}), bf16[64,24,128]{2,1,0:T(8,128)(2,1)S(1)}, u32[]{:S(2)}, u32[]{:S(2)}) %all-to-all-start.1) | async-done | bytes 393248 | tf_op jit(solution)/shard_map/all_to_all | solution.py:466
  102.7 0.8 far_sum.1
  103.5 6.6 %all-to-all-start.2 = ((f32[16,12,128]{2,1,0:T(8,128)}), f32[16,12,128]{2,1,0:T(8,128)S(1)}, u32[]{:S(2)}, u32[]{:S(2)}) async-start(f32[16,12,128]{2,1,0:T(8,128)} %get-tuple-element.37), calls=%async_computation.2 | async-start | bytes 262144 | tf_op jit(solution)/shard_map/all_to_all | solution.py:479
  110.0 2.1 %input_grad.1 = bf16[8,16,384]{2,1,0:T(8,128)(2,1)} custom-call(f32[8,16,384]{2,1,0:T(8,128)S(1)} %get-tuple-element.30.g_ref, bf16[3,16,384]{2,1,0:T(8,128)(2,1)S(1)} %collective-permute-done.4.top_ref.top_any, bf16[3,16,384]{2,1,0:T(8,128)(2,1)S(1)} %collective-permute-done.5.bot_ref.bot_any, ...), custom_call_target="tpu_custom_call" | custom-call | tf_op jit(solution)/shard_map/input_grad/pallas_call | solution.py:457
  112.2 3.3 %all-to-all-done.2.got_ref = f32[16,12,128]{2,1,0:T(8,128)S(1)} async-done(((f32[16,12,128]{2,1,0:T(8,128)}), f32[16,12,128]{2,1,0:T(8,128)S(1)}, u32[]{:S(2)}, u32[]{:S(2)}) %all-to-all-start.2) | async-done | bytes 98336 | tf_op jit(solution)/shard_map/all_to_all | solution.py:479
  115.5 0.7 spread.1
  (11 shorter events, 0.2 us)
Async XLA Ops:
  1.4 8.5 %collective-permute-start.1 = (bf16[3,16,384]{2,1,0:T(8,128)(2,1)S(1)}, bf16[3,16,384]{2,1,0:T(8,128)(2,1)S(1)}, u32[]{:S(2)}, u32[]{:S(2)}) collective-permute-start(bf16[3,16,384]{2,1,0:T(8,128)(2,1)S(1)} %get-tuple-element.47), channel_id=1, source_target_pairs={{128,0},{256,128},{384,256},{512,384},{640,512},{768,640},{896,768... | collective-permute-start | bytes 110600 | tf_op jit(solution)/shard_map/ppermute | solution.py:321
  2.7 7.4 %collective-permute-start = (bf16[3,16,384]{2,1,0:T(8,128)(2,1)S(1)}, bf16[3,16,384]{2,1,0:T(8,128)(2,1)S(1)}, u32[]{:S(2)}, u32[]{:S(2)}) collective-permute-start(bf16[3,16,384]{2,1,0:T(8,128)(2,1)S(1)} %get-tuple-element.48), channel_id=1, source_target_pairs={{0,128},{128,256},{256,384},{384,512},{512,640},{640,768},{768,896... | collective-permute-start | bytes 110600 | tf_op jit(solution)/shard_map/ppermute | solution.py:320
  10.2 6.3 %collective-permute-start.2 = (bf16[14,3,384]{2,1,0:T(4,128)(2,1)S(1)}, bf16[14,3,384]{2,1,0:T(4,128)(2,1)S(1)}, u32[]{:S(2)}, u32[]{:S(2)}) collective-permute-start(bf16[14,3,384]{2,1,0:T(4,128)(2,1)S(1)} %pad_maximum_fusion), channel_id=1, source_target_pairs={{0,16},{16,32},{32,48},{48,64},{64,80},{80,96},{96,112},{1,17},{17... | collective-permute-start | bytes 96776 | tf_op jit(solution)/shard_map/ppermute | solution.py:330
  13.4 4.8 %collective-permute-start.3 = (bf16[14,3,384]{2,1,0:T(4,128)(2,1)S(1)}, bf16[14,3,384]{2,1,0:T(4,128)(2,1)S(1)}, u32[]{:S(2)}, u32[]{:S(2)}) collective-permute-start(bf16[14,3,384]{2,1,0:T(4,128)(2,1)S(1)} %pad_maximum_fusion.1), channel_id=1, source_target_pairs={{16,0},{32,16},{48,32},{64,48},{80,64},{96,80},{112,96},{17,1},{33... | collective-permute-start | bytes 96776 | tf_op jit(solution)/shard_map/ppermute | solution.py:331
  24.5 16.9 %collective-permute-start.8 = (bf16[8,600,128]{2,1,0:T(8,128)(2,1)}, bf16[8,600,128]{2,1,0:T(8,128)(2,1)S(1)}, u32[]{:S(2)}, u32[]{:S(2)}) collective-permute-start(bf16[8,600,128]{2,1,0:T(8,128)(2,1)} %get-tuple-element.34), channel_id=1, source_target_pairs={{0,1},{1,0},{2,3},{3,2},{4,5},{5,4},{6,7},{7,6},{8,9},{9,8},{10,11... | collective-permute-start | bytes 3686408 | tf_op jit(solution)/shard_map/ppermute | solution.py:418
  43.1 22.5 %all-to-all-start = ((bf16[8,600,128]{2,1,0:T(8,128)(2,1)}), bf16[8,600,128]{2,1,0:T(8,128)(2,1)S(1)}, u32[]{:S(2)}, u32[]{:S(2)}) async-start(bf16[8,600,128]{2,1,0:T(8,128)(2,1)} %join.1), calls=%async_computation | async-start | bytes 2457600 | tf_op jit(solution)/shard_map/all_to_all | solution.py:447
  46.7 7.9 %collective-permute-start.5 = (bf16[3,16,384]{2,1,0:T(8,128)(2,1)S(1)}, bf16[3,16,384]{2,1,0:T(8,128)(2,1)S(1)}, u32[]{:S(2)}, u32[]{:S(2)}) collective-permute-start(bf16[3,16,384]{2,1,0:T(8,128)(2,1)S(1)} %get-tuple-element.43), channel_id=1, source_target_pairs={{128,0},{256,128},{384,256},{512,384},{640,512},{768,640},{896,768... | collective-permute-start | bytes 110600 | tf_op jit(solution)/shard_map/ppermute | solution.py:321
  48.0 7.6 %collective-permute-start.4 = (bf16[3,16,384]{2,1,0:T(8,128)(2,1)S(1)}, bf16[3,16,384]{2,1,0:T(8,128)(2,1)S(1)}, u32[]{:S(2)}, u32[]{:S(2)}) collective-permute-start(bf16[3,16,384]{2,1,0:T(8,128)(2,1)S(1)} %get-tuple-element.44), channel_id=1, source_target_pairs={{0,128},{128,256},{256,384},{384,512},{512,640},{640,768},{768,896... | collective-permute-start | bytes 110600 | tf_op jit(solution)/shard_map/ppermute | solution.py:320
  66.7 36.0 %all-to-all-start.1 = ((bf16[64,24,128]{2,1,0:T(8,128)(2,1)}), bf16[64,24,128]{2,1,0:T(8,128)(2,1)S(1)}, u32[]{:S(2)}, u32[]{:S(2)}) async-start(bf16[64,24,128]{2,1,0:T(8,128)(2,1)} %block_sum.1), calls=%async_computation.1 | async-start | bytes 786432 | tf_op jit(solution)/shard_map/all_to_all | solution.py:466
  83.5 5.8 %collective-permute-start.6 = (bf16[14,3,384]{2,1,0:T(4,128)(2,1)S(1)}, bf16[14,3,384]{2,1,0:T(4,128)(2,1)S(1)}, u32[]{:S(2)}, u32[]{:S(2)}) collective-permute-start(bf16[14,3,384]{2,1,0:T(4,128)(2,1)S(1)} %pad_maximum_fusion.2), channel_id=1, source_target_pairs={{0,16},{16,32},{32,48},{48,64},{64,80},{80,96},{96,112},{1,17},{17... | collective-permute-start | bytes 96776 | tf_op jit(solution)/shard_map/ppermute | solution.py:330
  85.6 6.2 %collective-permute-start.7 = (bf16[14,3,384]{2,1,0:T(4,128)(2,1)S(1)}, bf16[14,3,384]{2,1,0:T(4,128)(2,1)S(1)}, u32[]{:S(2)}, u32[]{:S(2)}) collective-permute-start(bf16[14,3,384]{2,1,0:T(4,128)(2,1)S(1)} %pad_maximum_fusion.3), channel_id=1, source_target_pairs={{16,0},{32,16},{48,32},{64,48},{80,64},{96,80},{112,96},{17,1},{33... | collective-permute-start | bytes 96776 | tf_op jit(solution)/shard_map/ppermute | solution.py:331
  103.5 12.1 %all-to-all-start.2 = ((f32[16,12,128]{2,1,0:T(8,128)}), f32[16,12,128]{2,1,0:T(8,128)S(1)}, u32[]{:S(2)}, u32[]{:S(2)}) async-start(f32[16,12,128]{2,1,0:T(8,128)} %get-tuple-element.37), calls=%async_computation.2 | async-start | bytes 262144 | tf_op jit(solution)/shard_map/all_to_all | solution.py:479

commit v6 on v5

--- a/solution.py
+++ b/solution.py
@@ -27,7 +27,7 @@
 ROWS = BIG + 2 * SHARE
 TALL = ("zh", "zl")
 WIDE = ("xh", "xl")
-LIMIT = pltpu.CompilerParams(vmem_limit_bytes=50 * 1024 * 1024)
+LIMIT = pltpu.CompilerParams(vmem_limit_bytes=30 * 1024 * 1024)
 
 
 def matmul(a, b, ca, cb):
@@ -233,13 +233,20 @@
     products(core_ref[0], both_ref, stack_ref[...], out_ref, out_hbm, sems)
 
 
-def join_kernel(mine_ref, got_ref, out_ref):
-    big = mine_ref[:, 0:BIG, :].astype(F32) + got_ref[:, 0:BIG, :].astype(F32)
-    out_ref[:, 0:BIG, :] = big.astype(BF16)
+def join_kernel(mine_ref, got_ref, out_hbm, out_ref, sems):
     both = mine_ref[:, BIG:ROWS, :].astype(F32) + got_ref[:, BIG:ROWS, :].astype(F32)
     value = both[:, 0:SHARE] + both[:, SHARE : 2 * SHARE]
     low = value - value.astype(BF16).astype(F32)
     out_ref[:, BIG:ROWS, :] = jnp.concatenate([value, low], axis=1).astype(BF16)
+    copies = []
+    for k in range(PIECES):
+        big = mine_ref[k, 0:BIG, :].astype(F32) + got_ref[k, 0:BIG, :].astype(F32)
+        out_ref[k, 0:BIG, :] = big.astype(BF16)
+        c = pltpu.make_async_copy(out_ref.at[k], out_hbm.at[k], sems.at[k])
+        c.start()
+        copies.append(c)
+    for c in copies:
+        c.wait()
 
 
 def block_sum_kernel(yl_ref, got_ref, top_any, bot_any, out_ref, total):
@@ -351,7 +358,6 @@
     core = lax.axis_index("core").astype(jnp.int32)
     yl = lax.axis_index("yl").astype(jnp.int32)
     top, bot = shifted(x, TALL, 0)
-    left, right = column_halo(x, top, bot)
 
     whole = lambda n: [pl.BlockSpec(memory_space=pltpu.VMEM)] * n
     away = lambda v: pltpu.with_memory_space_constraint(v, pltpu.HBM)
@@ -366,6 +372,7 @@
         compiler_params=LIMIT,
         name="fetch",
     )(*[away(v) for v in fetched])
+    left, right = column_halo(x_near, top, bot)
     smem = [pl.BlockSpec(memory_space=pltpu.SMEM)]
     pixels = height * width
     block_out, gconv, send, both, stack, own = pl.pallas_call(
@@ -432,15 +439,16 @@
     gtop, gbot = shifted(edges, TALL, 0)
     gleft, gright = column_halo(edges, gtop, gbot)
 
-    step = 2
-    spec = pl.BlockSpec((step, ROWS, LANES), lambda i: (i, 0, 0))
     free = lambda n: [pl.BlockSpec(memory_space=pl.ANY)] * n
     joined = pl.pallas_call(
         join_kernel,
         out_shape=jax.ShapeDtypeStruct((PIECES, ROWS, LANES), BF16),
-        grid=(PIECES // step,),
-        in_specs=[spec, spec],
-        out_specs=spec,
+        in_specs=whole(2),
+        out_specs=hbm(1)[0],
+        scratch_shapes=[
+            pltpu.VMEM((PIECES, ROWS, LANES), BF16),
+            pltpu.SemaphoreType.DMA((PIECES,)),
+        ],
         compiler_params=LIMIT,
         name="join",
     )(mine, got)

time: 117 us -> 116 us (level)
  waiting for transfers between devices: 35.3 us -> 37.2 us
  starting transfers between devices: 62.2 us -> 60.7 us
    ppermute x2, waiting for transfers between devices: 4.05 us -> 6.14 us  [column_halo(): right = lax.ppermute(head, WIDE, [(i + 1, i) for i in range(count - 1)])]
  transfers between devices with their start and end apart: 12 -> 12, of which waited for: 10 -> 9; matrix products, arithmetic and copies ran while one was open for 1% -> 0% of each run, Pallas kernels for 5% -> 5%
where the time goes in v6:
time: 116 us; the launch traced here: 115 us
  starting transfers between devices  60.7 us (52%)
  waiting for transfers between devices  37.2 us (32%)
  Pallas kernels  15.4 us (13%)
    all_to_all x1, starting transfers between devices, per_device(): by_block = lax.all_to_all(by_block, ('zh', 'xh', 'yh'), 0, 0, tiled=True)  16 us
    ppermute x1, starting transfers between devices, per_device(): got = lax.ppermute(send, 'core', [(0, 1), (1, 0)])  13.6 us
    all_to_all x1, waiting for transfers between devices, per_device(): by_block = lax.all_to_all(by_block, ('zh', 'xh', 'yh'), 0, 0, tiled=True)  10.6 us
    ppermute x2, starting transfers between devices, shifted(): before = lax.ppermute(tail, axis, [(i, i + 1) for i in range(count - 1)])  10.6 us
    all_to_all x1, waiting for transfers between devices, per_device(): near = lax.all_to_all(joined, ('zl', 'xl', 'yl'), 0, 0, tiled=True)  10.2 us
    all_to_all x1, starting transfers between devices, per_device(): small = lax.all_to_all(small, ('zl', 'xl', 'yl', 'core'), 0, 0, tiled=True)  6.71 us
    pallas_call x1, Pallas kernels, per_device(): pl.pallas_call(front_kernel, out_shape=(jax.ShapeDtypeStruct((height, wid...  6.31 us
    ppermute x2, waiting for transfers between devices, column_halo(): right = lax.ppermute(head, WIDE, [(i + 1, i) for i in range(count - 1)])  6.14 us
  transfers between devices with their start and end apart: 12, of which 9 were waited for; matrix products, arithmetic and copies ran while one was open for 0% of the time, Pallas kernels for 5%

profile of v6, /device:TPU:1, one launch (start us, length us, event | category | flops | bytes accessed | tf_op | source)
XLA Modules:
  0.0 115.3 jit_solution(17699362540857702407)
XLA Ops:
  0.6 0.8 slice_bitcast_fusion
  1.4 1.3 %collective-permute-start.1 = (bf16[3,16,384]{2,1,0:T(8,128)(2,1)S(1)}, bf16[3,16,384]{2,1,0:T(8,128)(2,1)S(1)}, u32[]{:S(2)}, u32[]{:S(2)}) collective-permute-start(bf16[3,16,384]{2,1,0:T(8,128)(2,1)S(1)} %get-tuple-element.47), channel_id=1, source_target_pairs={{128,0},{256,128},{384,256},{512,384},{640,512},{768,640},{896,768... | collective-permute-start | bytes 110600 | tf_op jit(solution)/shard_map/ppermute | solution.py:328
  2.7 6.4 %collective-permute-start = (bf16[3,16,384]{2,1,0:T(8,128)(2,1)S(1)}, bf16[3,16,384]{2,1,0:T(8,128)(2,1)S(1)}, u32[]{:S(2)}, u32[]{:S(2)}) collective-permute-start(bf16[3,16,384]{2,1,0:T(8,128)(2,1)S(1)} %get-tuple-element.48), channel_id=1, source_target_pairs={{0,128},{128,256},{256,384},{384,512},{512,640},{640,768},{768,896... | collective-permute-start | bytes 110600 | tf_op jit(solution)/shard_map/ppermute | solution.py:327
  9.1 1.8 %fetch.1 = (bf16[8,16,384]{2,1,0:T(8,128)(2,1)S(1)}, bf16[8,16,384]{2,1,0:T(8,128)(2,1)S(1)}, f32[7,7,384]{2,1,0:T(8,128)S(1)}, bf16[384,1536]{1,0:T(8,128)(2,1)S(1)}, bf16[1536,384]{1,0:T(8,128)(2,1)S(1)}) custom-call(bf16[8,16,384]{2,1,0:T(8,128)(2,1)} %bitcast.10, bf16[8,16,384]{2,1,0:T(8,128)(2,1)} %bitcast.11, f32[7,7,384]{2,1,0:T(8,128)} %refs_2_.1, ...), custom_call_target="tpu_custom_call" | custom-call | tf_op jit(solution)/shard_map/fetch/pallas_call | solution.py:366
  11.0 0.0 collective-permute-done.1.bot_ref
  11.0 0.0 collective-permute-done.top_ref
  11.1 3.1 %collective-permute-start.2 = (bf16[14,3,384]{2,1,0:T(4,128)(2,1)S(1)}, bf16[14,3,384]{2,1,0:T(4,128)(2,1)S(1)}, u32[]{:S(2)}, u32[]{:S(2)}) collective-permute-start(bf16[14,3,384]{2,1,0:T(4,128)(2,1)S(1)} %pad_maximum_fusion), channel_id=1, source_target_pairs={{0,16},{16,32},{32,48},{48,64},{64,80},{80,96},{96,112},{1,17},{17... | collective-permute-start | bytes 96776 | tf_op jit(solution)/shard_map/ppermute | solution.py:337
  14.2 1.3 %collective-permute-start.3 = (bf16[14,3,384]{2,1,0:T(4,128)(2,1)S(1)}, bf16[14,3,384]{2,1,0:T(4,128)(2,1)S(1)}, u32[]{:S(2)}, u32[]{:S(2)}) collective-permute-start(bf16[14,3,384]{2,1,0:T(4,128)(2,1)S(1)} %pad_maximum_fusion.1), channel_id=1, source_target_pairs={{16,0},{32,16},{48,32},{64,48},{80,64},{96,80},{112,96},{17,1},{33... | collective-permute-start | bytes 96776 | tf_op jit(solution)/shard_map/ppermute | solution.py:338
  15.5 0.0 collective-permute-done.2.left_ref
  15.6 3.5 %collective-permute-done.3.right_ref = bf16[14,3,384]{2,1,0:T(4,128)(2,1)S(1)} collective-permute-done((bf16[14,3,384]{2,1,0:T(4,128)(2,1)S(1)}, bf16[14,3,384]{2,1,0:T(4,128)(2,1)S(1)}, u32[]{:S(2)}, u32[]{:S(2)}) %collective-permute-start.3) | collective-permute-done | bytes 32288 | tf_op jit(solution)/shard_map/ppermute | solution.py:338
  19.0 6.3 %front.1 = (bf16[8,16,384]{2,1,0:T(8,128)(2,1)}, f32[8,16,384]{2,1,0:T(8,128)S(1)}, bf16[8,600,128]{2,1,0:T(8,128)(2,1)S(1)}, bf16[256,1536]{1,0:T(8,128)(2,1)S(...) custom-call(s32[1]{0:T(128)} %bitcast.core_ref, bf16[8,16,384]{2,1,0:T(8,128)(2,1)S(1)} %get-tuple-element.24.x_ref, ...), custom_call_target="tpu_custom_call" | custom-call | tf_op jit(solution)/shard_map/front/pallas_call | solution.py:378
  25.3 13.6 %collective-permute-start.8 = (bf16[8,600,128]{2,1,0:T(8,128)(2,1)S(1)}, bf16[8,600,128]{2,1,0:T(8,128)(2,1)S(1)}, u32[]{:S(2)}, u32[]{:S(2)}) collective-permute-start(bf16[8,600,128]{2,1,0:T(8,128)(2,1)S(1)} %get-tuple-element.34), channel_id=1, source_target_pairs={{0,1},{1,0},{2,3},{3,2},{4,5},{5,4},{6,7},{7,6},{8,9},{9,8},{10,11... | collective-permute-start | bytes 3686408 | tf_op jit(solution)/shard_map/ppermute | solution.py:425
  38.9 1.3 %own.1.mine_ref = bf16[8,600,128]{2,1,0:T(8,128)(2,1)S(1)} custom-call(s32[1]{0:T(128)} %bitcast.core_ref, bf16[256,1536]{1,0:T(8,128)(2,1)S(1)} %get-tuple-element.31.both_ref, bf16[256,384]{1,0:T(8,128)(2,1)S(1)} %get-tuple-element.32.stack_ref, f32[8,24,128]{2,1,0:T(8,128)S(1)} %get-tuple-element.33.small_ref), custom_call_target="tpu_custom_call" | custom-call | tf_op jit(solution)/shard_map/own/pallas_call | solution.py:426
  40.3 1.2 %collective-permute-done.8.got_ref = bf16[8,600,128]{2,1,0:T(8,128)(2,1)S(1)} collective-permute-done((bf16[8,600,128]{2,1,0:T(8,128)(2,1)S(1)}, bf16[8,600,128]{2,1,0:T(8,128)(2,1)S(1)}, u32[]{:S(2)}, u32[]{:S(2)}) %collective-permute-start.8) | collective-permute-done | bytes 1228832 | tf_op jit(solution)/shard_map/ppermute | solution.py:425
  41.4 1.2 %join.1 = bf16[8,600,128]{2,1,0:T(8,128)(2,1)} custom-call(bf16[8,600,128]{2,1,0:T(8,128)(2,1)S(1)} %own.1.mine_ref, bf16[8,600,128]{2,1,0:T(8,128)(2,1)S(1)} %collective-permute-done.8.got_ref), custom_call_target="tpu_custom_call" | custom-call | tf_op jit(solution)/shard_map/join/pallas_call | solution.py:443
  42.6 3.6 %all-to-all-start = ((bf16[8,600,128]{2,1,0:T(8,128)(2,1)}), bf16[8,600,128]{2,1,0:T(8,128)(2,1)S(1)}, u32[]{:S(2)}, u32[]{:S(2)}) async-start(bf16[8,600,128]{2,1,0:T(8,128)(2,1)} %join.1), calls=%async_computation | async-start | bytes 2457600 | tf_op jit(solution)/shard_map/all_to_all | solution.py:455
  46.2 1.3 %collective-permute-start.5 = (bf16[3,16,384]{2,1,0:T(8,128)(2,1)S(1)}, bf16[3,16,384]{2,1,0:T(8,128)(2,1)S(1)}, u32[]{:S(2)}, u32[]{:S(2)}) collective-permute-start(bf16[3,16,384]{2,1,0:T(8,128)(2,1)S(1)} %get-tuple-element.43), channel_id=1, source_target_pairs={{128,0},{256,128},{384,256},{512,384},{640,512},{768,640},{896,768... | collective-permute-start | bytes 110600 | tf_op jit(solution)/shard_map/ppermute | solution.py:328
  47.5 4.2 %collective-permute-start.4 = (bf16[3,16,384]{2,1,0:T(8,128)(2,1)S(1)}, bf16[3,16,384]{2,1,0:T(8,128)(2,1)S(1)}, u32[]{:S(2)}, u32[]{:S(2)}) collective-permute-start(bf16[3,16,384]{2,1,0:T(8,128)(2,1)S(1)} %get-tuple-element.44), channel_id=1, source_target_pairs={{0,128},{128,256},{256,384},{384,512},{512,640},{640,768},{768,896... | collective-permute-start | bytes 110600 | tf_op jit(solution)/shard_map/ppermute | solution.py:327
  51.8 1.7 %collective-permute-done.5.bot_ref.bot_any = bf16[3,16,384]{2,1,0:T(8,128)(2,1)S(1)} collective-permute-done((bf16[3,16,384]{2,1,0:T(8,128)(2,1)S(1)}, bf16[3,16,384]{2,1,0:T(8,128)(2,1)S(1)}, u32[]{:S(2)}, u32[]{:S(2)}) %collective-permute-start.5) | collective-permute-done | bytes 36896 | tf_op jit(solution)/shard_map/ppermute | solution.py:328
  53.4 1.7 %collective-permute-done.4.top_ref.top_any = bf16[3,16,384]{2,1,0:T(8,128)(2,1)S(1)} collective-permute-done((bf16[3,16,384]{2,1,0:T(8,128)(2,1)S(1)}, bf16[3,16,384]{2,1,0:T(8,128)(2,1)S(1)}, u32[]{:S(2)}, u32[]{:S(2)}) %collective-permute-start.4) | collective-permute-done | bytes 36896 | tf_op jit(solution)/shard_map/ppermute | solution.py:327
  55.1 10.2 %all-to-all-done.got_ref = bf16[8,600,128]{2,1,0:T(8,128)(2,1)S(1)} async-done(((bf16[8,600,128]{2,1,0:T(8,128)(2,1)}), bf16[8,600,128]{2,1,0:T(8,128)(2,1)S(1)}, u32[]{:S(2)}, u32[]{:S(2)}) %all-to-all-start) | async-done | bytes 1228832 | tf_op jit(solution)/shard_map/all_to_all | solution.py:455
  65.4 1.1 block_sum.1
  66.5 16.0 %all-to-all-start.1 = ((bf16[64,24,128]{2,1,0:T(8,128)(2,1)}), bf16[64,24,128]{2,1,0:T(8,128)(2,1)S(1)}, u32[]{:S(2)}, u32[]{:S(2)}) async-start(bf16[64,24,128]{2,1,0:T(8,128)(2,1)} %block_sum.1), calls=%async_computation.1 | async-start | bytes 786432 | tf_op jit(solution)/shard_map/all_to_all | solution.py:474
  82.6 2.0 %collective-permute-start.6 = (bf16[14,3,384]{2,1,0:T(4,128)(2,1)S(1)}, bf16[14,3,384]{2,1,0:T(4,128)(2,1)S(1)}, u32[]{:S(2)}, u32[]{:S(2)}) collective-permute-start(bf16[14,3,384]{2,1,0:T(4,128)(2,1)S(1)} %pad_maximum_fusion.2), channel_id=1, source_target_pairs={{0,16},{16,32},{32,48},{48,64},{64,80},{80,96},{96,112},{1,17},{17... | collective-permute-start | bytes 96776 | tf_op jit(solution)/shard_map/ppermute | solution.py:337
  84.6 1.3 %collective-permute-start.7 = (bf16[14,3,384]{2,1,0:T(4,128)(2,1)S(1)}, bf16[14,3,384]{2,1,0:T(4,128)(2,1)S(1)}, u32[]{:S(2)}, u32[]{:S(2)}) collective-permute-start(bf16[14,3,384]{2,1,0:T(4,128)(2,1)S(1)} %pad_maximum_fusion.3), channel_id=1, source_target_pairs={{16,0},{32,16},{48,32},{64,48},{80,64},{96,80},{112,96},{17,1},{33... | collective-permute-start | bytes 96776 | tf_op jit(solution)/shard_map/ppermute | solution.py:338
  85.9 2.4 %collective-permute-done.6.left_ref.left_any = bf16[14,3,384]{2,1,0:T(4,128)(2,1)S(1)} collective-permute-done((bf16[14,3,384]{2,1,0:T(4,128)(2,1)S(1)}, bf16[14,3,384]{2,1,0:T(4,128)(2,1)S(1)}, u32[]{:S(2)}, u32[]{:S(2)}) %collective-permute-start.6) | collective-permute-done | bytes 32288 | tf_op jit(solution)/shard_map/ppermute | solution.py:337
  88.3 2.7 %collective-permute-done.7.right_ref.right_any = bf16[14,3,384]{2,1,0:T(4,128)(2,1)S(1)} collective-permute-done((bf16[14,3,384]{2,1,0:T(4,128)(2,1)S(1)}, bf16[14,3,384]{2,1,0:T(4,128)(2,1)S(1)}, u32[]{:S(2)}, u32[]{:S(2)}) %collective-permute-start.7) | collective-permute-done | bytes 32288 | tf_op jit(solution)/shard_map/ppermute | solution.py:338
  91.0 10.6 %all-to-all-done.1.got_ref = bf16[64,24,128]{2,1,0:T(8,128)(2,1)S(1)} async-done(((bf16[64,24,128]{2,1,0:T(8,128)(2,1)}), bf16[64,24,128]{2,1,0:T(8,128)(2,1)S(1)}, u32[]{:S(2)}, u32[]{:S(2)}) %all-to-all-start.1) | async-done | bytes 393248 | tf_op jit(solution)/shard_map/all_to_all | solution.py:474
  101.6 0.8 far_sum.1
  102.4 6.7 %all-to-all-start.2 = ((f32[16,12,128]{2,1,0:T(8,128)}), f32[16,12,128]{2,1,0:T(8,128)S(1)}, u32[]{:S(2)}, u32[]{:S(2)}) async-start(f32[16,12,128]{2,1,0:T(8,128)} %get-tuple-element.37), calls=%async_computation.2 | async-start | bytes 262144 | tf_op jit(solution)/shard_map/all_to_all | solution.py:487
  109.1 2.1 %input_grad.1 = bf16[8,16,384]{2,1,0:T(8,128)(2,1)} custom-call(f32[8,16,384]{2,1,0:T(8,128)S(1)} %get-tuple-element.30.g_ref, bf16[3,16,384]{2,1,0:T(8,128)(2,1)S(1)} %collective-permute-done.4.top_ref.top_any, bf16[3,16,384]{2,1,0:T(8,128)(2,1)S(1)} %collective-permute-done.5.bot_ref.bot_any, ...), custom_call_target="tpu_custom_call" | custom-call | tf_op jit(solution)/shard_map/input_grad/pallas_call | solution.py:465
  111.2 3.3 %all-to-all-done.2.got_ref = f32[16,12,128]{2,1,0:T(8,128)S(1)} async-done(((f32[16,12,128]{2,1,0:T(8,128)}), f32[16,12,128]{2,1,0:T(8,128)S(1)}, u32[]{:S(2)}, u32[]{:S(2)}) %all-to-all-start.2) | async-done | bytes 98336 | tf_op jit(solution)/shard_map/all_to_all | solution.py:487
  114.6 0.7 spread.1
  (12 shorter events, 0.3 us)
Async XLA Ops:
  1.4 9.5 %collective-permute-start.1 = (bf16[3,16,384]{2,1,0:T(8,128)(2,1)S(1)}, bf16[3,16,384]{2,1,0:T(8,128)(2,1)S(1)}, u32[]{:S(2)}, u32[]{:S(2)}) collective-permute-start(bf16[3,16,384]{2,1,0:T(8,128)(2,1)S(1)} %get-tuple-element.47), channel_id=1, source_target_pairs={{128,0},{256,128},{384,256},{512,384},{640,512},{768,640},{896,768... | collective-permute-start | bytes 110600 | tf_op jit(solution)/shard_map/ppermute | solution.py:328
  2.7 8.3 %collective-permute-start = (bf16[3,16,384]{2,1,0:T(8,128)(2,1)S(1)}, bf16[3,16,384]{2,1,0:T(8,128)(2,1)S(1)}, u32[]{:S(2)}, u32[]{:S(2)}) collective-permute-start(bf16[3,16,384]{2,1,0:T(8,128)(2,1)S(1)} %get-tuple-element.48), channel_id=1, source_target_pairs={{0,128},{128,256},{256,384},{384,512},{512,640},{640,768},{768,896... | collective-permute-start | bytes 110600 | tf_op jit(solution)/shard_map/ppermute | solution.py:327
  11.1 4.5 %collective-permute-start.2 = (bf16[14,3,384]{2,1,0:T(4,128)(2,1)S(1)}, bf16[14,3,384]{2,1,0:T(4,128)(2,1)S(1)}, u32[]{:S(2)}, u32[]{:S(2)}) collective-permute-start(bf16[14,3,384]{2,1,0:T(4,128)(2,1)S(1)} %pad_maximum_fusion), channel_id=1, source_target_pairs={{0,16},{16,32},{32,48},{48,64},{64,80},{80,96},{96,112},{1,17},{17... | collective-permute-start | bytes 96776 | tf_op jit(solution)/shard_map/ppermute | solution.py:337
  14.2 4.8 %collective-permute-start.3 = (bf16[14,3,384]{2,1,0:T(4,128)(2,1)S(1)}, bf16[14,3,384]{2,1,0:T(4,128)(2,1)S(1)}, u32[]{:S(2)}, u32[]{:S(2)}) collective-permute-start(bf16[14,3,384]{2,1,0:T(4,128)(2,1)S(1)} %pad_maximum_fusion.1), channel_id=1, source_target_pairs={{16,0},{32,16},{48,32},{64,48},{80,64},{96,80},{112,96},{17,1},{33... | collective-permute-start | bytes 96776 | tf_op jit(solution)/shard_map/ppermute | solution.py:338
  25.3 16.1 %collective-permute-start.8 = (bf16[8,600,128]{2,1,0:T(8,128)(2,1)S(1)}, bf16[8,600,128]{2,1,0:T(8,128)(2,1)S(1)}, u32[]{:S(2)}, u32[]{:S(2)}) collective-permute-start(bf16[8,600,128]{2,1,0:T(8,128)(2,1)S(1)} %get-tuple-element.34), channel_id=1, source_target_pairs={{0,1},{1,0},{2,3},{3,2},{4,5},{5,4},{6,7},{7,6},{8,9},{9,8},{10,11... | collective-permute-start | bytes 3686408 | tf_op jit(solution)/shard_map/ppermute | solution.py:425
  42.6 22.7 %all-to-all-start = ((bf16[8,600,128]{2,1,0:T(8,128)(2,1)}), bf16[8,600,128]{2,1,0:T(8,128)(2,1)S(1)}, u32[]{:S(2)}, u32[]{:S(2)}) async-start(bf16[8,600,128]{2,1,0:T(8,128)(2,1)} %join.1), calls=%async_computation | async-start | bytes 2457600 | tf_op jit(solution)/shard_map/all_to_all | solution.py:455
  46.2 7.2 %collective-permute-start.5 = (bf16[3,16,384]{2,1,0:T(8,128)(2,1)S(1)}, bf16[3,16,384]{2,1,0:T(8,128)(2,1)S(1)}, u32[]{:S(2)}, u32[]{:S(2)}) collective-permute-start(bf16[3,16,384]{2,1,0:T(8,128)(2,1)S(1)} %get-tuple-element.43), channel_id=1, source_target_pairs={{128,0},{256,128},{384,256},{512,384},{640,512},{768,640},{896,768... | collective-permute-start | bytes 110600 | tf_op jit(solution)/shard_map/ppermute | solution.py:328
  47.5 7.6 %collective-permute-start.4 = (bf16[3,16,384]{2,1,0:T(8,128)(2,1)S(1)}, bf16[3,16,384]{2,1,0:T(8,128)(2,1)S(1)}, u32[]{:S(2)}, u32[]{:S(2)}) collective-permute-start(bf16[3,16,384]{2,1,0:T(8,128)(2,1)S(1)} %get-tuple-element.44), channel_id=1, source_target_pairs={{0,128},{128,256},{256,384},{384,512},{512,640},{640,768},{768,896... | collective-permute-start | bytes 110600 | tf_op jit(solution)/shard_map/ppermute | solution.py:327
  66.5 35.1 %all-to-all-start.1 = ((bf16[64,24,128]{2,1,0:T(8,128)(2,1)}), bf16[64,24,128]{2,1,0:T(8,128)(2,1)S(1)}, u32[]{:S(2)}, u32[]{:S(2)}) async-start(bf16[64,24,128]{2,1,0:T(8,128)(2,1)} %block_sum.1), calls=%async_computation.1 | async-start | bytes 786432 | tf_op jit(solution)/shard_map/all_to_all | solution.py:474
  82.6 5.7 %collective-permute-start.6 = (bf16[14,3,384]{2,1,0:T(4,128)(2,1)S(1)}, bf16[14,3,384]{2,1,0:T(4,128)(2,1)S(1)}, u32[]{:S(2)}, u32[]{:S(2)}) collective-permute-start(bf16[14,3,384]{2,1,0:T(4,128)(2,1)S(1)} %pad_maximum_fusion.2), channel_id=1, source_target_pairs={{0,16},{16,32},{32,48},{48,64},{64,80},{80,96},{96,112},{1,17},{17... | collective-permute-start | bytes 96776 | tf_op jit(solution)/shard_map/ppermute | solution.py:337
  84.6 6.4 %collective-permute-start.7 = (bf16[14,3,384]{2,1,0:T(4,128)(2,1)S(1)}, bf16[14,3,384]{2,1,0:T(4,128)(2,1)S(1)}, u32[]{:S(2)}, u32[]{:S(2)}) collective-permute-start(bf16[14,3,384]{2,1,0:T(4,128)(2,1)S(1)} %pad_maximum_fusion.3), channel_id=1, source_target_pairs={{16,0},{32,16},{48,32},{64,48},{80,64},{96,80},{112,96},{17,1},{33... | collective-permute-start | bytes 96776 | tf_op jit(solution)/shard_map/ppermute | solution.py:338
  102.4 12.2 %all-to-all-start.2 = ((f32[16,12,128]{2,1,0:T(8,128)}), f32[16,12,128]{2,1,0:T(8,128)S(1)}, u32[]{:S(2)}, u32[]{:S(2)}) async-start(f32[16,12,128]{2,1,0:T(8,128)} %get-tuple-element.37), calls=%async_computation.2 | async-start | bytes 262144 | tf_op jit(solution)/shard_map/all_to_all | solution.py:487

commit v7 on v6

--- a/solution.py
+++ b/solution.py
@@ -54,44 +54,29 @@
     right_ref,
     cot_ref,
     dwk_ref,
-    dwb_hbm,
-    gain_hbm,
-    lnb_hbm,
+    dwb_ref,
+    gain_ref,
+    lnb_ref,
     wexp_ref,
-    bexp_hbm,
+    bexp_ref,
     wred_ref,
-    bred_hbm,
-    ls_hbm,
+    bred_ref,
+    ls_ref,
     block_ref,
     gconv_ref,
     send_hbm,
     both,
     stack_ref,
     own_ref,
-    dwb_ref,
-    gain_ref,
-    lnb_ref,
-    bexp_ref,
-    bred_ref,
-    ls_ref,
     xp,
     conv,
     small,
     send_ref,
-    sems,
+    bias_ref,
     out_sems,
 ):
-    pairs = (
-        (dwb_hbm, dwb_ref),
-        (gain_hbm, gain_ref),
-        (lnb_hbm, lnb_ref),
-        (ls_hbm, ls_ref),
-        (bexp_hbm, bexp_ref),
-        (bred_hbm, bred_ref),
-    )
-    copies = [pltpu.make_async_copy(a, b, sems.at[k]) for k, (a, b) in enumerate(pairs)]
-    for c in copies:
-        c.start()
+    first = pltpu.make_async_copy(dwb_ref, bias_ref, out_sems.at[6])
+    first.start()
     height, width = x_ref.shape[0], x_ref.shape[1]
     pixels = height * width
     row = lambda ref: ref[...].reshape(1, -1)
@@ -114,9 +99,8 @@
             for i in range(7):
                 acc = acc + dwk_ref[i, j : j + 1, ln] * s[i : i + height]
         conv[:, ln] = acc.reshape(pixels, LANES)
-    for c in copies:
-        c.wait()
-    flat = conv[...] + row(dwb_ref)
+    first.wait()
+    flat = conv[...] + row(bias_ref)
     centered = flat - jnp.mean(flat, axis=-1, keepdims=True)
     inv = lax.rsqrt(jnp.mean(centered * centered, axis=-1, keepdims=True) + EPS)
     xhat = centered * inv
@@ -137,6 +121,9 @@
         total = jnp.sum(g_pre, axis=0, keepdims=True)
         for l in range(BLOCKS):
             put(54 + f, l, total[:, LANES * l : LANES * (l + 1)])
+    stack_ref[0:pixels, :] = normed
+    stack_ref[pixels : 2 * pixels, :] = g_branch
+    outputs = products(1 - core_ref[0], both, stack_ref[...], send_ref, send_hbm, out_sems)
     branch = matmul(both[pixels : 2 * pixels, :], wred_ref[...], 1, 0) + row(bred_ref)
     block = x_ref[...].astype(F32).reshape(pixels, D) + row(ls_ref) * branch
     block_ref[...] = block.astype(BF16).reshape(height, width, D)
@@ -163,12 +150,14 @@
                 put(7 * i + j, l, jnp.sum(part, axis=0, keepdims=True))
     value = small[:, 0:SHARE, :]
     small[:, SHARE : 2 * SHARE, :] = value - value.astype(BF16).astype(F32)
-    stack_ref[0:pixels, :] = normed
-    stack_ref[pixels : 2 * pixels, :] = g_branch
     core = core_ref[0]
     own_ref[...] = small[pl.ds(PIECES * core, PIECES)]
     send_ref[:, BIG:ROWS, :] = small[pl.ds(PIECES * (1 - core), PIECES)].astype(BF16)
-    products(1 - core, both, stack_ref[...], send_ref, send_hbm, out_sems)
+    rows = slice(BIG, ROWS)
+    c = pltpu.make_async_copy(send_ref.at[:, rows], send_hbm.at[:, rows], out_sems.at[6])
+    c.start()
+    for c in outputs + [c]:
+        c.wait()
 
 
 def products(core, both, stack, out, hbm, sems):
@@ -180,7 +169,6 @@
         c.start()
         copies.append(c)
 
-    flush(slice(BIG, ROWS))
     chan = lax.broadcasted_iota(jnp.int32, (D, D), 0)
     column = lax.broadcasted_iota(jnp.int32, (1, D), 1)
     half = (column >= D // 2).astype(jnp.int32)
@@ -224,13 +212,16 @@
         for l in range(BLOCKS):
             at = 8 * FROWS * l + 4 * FROWS * low
             flush(slice(at, at + 4 * FROWS))
-    for c in copies:
-        c.wait()
+    return copies
 
 
 def own_kernel(core_ref, both_ref, stack_ref, small_ref, out_hbm, out_ref, sems):
     out_ref[:, BIG:ROWS, :] = small_ref[...].astype(BF16)
-    products(core_ref[0], both_ref, stack_ref[...], out_ref, out_hbm, sems)
+    rows = slice(BIG, ROWS)
+    c = pltpu.make_async_copy(out_ref.at[:, rows], out_hbm.at[:, rows], sems.at[6])
+    c.start()
+    for c in products(core_ref[0], both_ref, stack_ref[...], out_ref, out_hbm, sems) + [c]:
+        c.wait()
 
 
 def join_kernel(mine_ref, got_ref, out_hbm, out_ref, sems):
@@ -362,13 +353,25 @@
     whole = lambda n: [pl.BlockSpec(memory_space=pltpu.VMEM)] * n
     away = lambda v: pltpu.with_memory_space_constraint(v, pltpu.HBM)
     hbm = lambda n: [pl.BlockSpec(memory_space=pltpu.HBM)] * n
-    fetched = (x, cot, dw_kernel, w_expand, w_reduce)
-    x_near, cot_near, dwk_near, wexp_near, wred_near = pl.pallas_call(
+    fetched = (
+        x,
+        cot,
+        dw_kernel,
+        w_expand,
+        w_reduce,
+        dw_bias,
+        layer_norm_gain,
+        layer_norm_bias,
+        b_expand,
+        b_reduce,
+        layer_scale,
+    )
+    x_near, cot_near, dwk_near, wexp_near, wred_near, dwb, gain, lnb, bexp, bred, ls = pl.pallas_call(
         fetch_kernel,
         out_shape=tuple(jax.ShapeDtypeStruct(v.shape, v.dtype) for v in fetched),
-        in_specs=hbm(5),
-        out_specs=tuple(whole(5)),
-        scratch_shapes=[pltpu.SemaphoreType.DMA((5,))],
+        in_specs=hbm(11),
+        out_specs=tuple(whole(11)),
+        scratch_shapes=[pltpu.SemaphoreType.DMA((11,))],
         compiler_params=LIMIT,
         name="fetch",
     )(*[away(v) for v in fetched])
@@ -385,20 +388,14 @@
             jax.ShapeDtypeStruct((2 * pixels, D), BF16),
             jax.ShapeDtypeStruct((PIECES, 2 * SHARE, LANES), F32),
         ),
-        in_specs=smem + whole(7) + hbm(3) + whole(1) + hbm(1) + whole(1) + hbm(2),
+        in_specs=smem + whole(15),
         out_specs=tuple(whole(2) + hbm(1) + whole(3)),
         scratch_shapes=[
-            pltpu.VMEM((D,), F32),
-            pltpu.VMEM((D,), F32),
-            pltpu.VMEM((D,), F32),
-            pltpu.VMEM((FF,), F32),
-            pltpu.VMEM((D,), F32),
-            pltpu.VMEM((D,), F32),
             pltpu.VMEM((height + 2 * HALO, width + 8, D), F32),
             pltpu.VMEM((pixels, D), F32),
             pltpu.VMEM((2 * PIECES, 2 * SHARE, LANES), F32),
             pltpu.VMEM((PIECES, ROWS, LANES), BF16),
-            pltpu.SemaphoreType.DMA((6,)),
+            pltpu.VMEM((D,), F32),
             pltpu.SemaphoreType.DMA((7,)),
         ],
         compiler_params=LIMIT,
@@ -412,14 +409,14 @@
         right,
         cot_near,
         dwk_near,
-        away(dw_bias),
-        away(layer_norm_gain),
-        away(layer_norm_bias),
+        dwb,
+        gain,
+        lnb,
         wexp_near,
-        away(b_expand),
+        bexp,
         wred_near,
-        away(b_reduce),
-        away(layer_scale),
+        bred,
+        ls,
     )
 
     got = lax.ppermute(send, "core", [(0, 1), (1, 0)])

time: 116 us -> 116 us (level)
  no operation moved by 1% of the time
where the time goes in v7:
time: 116 us; the launch traced here: 115 us
  starting transfers between devices  60.4 us (52%)
  waiting for transfers between devices  37.3 us (32%)
  Pallas kernels  15.4 us (13%)
    all_to_all x1, starting transfers between devices, per_device(): by_block = lax.all_to_all(by_block, ('zh', 'xh', 'yh'), 0, 0, tiled=True)  16 us
    ppermute x1, starting transfers between devices, per_device(): got = lax.ppermute(send, 'core', [(0, 1), (1, 0)])  13.6 us
    all_to_all x1, waiting for transfers between devices, per_device(): by_block = lax.all_to_all(by_block, ('zh', 'xh', 'yh'), 0, 0, tiled=True)  10.7 us
    ppermute x2, starting transfers between devices, shifted(): before = lax.ppermute(tail, axis, [(i, i + 1) for i in range(count - 1)])  10.5 us
    all_to_all x1, waiting for transfers between devices, per_device(): near = lax.all_to_all(joined, ('zl', 'xl', 'yl'), 0, 0, tiled=True)  10.2 us
    all_to_all x1, starting transfers between devices, per_device(): small = lax.all_to_all(small, ('zl', 'xl', 'yl', 'core'), 0, 0, tiled=True)  6.29 us
    pallas_call x1, Pallas kernels, per_device(): pl.pallas_call(front_kernel, out_shape=(jax.ShapeDtypeStruct((height, wid...  6.27 us
    ppermute x2, waiting for transfers between devices, column_halo(): right = lax.ppermute(head, WIDE, [(i + 1, i) for i in range(count - 1)])  6.11 us
  transfers between devices with their start and end apart: 12, of which 9 were waited for; matrix products, arithmetic and copies ran while one was open for 0% of the time, Pallas kernels for 5%

profile of v7, /device:TPU:1, one launch (start us, length us, event | category | flops | bytes accessed | tf_op | source)
XLA Modules:
  0.0 115.1 jit_solution(6881559995243934402)
XLA Ops:
  0.6 0.8 slice_bitcast_fusion
  1.4 1.3 %collective-permute-start.1 = (bf16[3,16,384]{2,1,0:T(8,128)(2,1)S(1)}, bf16[3,16,384]{2,1,0:T(8,128)(2,1)S(1)}, u32[]{:S(2)}, u32[]{:S(2)}) collective-permute-start(bf16[3,16,384]{2,1,0:T(8,128)(2,1)S(1)} %get-tuple-element.59), channel_id=1, source_target_pairs={{128,0},{256,128},{384,256},{512,384},{640,512},{768,640},{896,768... | collective-permute-start | bytes 110600 | tf_op jit(solution)/shard_map/ppermute | solution.py:319
  2.7 6.4 %collective-permute-start = (bf16[3,16,384]{2,1,0:T(8,128)(2,1)S(1)}, bf16[3,16,384]{2,1,0:T(8,128)(2,1)S(1)}, u32[]{:S(2)}, u32[]{:S(2)}) collective-permute-start(bf16[3,16,384]{2,1,0:T(8,128)(2,1)S(1)} %get-tuple-element.60), channel_id=1, source_target_pairs={{0,128},{128,256},{256,384},{384,512},{512,640},{640,768},{768,896... | collective-permute-start | bytes 110600 | tf_op jit(solution)/shard_map/ppermute | solution.py:318
  9.1 1.9 %fetch.1 = (bf16[8,16,384]{2,1,0:T(8,128)(2,1)S(1)}, bf16[8,16,384]{2,1,0:T(8,128)(2,1)S(1)}, f32[7,7,384]{2,1,0:T(8,128)S(1)}, bf16[384,1536]{1,0:T(8,128)(2,1)...) custom-call(bf16[8,16,384]{2,1,0:T(8,128)(2,1)} %bitcast.10, ...), custom_call_target="tpu_custom_call" | custom-call | tf_op jit(solution)/shard_map/fetch/pallas_call | solution.py:369
  11.0 0.0 collective-permute-done.1.bot_ref
  11.1 0.0 collective-permute-done.top_ref
  11.1 3.1 %collective-permute-start.2 = (bf16[14,3,384]{2,1,0:T(4,128)(2,1)S(1)}, bf16[14,3,384]{2,1,0:T(4,128)(2,1)S(1)}, u32[]{:S(2)}, u32[]{:S(2)}) collective-permute-start(bf16[14,3,384]{2,1,0:T(4,128)(2,1)S(1)} %pad_maximum_fusion), channel_id=1, source_target_pairs={{0,16},{16,32},{32,48},{48,64},{64,80},{80,96},{96,112},{1,17},{17... | collective-permute-start | bytes 96776 | tf_op jit(solution)/shard_map/ppermute | solution.py:328
  14.3 1.3 %collective-permute-start.3 = (bf16[14,3,384]{2,1,0:T(4,128)(2,1)S(1)}, bf16[14,3,384]{2,1,0:T(4,128)(2,1)S(1)}, u32[]{:S(2)}, u32[]{:S(2)}) collective-permute-start(bf16[14,3,384]{2,1,0:T(4,128)(2,1)S(1)} %pad_maximum_fusion.1), channel_id=1, source_target_pairs={{16,0},{32,16},{48,32},{64,48},{80,64},{96,80},{112,96},{17,1},{33... | collective-permute-start | bytes 96776 | tf_op jit(solution)/shard_map/ppermute | solution.py:329
  15.6 0.0 collective-permute-done.2.left_ref
  15.6 3.5 %collective-permute-done.3.right_ref = bf16[14,3,384]{2,1,0:T(4,128)(2,1)S(1)} collective-permute-done((bf16[14,3,384]{2,1,0:T(4,128)(2,1)S(1)}, bf16[14,3,384]{2,1,0:T(4,128)(2,1)S(1)}, u32[]{:S(2)}, u32[]{:S(2)}) %collective-permute-start.3) | collective-permute-done | bytes 32288 | tf_op jit(solution)/shard_map/ppermute | solution.py:329
  19.1 6.3 %front.1 = (bf16[8,16,384]{2,1,0:T(8,128)(2,1)}, f32[8,16,384]{2,1,0:T(8,128)S(1)}, bf16[8,600,128]{2,1,0:T(8,128)(2,1)S(1)}, bf16[256,1536]{1,0:T(8,128)(2,1)S(...) custom-call(s32[1]{0:T(128)} %bitcast.core_ref, bf16[8,16,384]{2,1,0:T(8,128)(2,1)S(1)} %get-tuple-element.30.x_ref, ...), custom_call_target="tpu_custom_call" | custom-call | tf_op jit(solution)/shard_map/front/pallas_call | solution.py:381
  25.4 13.6 %collective-permute-start.8 = (bf16[8,600,128]{2,1,0:T(8,128)(2,1)S(1)}, bf16[8,600,128]{2,1,0:T(8,128)(2,1)S(1)}, u32[]{:S(2)}, u32[]{:S(2)}) collective-permute-start(bf16[8,600,128]{2,1,0:T(8,128)(2,1)S(1)} %get-tuple-element.46), channel_id=1, source_target_pairs={{0,1},{1,0},{2,3},{3,2},{4,5},{5,4},{6,7},{7,6},{8,9},{9,8},{10,11... | collective-permute-start | bytes 3686408 | tf_op jit(solution)/shard_map/ppermute | solution.py:422
  38.9 1.3 %own.1.mine_ref = bf16[8,600,128]{2,1,0:T(8,128)(2,1)S(1)} custom-call(s32[1]{0:T(128)} %bitcast.core_ref, bf16[256,1536]{1,0:T(8,128)(2,1)S(1)} %get-tuple-element.43.both_ref, bf16[256,384]{1,0:T(8,128)(2,1)S(1)} %get-tuple-element.44.stack_ref, f32[8,24,128]{2,1,0:T(8,128)S(1)} %get-tuple-element.45.small_ref), custom_call_target="tpu_custom_call" | custom-call | tf_op jit(solution)/shard_map/own/pallas_call | solution.py:423
  40.3 1.2 %collective-permute-done.8.got_ref = bf16[8,600,128]{2,1,0:T(8,128)(2,1)S(1)} collective-permute-done((bf16[8,600,128]{2,1,0:T(8,128)(2,1)S(1)}, bf16[8,600,128]{2,1,0:T(8,128)(2,1)S(1)}, u32[]{:S(2)}, u32[]{:S(2)}) %collective-permute-start.8) | collective-permute-done | bytes 1228832 | tf_op jit(solution)/shard_map/ppermute | solution.py:422
  41.5 1.2 %join.1 = bf16[8,600,128]{2,1,0:T(8,128)(2,1)} custom-call(bf16[8,600,128]{2,1,0:T(8,128)(2,1)S(1)} %own.1.mine_ref, bf16[8,600,128]{2,1,0:T(8,128)(2,1)S(1)} %collective-permute-done.8.got_ref), custom_call_target="tpu_custom_call" | custom-call | tf_op jit(solution)/shard_map/join/pallas_call | solution.py:440
  42.7 3.6 %all-to-all-start = ((bf16[8,600,128]{2,1,0:T(8,128)(2,1)}), bf16[8,600,128]{2,1,0:T(8,128)(2,1)S(1)}, u32[]{:S(2)}, u32[]{:S(2)}) async-start(bf16[8,600,128]{2,1,0:T(8,128)(2,1)} %join.1), calls=%async_computation | async-start | bytes 2457600 | tf_op jit(solution)/shard_map/all_to_all | solution.py:452
  46.3 1.3 %collective-permute-start.5 = (bf16[3,16,384]{2,1,0:T(8,128)(2,1)S(1)}, bf16[3,16,384]{2,1,0:T(8,128)(2,1)S(1)}, u32[]{:S(2)}, u32[]{:S(2)}) collective-permute-start(bf16[3,16,384]{2,1,0:T(8,128)(2,1)S(1)} %get-tuple-element.55), channel_id=1, source_target_pairs={{128,0},{256,128},{384,256},{512,384},{640,512},{768,640},{896,768... | collective-permute-start | bytes 110600 | tf_op jit(solution)/shard_map/ppermute | solution.py:319
  47.6 4.2 %collective-permute-start.4 = (bf16[3,16,384]{2,1,0:T(8,128)(2,1)S(1)}, bf16[3,16,384]{2,1,0:T(8,128)(2,1)S(1)}, u32[]{:S(2)}, u32[]{:S(2)}) collective-permute-start(bf16[3,16,384]{2,1,0:T(8,128)(2,1)S(1)} %get-tuple-element.56), channel_id=1, source_target_pairs={{0,128},{128,256},{256,384},{384,512},{512,640},{640,768},{768,896... | collective-permute-start | bytes 110600 | tf_op jit(solution)/shard_map/ppermute | solution.py:318
  51.7 1.5 %collective-permute-done.5.bot_ref.bot_any = bf16[3,16,384]{2,1,0:T(8,128)(2,1)S(1)} collective-permute-done((bf16[3,16,384]{2,1,0:T(8,128)(2,1)S(1)}, bf16[3,16,384]{2,1,0:T(8,128)(2,1)S(1)}, u32[]{:S(2)}, u32[]{:S(2)}) %collective-permute-start.5) | collective-permute-done | bytes 36896 | tf_op jit(solution)/shard_map/ppermute | solution.py:319
  53.2 2.0 %collective-permute-done.4.top_ref.top_any = bf16[3,16,384]{2,1,0:T(8,128)(2,1)S(1)} collective-permute-done((bf16[3,16,384]{2,1,0:T(8,128)(2,1)S(1)}, bf16[3,16,384]{2,1,0:T(8,128)(2,1)S(1)}, u32[]{:S(2)}, u32[]{:S(2)}) %collective-permute-start.4) | collective-permute-done | bytes 36896 | tf_op jit(solution)/shard_map/ppermute | solution.py:318
  55.2 10.2 %all-to-all-done.got_ref = bf16[8,600,128]{2,1,0:T(8,128)(2,1)S(1)} async-done(((bf16[8,600,128]{2,1,0:T(8,128)(2,1)}), bf16[8,600,128]{2,1,0:T(8,128)(2,1)S(1)}, u32[]{:S(2)}, u32[]{:S(2)}) %all-to-all-start) | async-done | bytes 1228832 | tf_op jit(solution)/shard_map/all_to_all | solution.py:452
  65.4 1.1 block_sum.1
  66.5 16.0 %all-to-all-start.1 = ((bf16[64,24,128]{2,1,0:T(8,128)(2,1)}), bf16[64,24,128]{2,1,0:T(8,128)(2,1)S(1)}, u32[]{:S(2)}, u32[]{:S(2)}) async-start(bf16[64,24,128]{2,1,0:T(8,128)(2,1)} %block_sum.1), calls=%async_computation.1 | async-start | bytes 786432 | tf_op jit(solution)/shard_map/all_to_all | solution.py:471
  82.6 2.2 %collective-permute-start.6 = (bf16[14,3,384]{2,1,0:T(4,128)(2,1)S(1)}, bf16[14,3,384]{2,1,0:T(4,128)(2,1)S(1)}, u32[]{:S(2)}, u32[]{:S(2)}) collective-permute-start(bf16[14,3,384]{2,1,0:T(4,128)(2,1)S(1)} %pad_maximum_fusion.2), channel_id=1, source_target_pairs={{0,16},{16,32},{32,48},{48,64},{64,80},{80,96},{96,112},{1,17},{17... | collective-permute-start | bytes 96776 | tf_op jit(solution)/shard_map/ppermute | solution.py:328
  84.9 1.3 %collective-permute-start.7 = (bf16[14,3,384]{2,1,0:T(4,128)(2,1)S(1)}, bf16[14,3,384]{2,1,0:T(4,128)(2,1)S(1)}, u32[]{:S(2)}, u32[]{:S(2)}) collective-permute-start(bf16[14,3,384]{2,1,0:T(4,128)(2,1)S(1)} %pad_maximum_fusion.3), channel_id=1, source_target_pairs={{16,0},{32,16},{48,32},{64,48},{80,64},{96,80},{112,96},{17,1},{33... | collective-permute-start | bytes 96776 | tf_op jit(solution)/shard_map/ppermute | solution.py:329
  86.2 2.3 %collective-permute-done.6.left_ref.left_any = bf16[14,3,384]{2,1,0:T(4,128)(2,1)S(1)} collective-permute-done((bf16[14,3,384]{2,1,0:T(4,128)(2,1)S(1)}, bf16[14,3,384]{2,1,0:T(4,128)(2,1)S(1)}, u32[]{:S(2)}, u32[]{:S(2)}) %collective-permute-start.6) | collective-permute-done | bytes 32288 | tf_op jit(solution)/shard_map/ppermute | solution.py:328
  88.4 2.7 %collective-permute-done.7.right_ref.right_any = bf16[14,3,384]{2,1,0:T(4,128)(2,1)S(1)} collective-permute-done((bf16[14,3,384]{2,1,0:T(4,128)(2,1)S(1)}, bf16[14,3,384]{2,1,0:T(4,128)(2,1)S(1)}, u32[]{:S(2)}, u32[]{:S(2)}) %collective-permute-start.7) | collective-permute-done | bytes 32288 | tf_op jit(solution)/shard_map/ppermute | solution.py:329
  91.1 10.7 %all-to-all-done.1.got_ref = bf16[64,24,128]{2,1,0:T(8,128)(2,1)S(1)} async-done(((bf16[64,24,128]{2,1,0:T(8,128)(2,1)}), bf16[64,24,128]{2,1,0:T(8,128)(2,1)S(1)}, u32[]{:S(2)}, u32[]{:S(2)}) %all-to-all-start.1) | async-done | bytes 393248 | tf_op jit(solution)/shard_map/all_to_all | solution.py:471
  101.8 0.8 far_sum.1
  102.7 6.3 %all-to-all-start.2 = ((f32[16,12,128]{2,1,0:T(8,128)}), f32[16,12,128]{2,1,0:T(8,128)S(1)}, u32[]{:S(2)}, u32[]{:S(2)}) async-start(f32[16,12,128]{2,1,0:T(8,128)} %get-tuple-element.49), calls=%async_computation.2 | async-start | bytes 262144 | tf_op jit(solution)/shard_map/all_to_all | solution.py:484
  108.9 2.1 %input_grad.1 = bf16[8,16,384]{2,1,0:T(8,128)(2,1)} custom-call(f32[8,16,384]{2,1,0:T(8,128)S(1)} %get-tuple-element.42.g_ref, bf16[3,16,384]{2,1,0:T(8,128)(2,1)S(1)} %collective-permute-done.4.top_ref.top_any, bf16[3,16,384]{2,1,0:T(8,128)(2,1)S(1)} %collective-permute-done.5.bot_ref.bot_any, ...), custom_call_target="tpu_custom_call" | custom-call | tf_op jit(solution)/shard_map/input_grad/pallas_call | solution.py:462
  111.1 3.3 %all-to-all-done.2.got_ref = f32[16,12,128]{2,1,0:T(8,128)S(1)} async-done(((f32[16,12,128]{2,1,0:T(8,128)}), f32[16,12,128]{2,1,0:T(8,128)S(1)}, u32[]{:S(2)}, u32[]{:S(2)}) %all-to-all-start.2) | async-done | bytes 98336 | tf_op jit(solution)/shard_map/all_to_all | solution.py:484
  114.4 0.7 spread.1
  (12 shorter events, 0.3 us)
Async XLA Ops:
  1.4 9.6 %collective-permute-start.1 = (bf16[3,16,384]{2,1,0:T(8,128)(2,1)S(1)}, bf16[3,16,384]{2,1,0:T(8,128)(2,1)S(1)}, u32[]{:S(2)}, u32[]{:S(2)}) collective-permute-start(bf16[3,16,384]{2,1,0:T(8,128)(2,1)S(1)} %get-tuple-element.59), channel_id=1, source_target_pairs={{128,0},{256,128},{384,256},{512,384},{640,512},{768,640},{896,768... | collective-permute-start | bytes 110600 | tf_op jit(solution)/shard_map/ppermute | solution.py:319
  2.7 8.3 %collective-permute-start = (bf16[3,16,384]{2,1,0:T(8,128)(2,1)S(1)}, bf16[3,16,384]{2,1,0:T(8,128)(2,1)S(1)}, u32[]{:S(2)}, u32[]{:S(2)}) collective-permute-start(bf16[3,16,384]{2,1,0:T(8,128)(2,1)S(1)} %get-tuple-element.60), channel_id=1, source_target_pairs={{0,128},{128,256},{256,384},{384,512},{512,640},{640,768},{768,896... | collective-permute-start | bytes 110600 | tf_op jit(solution)/shard_map/ppermute | solution.py:318
  11.1 4.5 %collective-permute-start.2 = (bf16[14,3,384]{2,1,0:T(4,128)(2,1)S(1)}, bf16[14,3,384]{2,1,0:T(4,128)(2,1)S(1)}, u32[]{:S(2)}, u32[]{:S(2)}) collective-permute-start(bf16[14,3,384]{2,1,0:T(4,128)(2,1)S(1)} %pad_maximum_fusion), channel_id=1, source_target_pairs={{0,16},{16,32},{32,48},{48,64},{64,80},{80,96},{96,112},{1,17},{17... | collective-permute-start | bytes 96776 | tf_op jit(solution)/shard_map/ppermute | solution.py:328
  14.3 4.8 %collective-permute-start.3 = (bf16[14,3,384]{2,1,0:T(4,128)(2,1)S(1)}, bf16[14,3,384]{2,1,0:T(4,128)(2,1)S(1)}, u32[]{:S(2)}, u32[]{:S(2)}) collective-permute-start(bf16[14,3,384]{2,1,0:T(4,128)(2,1)S(1)} %pad_maximum_fusion.1), channel_id=1, source_target_pairs={{16,0},{32,16},{48,32},{64,48},{80,64},{96,80},{112,96},{17,1},{33... | collective-permute-start | bytes 96776 | tf_op jit(solution)/shard_map/ppermute | solution.py:329
  25.4 16.1 %collective-permute-start.8 = (bf16[8,600,128]{2,1,0:T(8,128)(2,1)S(1)}, bf16[8,600,128]{2,1,0:T(8,128)(2,1)S(1)}, u32[]{:S(2)}, u32[]{:S(2)}) collective-permute-start(bf16[8,600,128]{2,1,0:T(8,128)(2,1)S(1)} %get-tuple-element.46), channel_id=1, source_target_pairs={{0,1},{1,0},{2,3},{3,2},{4,5},{5,4},{6,7},{7,6},{8,9},{9,8},{10,11... | collective-permute-start | bytes 3686408 | tf_op jit(solution)/shard_map/ppermute | solution.py:422
  42.7 22.7 %all-to-all-start = ((bf16[8,600,128]{2,1,0:T(8,128)(2,1)}), bf16[8,600,128]{2,1,0:T(8,128)(2,1)S(1)}, u32[]{:S(2)}, u32[]{:S(2)}) async-start(bf16[8,600,128]{2,1,0:T(8,128)(2,1)} %join.1), calls=%async_computation | async-start | bytes 2457600 | tf_op jit(solution)/shard_map/all_to_all | solution.py:452
  46.3 6.9 %collective-permute-start.5 = (bf16[3,16,384]{2,1,0:T(8,128)(2,1)S(1)}, bf16[3,16,384]{2,1,0:T(8,128)(2,1)S(1)}, u32[]{:S(2)}, u32[]{:S(2)}) collective-permute-start(bf16[3,16,384]{2,1,0:T(8,128)(2,1)S(1)} %get-tuple-element.55), channel_id=1, source_target_pairs={{128,0},{256,128},{384,256},{512,384},{640,512},{768,640},{896,768... | collective-permute-start | bytes 110600 | tf_op jit(solution)/shard_map/ppermute | solution.py:319
  47.6 7.6 %collective-permute-start.4 = (bf16[3,16,384]{2,1,0:T(8,128)(2,1)S(1)}, bf16[3,16,384]{2,1,0:T(8,128)(2,1)S(1)}, u32[]{:S(2)}, u32[]{:S(2)}) collective-permute-start(bf16[3,16,384]{2,1,0:T(8,128)(2,1)S(1)} %get-tuple-element.56), channel_id=1, source_target_pairs={{0,128},{128,256},{256,384},{384,512},{512,640},{640,768},{768,896... | collective-permute-start | bytes 110600 | tf_op jit(solution)/shard_map/ppermute | solution.py:318
  66.5 35.4 %all-to-all-start.1 = ((bf16[64,24,128]{2,1,0:T(8,128)(2,1)}), bf16[64,24,128]{2,1,0:T(8,128)(2,1)S(1)}, u32[]{:S(2)}, u32[]{:S(2)}) async-start(bf16[64,24,128]{2,1,0:T(8,128)(2,1)} %block_sum.1), calls=%async_computation.1 | async-start | bytes 786432 | tf_op jit(solution)/shard_map/all_to_all | solution.py:471
  82.6 5.8 %collective-permute-start.6 = (bf16[14,3,384]{2,1,0:T(4,128)(2,1)S(1)}, bf16[14,3,384]{2,1,0:T(4,128)(2,1)S(1)}, u32[]{:S(2)}, u32[]{:S(2)}) collective-permute-start(bf16[14,3,384]{2,1,0:T(4,128)(2,1)S(1)} %pad_maximum_fusion.2), channel_id=1, source_target_pairs={{0,16},{16,32},{32,48},{48,64},{64,80},{80,96},{96,112},{1,17},{17... | collective-permute-start | bytes 96776 | tf_op jit(solution)/shard_map/ppermute | solution.py:328
  84.9 6.2 %collective-permute-start.7 = (bf16[14,3,384]{2,1,0:T(4,128)(2,1)S(1)}, bf16[14,3,384]{2,1,0:T(4,128)(2,1)S(1)}, u32[]{:S(2)}, u32[]{:S(2)}) collective-permute-start(bf16[14,3,384]{2,1,0:T(4,128)(2,1)S(1)} %pad_maximum_fusion.3), channel_id=1, source_target_pairs={{16,0},{32,16},{48,32},{64,48},{80,64},{96,80},{112,96},{17,1},{33... | collective-permute-start | bytes 96776 | tf_op jit(solution)/shard_map/ppermute | solution.py:329
  102.7 11.8 %all-to-all-start.2 = ((f32[16,12,128]{2,1,0:T(8,128)}), f32[16,12,128]{2,1,0:T(8,128)S(1)}, u32[]{:S(2)}, u32[]{:S(2)}) async-start(f32[16,12,128]{2,1,0:T(8,128)} %get-tuple-element.49), calls=%async_computation.2 | async-start | bytes 262144 | tf_op jit(solution)/shard_map/all_to_all | solution.py:484

commit v8 on v7

--- a/solution.py
+++ b/solution.py
@@ -240,7 +240,8 @@
         c.wait()
 
 
-def block_sum_kernel(yl_ref, got_ref, top_any, bot_any, out_ref, total):
+def block_sum_kernel(yl_ref, got_ref, top_any, bot_any, out_hbm, out_ref, total, sems):
+    copies = []
     total[...] = jnp.sum(got_ref[...].astype(F32), axis=0)
     small = total[BIG : BIG + SHARE, :] + total[BIG + SHARE : ROWS, :]
     side = LANES // 2
@@ -264,6 +265,13 @@
                     start = D // 2 * half + 2 * DROWS * yh
                     piece = jnp.concatenate([wide[:, start : start + 2 * DROWS], tail], axis=1)
                     out_ref[16 * zh + 4 * xh + yh] = piece.astype(BF16)
+        for k, zh in enumerate((low, low + 2)):
+            at = slice(16 * zh, 16 * (zh + 1))
+            c = pltpu.make_async_copy(out_ref.at[at], out_hbm.at[at], sems.at[2 * low + k])
+            c.start()
+            copies.append(c)
+    for c in copies:
+        c.wait()
 
 
 def far_sum_kernel(scale, got_ref, left_any, right_any, ge_ref, gr_ref, small_ref):
@@ -454,8 +462,12 @@
         block_sum_kernel,
         out_shape=jax.ShapeDtypeStruct((FAR, FROWS, LANES), BF16),
         in_specs=smem + whole(1) + free(2),
-        out_specs=whole(1)[0],
-        scratch_shapes=[pltpu.VMEM((ROWS, LANES), F32)],
+        out_specs=hbm(1)[0],
+        scratch_shapes=[
+            pltpu.VMEM((FAR, FROWS, LANES), BF16),
+            pltpu.VMEM((ROWS, LANES), F32),
+            pltpu.SemaphoreType.DMA((4,)),
+        ],
         compiler_params=LIMIT,
         name="block_sum",
     )(yl.reshape(1), near, gtop, gbot)

time: 116 us -> 116 us (level)
  no operation moved by 1% of the time
where the time goes in v8:
time: 116 us; the launch traced here: 115 us
  starting transfers between devices  60.4 us (52%)
  waiting for transfers between devices  37.3 us (32%)
  Pallas kernels  15.5 us (13%)
    all_to_all x1, starting transfers between devices, per_device(): by_block = lax.all_to_all(by_block, ('zh', 'xh', 'yh'), 0, 0, tiled=True)  16 us
    ppermute x1, starting transfers between devices, per_device(): got = lax.ppermute(send, 'core', [(0, 1), (1, 0)])  13.6 us
    all_to_all x1, waiting for transfers between devices, per_device(): by_block = lax.all_to_all(by_block, ('zh', 'xh', 'yh'), 0, 0, tiled=True)  10.7 us
    ppermute x2, starting transfers between devices, shifted(): before = lax.ppermute(tail, axis, [(i, i + 1) for i in range(count - 1)])  10.5 us
    all_to_all x1, waiting for transfers between devices, per_device(): near = lax.all_to_all(joined, ('zl', 'xl', 'yl'), 0, 0, tiled=True)  10.2 us
    all_to_all x1, starting transfers between devices, per_device(): small = lax.all_to_all(small, ('zl', 'xl', 'yl', 'core'), 0, 0, tiled=True)  6.29 us
    pallas_call x1, Pallas kernels, per_device(): pl.pallas_call(front_kernel, out_shape=(jax.ShapeDtypeStruct((height, wid...  6.27 us
    ppermute x2, waiting for transfers between devices, column_halo(): right = lax.ppermute(head, WIDE, [(i + 1, i) for i in range(count - 1)])  6.11 us
  transfers between devices with their start and end apart: 12, of which 9 were waited for; matrix products, arithmetic and copies ran while one was open for 0% of the time, Pallas kernels for 5%

profile of v8, /device:TPU:1, one launch (start us, length us, event | category | flops | bytes accessed | tf_op | source)
XLA Modules:
  0.0 115.2 jit_solution(6511781362407487625)
XLA Ops:
  0.6 0.8 slice_bitcast_fusion
  1.4 1.3 %collective-permute-start.1 = (bf16[3,16,384]{2,1,0:T(8,128)(2,1)S(1)}, bf16[3,16,384]{2,1,0:T(8,128)(2,1)S(1)}, u32[]{:S(2)}, u32[]{:S(2)}) collective-permute-start(bf16[3,16,384]{2,1,0:T(8,128)(2,1)S(1)} %get-tuple-element.59), channel_id=1, source_target_pairs={{128,0},{256,128},{384,256},{512,384},{640,512},{768,640},{896,768... | collective-permute-start | bytes 110600 | tf_op jit(solution)/shard_map/ppermute | solution.py:327
  2.7 6.4 %collective-permute-start = (bf16[3,16,384]{2,1,0:T(8,128)(2,1)S(1)}, bf16[3,16,384]{2,1,0:T(8,128)(2,1)S(1)}, u32[]{:S(2)}, u32[]{:S(2)}) collective-permute-start(bf16[3,16,384]{2,1,0:T(8,128)(2,1)S(1)} %get-tuple-element.60), channel_id=1, source_target_pairs={{0,128},{128,256},{256,384},{384,512},{512,640},{640,768},{768,896... | collective-permute-start | bytes 110600 | tf_op jit(solution)/shard_map/ppermute | solution.py:326
  9.1 1.9 %fetch.1 = (bf16[8,16,384]{2,1,0:T(8,128)(2,1)S(1)}, bf16[8,16,384]{2,1,0:T(8,128)(2,1)S(1)}, f32[7,7,384]{2,1,0:T(8,128)S(1)}, bf16[384,1536]{1,0:T(8,128)(2,1)...) custom-call(bf16[8,16,384]{2,1,0:T(8,128)(2,1)} %bitcast.10, ...), custom_call_target="tpu_custom_call" | custom-call | tf_op jit(solution)/shard_map/fetch/pallas_call | solution.py:377
  11.0 0.0 collective-permute-done.1.bot_ref
  11.1 0.0 collective-permute-done.top_ref
  11.1 3.1 %collective-permute-start.2 = (bf16[14,3,384]{2,1,0:T(4,128)(2,1)S(1)}, bf16[14,3,384]{2,1,0:T(4,128)(2,1)S(1)}, u32[]{:S(2)}, u32[]{:S(2)}) collective-permute-start(bf16[14,3,384]{2,1,0:T(4,128)(2,1)S(1)} %pad_maximum_fusion), channel_id=1, source_target_pairs={{0,16},{16,32},{32,48},{48,64},{64,80},{80,96},{96,112},{1,17},{17... | collective-permute-start | bytes 96776 | tf_op jit(solution)/shard_map/ppermute | solution.py:336
  14.3 1.3 %collective-permute-start.3 = (bf16[14,3,384]{2,1,0:T(4,128)(2,1)S(1)}, bf16[14,3,384]{2,1,0:T(4,128)(2,1)S(1)}, u32[]{:S(2)}, u32[]{:S(2)}) collective-permute-start(bf16[14,3,384]{2,1,0:T(4,128)(2,1)S(1)} %pad_maximum_fusion.1), channel_id=1, source_target_pairs={{16,0},{32,16},{48,32},{64,48},{80,64},{96,80},{112,96},{17,1},{33... | collective-permute-start | bytes 96776 | tf_op jit(solution)/shard_map/ppermute | solution.py:337
  15.6 0.0 collective-permute-done.2.left_ref
  15.6 3.5 %collective-permute-done.3.right_ref = bf16[14,3,384]{2,1,0:T(4,128)(2,1)S(1)} collective-permute-done((bf16[14,3,384]{2,1,0:T(4,128)(2,1)S(1)}, bf16[14,3,384]{2,1,0:T(4,128)(2,1)S(1)}, u32[]{:S(2)}, u32[]{:S(2)}) %collective-permute-start.3) | collective-permute-done | bytes 32288 | tf_op jit(solution)/shard_map/ppermute | solution.py:337
  19.1 6.3 %front.1 = (bf16[8,16,384]{2,1,0:T(8,128)(2,1)}, f32[8,16,384]{2,1,0:T(8,128)S(1)}, bf16[8,600,128]{2,1,0:T(8,128)(2,1)S(1)}, bf16[256,1536]{1,0:T(8,128)(2,1)S(...) custom-call(s32[1]{0:T(128)} %bitcast.core_ref, bf16[8,16,384]{2,1,0:T(8,128)(2,1)S(1)} %get-tuple-element.30.x_ref, ...), custom_call_target="tpu_custom_call" | custom-call | tf_op jit(solution)/shard_map/front/pallas_call | solution.py:389
  25.4 13.6 %collective-permute-start.8 = (bf16[8,600,128]{2,1,0:T(8,128)(2,1)S(1)}, bf16[8,600,128]{2,1,0:T(8,128)(2,1)S(1)}, u32[]{:S(2)}, u32[]{:S(2)}) collective-permute-start(bf16[8,600,128]{2,1,0:T(8,128)(2,1)S(1)} %get-tuple-element.46), channel_id=1, source_target_pairs={{0,1},{1,0},{2,3},{3,2},{4,5},{5,4},{6,7},{7,6},{8,9},{9,8},{10,11... | collective-permute-start | bytes 3686408 | tf_op jit(solution)/shard_map/ppermute | solution.py:430
  38.9 1.3 %own.1.mine_ref = bf16[8,600,128]{2,1,0:T(8,128)(2,1)S(1)} custom-call(s32[1]{0:T(128)} %bitcast.core_ref, bf16[256,1536]{1,0:T(8,128)(2,1)S(1)} %get-tuple-element.43.both_ref, bf16[256,384]{1,0:T(8,128)(2,1)S(1)} %get-tuple-element.44.stack_ref, f32[8,24,128]{2,1,0:T(8,128)S(1)} %get-tuple-element.45.small_ref), custom_call_target="tpu_custom_call" | custom-call | tf_op jit(solution)/shard_map/own/pallas_call | solution.py:431
  40.3 1.2 %collective-permute-done.8.got_ref = bf16[8,600,128]{2,1,0:T(8,128)(2,1)S(1)} collective-permute-done((bf16[8,600,128]{2,1,0:T(8,128)(2,1)S(1)}, bf16[8,600,128]{2,1,0:T(8,128)(2,1)S(1)}, u32[]{:S(2)}, u32[]{:S(2)}) %collective-permute-start.8) | collective-permute-done | bytes 1228832 | tf_op jit(solution)/shard_map/ppermute | solution.py:430
  41.5 1.2 %join.1 = bf16[8,600,128]{2,1,0:T(8,128)(2,1)} custom-call(bf16[8,600,128]{2,1,0:T(8,128)(2,1)S(1)} %own.1.mine_ref, bf16[8,600,128]{2,1,0:T(8,128)(2,1)S(1)} %collective-permute-done.8.got_ref), custom_call_target="tpu_custom_call" | custom-call | tf_op jit(solution)/shard_map/join/pallas_call | solution.py:448
  42.7 3.6 %all-to-all-start = ((bf16[8,600,128]{2,1,0:T(8,128)(2,1)}), bf16[8,600,128]{2,1,0:T(8,128)(2,1)S(1)}, u32[]{:S(2)}, u32[]{:S(2)}) async-start(bf16[8,600,128]{2,1,0:T(8,128)(2,1)} %join.1), calls=%async_computation | async-start | bytes 2457600 | tf_op jit(solution)/shard_map/all_to_all | solution.py:460
  46.3 1.3 %collective-permute-start.5 = (bf16[3,16,384]{2,1,0:T(8,128)(2,1)S(1)}, bf16[3,16,384]{2,1,0:T(8,128)(2,1)S(1)}, u32[]{:S(2)}, u32[]{:S(2)}) collective-permute-start(bf16[3,16,384]{2,1,0:T(8,128)(2,1)S(1)} %get-tuple-element.55), channel_id=1, source_target_pairs={{128,0},{256,128},{384,256},{512,384},{640,512},{768,640},{896,768... | collective-permute-start | bytes 110600 | tf_op jit(solution)/shard_map/ppermute | solution.py:327
  47.6 4.2 %collective-permute-start.4 = (bf16[3,16,384]{2,1,0:T(8,128)(2,1)S(1)}, bf16[3,16,384]{2,1,0:T(8,128)(2,1)S(1)}, u32[]{:S(2)}, u32[]{:S(2)}) collective-permute-start(bf16[3,16,384]{2,1,0:T(8,128)(2,1)S(1)} %get-tuple-element.56), channel_id=1, source_target_pairs={{0,128},{128,256},{256,384},{384,512},{512,640},{640,768},{768,896... | collective-permute-start | bytes 110600 | tf_op jit(solution)/shard_map/ppermute | solution.py:326
  51.7 1.5 %collective-permute-done.5.bot_ref.bot_any = bf16[3,16,384]{2,1,0:T(8,128)(2,1)S(1)} collective-permute-done((bf16[3,16,384]{2,1,0:T(8,128)(2,1)S(1)}, bf16[3,16,384]{2,1,0:T(8,128)(2,1)S(1)}, u32[]{:S(2)}, u32[]{:S(2)}) %collective-permute-start.5) | collective-permute-done | bytes 36896 | tf_op jit(solution)/shard_map/ppermute | solution.py:327
  53.2 2.0 %collective-permute-done.4.top_ref.top_any = bf16[3,16,384]{2,1,0:T(8,128)(2,1)S(1)} collective-permute-done((bf16[3,16,384]{2,1,0:T(8,128)(2,1)S(1)}, bf16[3,16,384]{2,1,0:T(8,128)(2,1)S(1)}, u32[]{:S(2)}, u32[]{:S(2)}) %collective-permute-start.4) | collective-permute-done | bytes 36896 | tf_op jit(solution)/shard_map/ppermute | solution.py:326
  55.2 10.2 %all-to-all-done.got_ref = bf16[8,600,128]{2,1,0:T(8,128)(2,1)S(1)} async-done(((bf16[8,600,128]{2,1,0:T(8,128)(2,1)}), bf16[8,600,128]{2,1,0:T(8,128)(2,1)S(1)}, u32[]{:S(2)}, u32[]{:S(2)}) %all-to-all-start) | async-done | bytes 1228832 | tf_op jit(solution)/shard_map/all_to_all | solution.py:460
  65.4 1.1 block_sum.1
  66.5 16.0 %all-to-all-start.1 = ((bf16[64,24,128]{2,1,0:T(8,128)(2,1)}), bf16[64,24,128]{2,1,0:T(8,128)(2,1)S(1)}, u32[]{:S(2)}, u32[]{:S(2)}) async-start(bf16[64,24,128]{2,1,0:T(8,128)(2,1)} %block_sum.1), calls=%async_computation.1 | async-start | bytes 786432 | tf_op jit(solution)/shard_map/all_to_all | solution.py:483
  82.6 2.2 %collective-permute-start.6 = (bf16[14,3,384]{2,1,0:T(4,128)(2,1)S(1)}, bf16[14,3,384]{2,1,0:T(4,128)(2,1)S(1)}, u32[]{:S(2)}, u32[]{:S(2)}) collective-permute-start(bf16[14,3,384]{2,1,0:T(4,128)(2,1)S(1)} %pad_maximum_fusion.2), channel_id=1, source_target_pairs={{0,16},{16,32},{32,48},{48,64},{64,80},{80,96},{96,112},{1,17},{17... | collective-permute-start | bytes 96776 | tf_op jit(solution)/shard_map/ppermute | solution.py:336
  84.9 1.3 %collective-permute-start.7 = (bf16[14,3,384]{2,1,0:T(4,128)(2,1)S(1)}, bf16[14,3,384]{2,1,0:T(4,128)(2,1)S(1)}, u32[]{:S(2)}, u32[]{:S(2)}) collective-permute-start(bf16[14,3,384]{2,1,0:T(4,128)(2,1)S(1)} %pad_maximum_fusion.3), channel_id=1, source_target_pairs={{16,0},{32,16},{48,32},{64,48},{80,64},{96,80},{112,96},{17,1},{33... | collective-permute-start | bytes 96776 | tf_op jit(solution)/shard_map/ppermute | solution.py:337
  86.2 2.3 %collective-permute-done.6.left_ref.left_any = bf16[14,3,384]{2,1,0:T(4,128)(2,1)S(1)} collective-permute-done((bf16[14,3,384]{2,1,0:T(4,128)(2,1)S(1)}, bf16[14,3,384]{2,1,0:T(4,128)(2,1)S(1)}, u32[]{:S(2)}, u32[]{:S(2)}) %collective-permute-start.6) | collective-permute-done | bytes 32288 | tf_op jit(solution)/shard_map/ppermute | solution.py:336
  88.5 2.7 %collective-permute-done.7.right_ref.right_any = bf16[14,3,384]{2,1,0:T(4,128)(2,1)S(1)} collective-permute-done((bf16[14,3,384]{2,1,0:T(4,128)(2,1)S(1)}, bf16[14,3,384]{2,1,0:T(4,128)(2,1)S(1)}, u32[]{:S(2)}, u32[]{:S(2)}) %collective-permute-start.7) | collective-permute-done | bytes 32288 | tf_op jit(solution)/shard_map/ppermute | solution.py:337
  91.1 10.7 %all-to-all-done.1.got_ref = bf16[64,24,128]{2,1,0:T(8,128)(2,1)S(1)} async-done(((bf16[64,24,128]{2,1,0:T(8,128)(2,1)}), bf16[64,24,128]{2,1,0:T(8,128)(2,1)S(1)}, u32[]{:S(2)}, u32[]{:S(2)}) %all-to-all-start.1) | async-done | bytes 393248 | tf_op jit(solution)/shard_map/all_to_all | solution.py:483
  101.9 0.8 far_sum.1
  102.7 6.3 %all-to-all-start.2 = ((f32[16,12,128]{2,1,0:T(8,128)}), f32[16,12,128]{2,1,0:T(8,128)S(1)}, u32[]{:S(2)}, u32[]{:S(2)}) async-start(f32[16,12,128]{2,1,0:T(8,128)} %get-tuple-element.49), calls=%async_computation.2 | async-start | bytes 262144 | tf_op jit(solution)/shard_map/all_to_all | solution.py:496
  109.0 2.1 %input_grad.1 = bf16[8,16,384]{2,1,0:T(8,128)(2,1)} custom-call(f32[8,16,384]{2,1,0:T(8,128)S(1)} %get-tuple-element.42.g_ref, bf16[3,16,384]{2,1,0:T(8,128)(2,1)S(1)} %collective-permute-done.4.top_ref.top_any, bf16[3,16,384]{2,1,0:T(8,128)(2,1)S(1)} %collective-permute-done.5.bot_ref.bot_any, ...), custom_call_target="tpu_custom_call" | custom-call | tf_op jit(solution)/shard_map/input_grad/pallas_call | solution.py:474
  111.1 3.3 %all-to-all-done.2.got_ref = f32[16,12,128]{2,1,0:T(8,128)S(1)} async-done(((f32[16,12,128]{2,1,0:T(8,128)}), f32[16,12,128]{2,1,0:T(8,128)S(1)}, u32[]{:S(2)}, u32[]{:S(2)}) %all-to-all-start.2) | async-done | bytes 98336 | tf_op jit(solution)/shard_map/all_to_all | solution.py:496
  114.5 0.7 spread.1
  (12 shorter events, 0.3 us)
Async XLA Ops:
  1.4 9.6 %collective-permute-start.1 = (bf16[3,16,384]{2,1,0:T(8,128)(2,1)S(1)}, bf16[3,16,384]{2,1,0:T(8,128)(2,1)S(1)}, u32[]{:S(2)}, u32[]{:S(2)}) collective-permute-start(bf16[3,16,384]{2,1,0:T(8,128)(2,1)S(1)} %get-tuple-element.59), channel_id=1, source_target_pairs={{128,0},{256,128},{384,256},{512,384},{640,512},{768,640},{896,768... | collective-permute-start | bytes 110600 | tf_op jit(solution)/shard_map/ppermute | solution.py:327
  2.7 8.3 %collective-permute-start = (bf16[3,16,384]{2,1,0:T(8,128)(2,1)S(1)}, bf16[3,16,384]{2,1,0:T(8,128)(2,1)S(1)}, u32[]{:S(2)}, u32[]{:S(2)}) collective-permute-start(bf16[3,16,384]{2,1,0:T(8,128)(2,1)S(1)} %get-tuple-element.60), channel_id=1, source_target_pairs={{0,128},{128,256},{256,384},{384,512},{512,640},{640,768},{768,896... | collective-permute-start | bytes 110600 | tf_op jit(solution)/shard_map/ppermute | solution.py:326
  11.1 4.5 %collective-permute-start.2 = (bf16[14,3,384]{2,1,0:T(4,128)(2,1)S(1)}, bf16[14,3,384]{2,1,0:T(4,128)(2,1)S(1)}, u32[]{:S(2)}, u32[]{:S(2)}) collective-permute-start(bf16[14,3,384]{2,1,0:T(4,128)(2,1)S(1)} %pad_maximum_fusion), channel_id=1, source_target_pairs={{0,16},{16,32},{32,48},{48,64},{64,80},{80,96},{96,112},{1,17},{17... | collective-permute-start | bytes 96776 | tf_op jit(solution)/shard_map/ppermute | solution.py:336
  14.3 4.8 %collective-permute-start.3 = (bf16[14,3,384]{2,1,0:T(4,128)(2,1)S(1)}, bf16[14,3,384]{2,1,0:T(4,128)(2,1)S(1)}, u32[]{:S(2)}, u32[]{:S(2)}) collective-permute-start(bf16[14,3,384]{2,1,0:T(4,128)(2,1)S(1)} %pad_maximum_fusion.1), channel_id=1, source_target_pairs={{16,0},{32,16},{48,32},{64,48},{80,64},{96,80},{112,96},{17,1},{33... | collective-permute-start | bytes 96776 | tf_op jit(solution)/shard_map/ppermute | solution.py:337
  25.4 16.1 %collective-permute-start.8 = (bf16[8,600,128]{2,1,0:T(8,128)(2,1)S(1)}, bf16[8,600,128]{2,1,0:T(8,128)(2,1)S(1)}, u32[]{:S(2)}, u32[]{:S(2)}) collective-permute-start(bf16[8,600,128]{2,1,0:T(8,128)(2,1)S(1)} %get-tuple-element.46), channel_id=1, source_target_pairs={{0,1},{1,0},{2,3},{3,2},{4,5},{5,4},{6,7},{7,6},{8,9},{9,8},{10,11... | collective-permute-start | bytes 3686408 | tf_op jit(solution)/shard_map/ppermute | solution.py:430
  42.7 22.7 %all-to-all-start = ((bf16[8,600,128]{2,1,0:T(8,128)(2,1)}), bf16[8,600,128]{2,1,0:T(8,128)(2,1)S(1)}, u32[]{:S(2)}, u32[]{:S(2)}) async-start(bf16[8,600,128]{2,1,0:T(8,128)(2,1)} %join.1), calls=%async_computation | async-start | bytes 2457600 | tf_op jit(solution)/shard_map/all_to_all | solution.py:460
  46.3 6.9 %collective-permute-start.5 = (bf16[3,16,384]{2,1,0:T(8,128)(2,1)S(1)}, bf16[3,16,384]{2,1,0:T(8,128)(2,1)S(1)}, u32[]{:S(2)}, u32[]{:S(2)}) collective-permute-start(bf16[3,16,384]{2,1,0:T(8,128)(2,1)S(1)} %get-tuple-element.55), channel_id=1, source_target_pairs={{128,0},{256,128},{384,256},{512,384},{640,512},{768,640},{896,768... | collective-permute-start | bytes 110600 | tf_op jit(solution)/shard_map/ppermute | solution.py:327
  47.6 7.6 %collective-permute-start.4 = (bf16[3,16,384]{2,1,0:T(8,128)(2,1)S(1)}, bf16[3,16,384]{2,1,0:T(8,128)(2,1)S(1)}, u32[]{:S(2)}, u32[]{:S(2)}) collective-permute-start(bf16[3,16,384]{2,1,0:T(8,128)(2,1)S(1)} %get-tuple-element.56), channel_id=1, source_target_pairs={{0,128},{128,256},{256,384},{384,512},{512,640},{640,768},{768,896... | collective-permute-start | bytes 110600 | tf_op jit(solution)/shard_map/ppermute | solution.py:326
  66.5 35.4 %all-to-all-start.1 = ((bf16[64,24,128]{2,1,0:T(8,128)(2,1)}), bf16[64,24,128]{2,1,0:T(8,128)(2,1)S(1)}, u32[]{:S(2)}, u32[]{:S(2)}) async-start(bf16[64,24,128]{2,1,0:T(8,128)(2,1)} %block_sum.1), calls=%async_computation.1 | async-start | bytes 786432 | tf_op jit(solution)/shard_map/all_to_all | solution.py:483
  82.6 5.8 %collective-permute-start.6 = (bf16[14,3,384]{2,1,0:T(4,128)(2,1)S(1)}, bf16[14,3,384]{2,1,0:T(4,128)(2,1)S(1)}, u32[]{:S(2)}, u32[]{:S(2)}) collective-permute-start(bf16[14,3,384]{2,1,0:T(4,128)(2,1)S(1)} %pad_maximum_fusion.2), channel_id=1, source_target_pairs={{0,16},{16,32},{32,48},{48,64},{64,80},{80,96},{96,112},{1,17},{17... | collective-permute-start | bytes 96776 | tf_op jit(solution)/shard_map/ppermute | solution.py:336
  84.9 6.2 %collective-permute-start.7 = (bf16[14,3,384]{2,1,0:T(4,128)(2,1)S(1)}, bf16[14,3,384]{2,1,0:T(4,128)(2,1)S(1)}, u32[]{:S(2)}, u32[]{:S(2)}) collective-permute-start(bf16[14,3,384]{2,1,0:T(4,128)(2,1)S(1)} %pad_maximum_fusion.3), channel_id=1, source_target_pairs={{16,0},{32,16},{48,32},{64,48},{80,64},{96,80},{112,96},{17,1},{33... | collective-permute-start | bytes 96776 | tf_op jit(solution)/shard_map/ppermute | solution.py:337
  102.7 11.8 %all-to-all-start.2 = ((f32[16,12,128]{2,1,0:T(8,128)}), f32[16,12,128]{2,1,0:T(8,128)S(1)}, u32[]{:S(2)}, u32[]{:S(2)}) async-start(f32[16,12,128]{2,1,0:T(8,128)} %get-tuple-element.49), calls=%async_computation.2 | async-start | bytes 262144 | tf_op jit(solution)/shard_map/all_to_all | solution.py:496
